TPU v7x, 128 devices: a whole 4x4x4 slice. The times are simulated.
128 devices in a mesh: req: 8 (over z, core), wide: 16 (over x, y).
Axes of the slice: x: 4, y: 4, z: 4, core: 2. Of those that a mesh axis runs over, the one named last changes fastest.
Arguments:
- queries: bfloat16 [16384, 3072], P(('req', 'wide'))
- suffix_latent: bfloat16 [16384, 512], P(('req', 'wide')), may hold values from -6 to 6
- suffix_rope: bfloat16 [64, 16384], P(None, ('req', 'wide')), may hold values from -6 to 6
- residual: bfloat16 [16384, 2048], P(('req', 'wide')), may hold values from -3 to 3
- prefix_latent: bfloat16 [8, 2, 2048, 512], P('req', None, 'wide'), may hold values from -6 to 6
- prefix_rope: bfloat16 [8, 2, 64, 2048], P('req', None, None, 'wide')
- suffix_lengths: int32 [128, 4], P(('req', 'wide')), may hold values from 1 to 64, 128 in all within a row
- prefix_ids: int32 [128, 4], P(('req', 'wide')), may hold values from 0 to 1
- w_ukv: bfloat16 [512, 4096], replicated, may hold values from -0.25 to 0.25
- w_out: bfloat16 [2048, 2048], replicated, may hold values from -0.5 to 0.5
- norm_gain: bfloat16 [2048], replicated, may hold values from 0.099609375 to 1.8984375
- expert_ids: int32 [16384, 6], P(('req', 'wide')), may hold values from 0 to 63, all different within a row; in each aligned block of 128 rows (0 to 127, 128 to 255, ...) at most 13 rows name the same one
- gate_values: float32 [16384, 6], P(('req', 'wide')), may hold values from 0.05 to 0.45
- expert_gate_up: bfloat16 [128, 2048, 1408], P(('req', 'wide')), may hold values from -0.125 to 0.125
- expert_down: bfloat16 [128, 704, 2048], P(('req', 'wide')), may hold values from -0.15625 to 0.15625
Outputs:
- layer_out: bfloat16 [16384, 2048], P(('req', 'wide'))
Inputs may be any that keep to these rules, and one draw needn't show every extreme that they name: `suffix_lengths`: row b gives, in order, the lengths of the 4 requests that make up tokens b * 128 to (b + 1) * 128 - 1; each row sums to 128 and its largest entry is 64. `expert_ids`: a token's 6 experts differ; among the 128 tokens of one device no expert is named more than 13 times, and in some device one expert is named exactly 13 times.
All inputs are finite; a program needn't handle non-finite values.
Results may differ from a plain program's by a relative error of at most 0.012.
Values may be sent and summed in bfloat16 or wider, within the bound.
No kernel may reach another device: no remote copies, remote signals or barrier semaphores. Data moves between devices by JAX's collectives and lax.ppermute only.
A program may use at most 192 MiB of HBM per device.

v0:
```python
import jax
import jax.numpy as jnp
from jax import lax
from jax.experimental import pallas as pl
from jax.experimental.pallas import tpu as pltpu
from jax.sharding import PartitionSpec as P


D = 2048
HEADS = 16
NOPE = 128
ROPE = 64
LAT = 512
TOP = 6
PREF = 2
EXPERTS = 64
TOK = 128
REQS = 4
TILE = 16
CAP = 13
SLOTS_A = 8
HALF = D // 2
PIECE = D // 8
WIDTH_B = HALF + PIECE
BLK = 144
EPS = 1e-06
SCALE = 1.0 / (NOPE + ROPE) ** 0.5
LOG2E = 1.4426950408889634
NEG = -1e30
bf16 = jnp.bfloat16
f32 = jnp.float32


def request_scalars(sc_ref):
    lens = [sc_ref[r] for r in range(REQS)]
    own = [sc_ref[REQS + r] for r in range(REQS)]
    starts, total = [], 0
    for r in range(REQS):
        starts.append(total)
        total = total + lens[r]
    zero_count = sum(jnp.where(own[r] == 0, lens[r], 0) for r in range(REQS))
    bases, next0, next1 = [], 0, zero_count
    for r in range(REQS):
        is0 = own[r] == 0
        bases.append(jnp.where(is0, next0, next1))
        next0 = next0 + jnp.where(is0, lens[r], 0)
        next1 = next1 + jnp.where(is0, 0, lens[r])
    return lens, starts, bases, zero_count


def place_of(tokens, starts, bases):
    place = tokens - starts[0] + bases[0]
    for r in range(1, REQS):
        place = jnp.where(tokens >= starts[r], tokens - starts[r] + bases[r], place)
    return place


def sort_matrix(sc_ref, transposed):
    _, starts, bases, _ = request_scalars(sc_ref)
    token_dim = 0 if transposed else 1
    tokens = lax.broadcasted_iota(jnp.int32, (TOK, TOK), token_dim)
    slots = lax.broadcasted_iota(jnp.int32, (TOK, TOK), 1 - token_dim)
    return jnp.where(place_of(tokens, starts, bases) == slots, 1.0, 0.0).astype(bf16)


def mm(a, b):
    return jnp.dot(a, b, preferred_element_type=f32)


def mm_nt(a, b):
    return lax.dot_general(a, b, (((1,), (1,)), ((), ())), preferred_element_type=f32)


def mm_tn(a, b):
    return lax.dot_general(a, b, (((0,), (0,)), ((), ())), preferred_element_type=f32)


HG = 4


def query_kernel(sc_ref, q_ref, qr_ref, w_ref, qa_ref, qo_ref):
    order = sort_matrix(sc_ref, False)
    nope = mm(order, q_ref[...]).astype(bf16)
    rope = mm(order, qr_ref[...]).astype(bf16)
    for h in range(HG):
        keys = w_ref[:, h * 256 : h * 256 + 128]
        qa_ref[h] = mm_nt(nope[:, h * 128 : (h + 1) * 128], keys).astype(bf16)
        qo_ref[h] = rope[:, h * ROPE : (h + 1) * ROPE]


def prepare_queries(scalars, queries, w_ukv):
    return pl.pallas_call(
        query_kernel,
        out_shape=(
            jax.ShapeDtypeStruct((HEADS, TOK, LAT), bf16),
            jax.ShapeDtypeStruct((HEADS, TOK, ROPE), bf16),
        ),
        grid_spec=pltpu.PrefetchScalarGridSpec(
            num_scalar_prefetch=1,
            grid=(HEADS // HG,),
            in_specs=[
                pl.BlockSpec((TOK, HG * NOPE), lambda i, s: (0, i)),
                pl.BlockSpec((TOK, HG * ROPE), lambda i, s: (0, HEADS * NOPE // (HG * ROPE) + i)),
                pl.BlockSpec((LAT, HG * 2 * NOPE), lambda i, s: (0, i)),
            ],
            out_specs=[
                pl.BlockSpec((HG, TOK, LAT), lambda i, s: (i, 0, 0)),
                pl.BlockSpec((HG, TOK, ROPE), lambda i, s: (i, 0, 0)),
            ],
        ),
        name="query_prep",
    )(scalars, queries, queries, w_ukv)


ROWS = HEADS * TILE


def block_views(refs):
    views = []
    for ref in refs:
        for b in range(ref.shape[0] // BLK):
            views.append((ref, b * BLK))
    return views


def attention_kernel(n_pieces, stage, sc_ref, qa_ref, qr_ref, *rest):
    rest = list(rest)
    local = [rest.pop(0), rest.pop(0)]
    pieces = (rest[:n_pieces], rest[n_pieces : 2 * n_pieces])
    rest = rest[2 * n_pieces :]
    if stage == LAST:
        o_ref, s_scr, m_scr, l_scr, acc_scr = rest
    else:
        ml_ref, acc_out, s_scr, m_scr, l_scr, acc_scr = rest
    lens, starts, bases, zero_count = request_scalars(sc_ref)
    first = pl.program_id(0) * TILE
    c = SCALE * LOG2E
    q = qa_ref[...].reshape(ROWS, LAT)
    qr = qr_ref[...].reshape(ROWS, ROPE)

    if stage == FIRST:
        ll_ref, lr_ref = local
        places = first + lax.broadcasted_iota(jnp.int32, (TILE, TOK), 0)
        keys_at = lax.broadcasted_iota(jnp.int32, (TILE, TOK), 1)
        bias = jnp.full((TILE, TOK), NEG, f32)
        for r in range(REQS):
            mine = (places >= bases[r]) & (places < bases[r] + lens[r])
            tok = places - bases[r] + starts[r]
            ok = mine & (keys_at >= starts[r]) & (keys_at <= tok)
            bias = jnp.where(ok, 0.0, bias)
        local_lat = ll_ref[...]
        s = mm_nt(q, local_lat) + mm(qr, lr_ref[...])
        s = (s.reshape(HEADS, TILE, TOK) + bias[None]).reshape(ROWS, TOK)
        m = jnp.max(s, axis=1, keepdims=True)
        p = jnp.exp2((s - m) * c)
        m_scr[...] = jnp.broadcast_to(m, (ROWS, 128))
        l_scr[...] = jnp.broadcast_to(jnp.sum(p, axis=1, keepdims=True), (ROWS, 128))
        acc_scr[...] = mm(p.astype(bf16), local_lat)
    else:
        ml_in, acc_in = local
        ml = ml_in[...].reshape(ROWS, 128)
        m_scr[...] = jnp.broadcast_to(ml[:, :1], (ROWS, 128))
        l_scr[...] = jnp.broadcast_to(ml[:, 1:2], (ROWS, 128))
        acc_scr[...] = acc_in[...].reshape(ROWS, LAT)

    for pre in range(PREF):
        needed = (first < zero_count) if pre == 0 else (first + TILE > zero_count)

        @pl.when(needed)
        def _(pre=pre):
            views = block_views(pieces[pre])
            place = first + lax.broadcasted_iota(jnp.int32, (ROWS, 1), 0) % TILE
            mine = (place < zero_count) if pre == 0 else (place >= zero_count)
            row_bias = jnp.where(mine, 0.0, NEG)
            chunks = [views[k : k + 4] for k in range(0, len(views), 4)]
            m_old = m_scr[:, :1]
            m_new = m_old
            for k, chunk in enumerate(chunks):
                lat = jnp.concatenate([ref[at : at + 128, :] for ref, at in chunk], axis=0)
                rope = jnp.concatenate(
                    [
                        jnp.concatenate(
                            [ref[at + 128 : at + 144, j * 128 : (j + 1) * 128] for j in range(4)],
                            axis=0,
                        )
                        for ref, at in chunk
                    ],
                    axis=1,
                )
                s = mm_nt(q, lat) + mm(qr, rope) + row_bias
                s_scr[k] = s
                m_new = jnp.maximum(m_new, jnp.max(s, axis=1, keepdims=True))
            scale_old = jnp.exp2((m_old - m_new) * c)
            total = l_scr[:, :1] * scale_old
            acc = acc_scr[...] * scale_old
            for k, chunk in enumerate(chunks):
                lat = jnp.concatenate([ref[at : at + 128, :] for ref, at in chunk], axis=0)
                p = jnp.exp2((s_scr[k] - m_new) * c)
                total = total + jnp.sum(p, axis=1, keepdims=True)
                acc = acc + mm(p.astype(bf16), lat)
            m_scr[...] = jnp.broadcast_to(m_new, (ROWS, 128))
            l_scr[...] = jnp.broadcast_to(total, (ROWS, 128))
            acc_scr[...] = acc

    if stage == LAST:
        out = acc_scr[...] / l_scr[:, :1]
        o_ref[...] = out.astype(bf16).reshape(HEADS, TILE, LAT)
    else:
        lane = lax.broadcasted_iota(jnp.int32, (ROWS, 128), 1)
        ml = jnp.where(lane == 0, m_scr[...], l_scr[...])
        ml_ref[...] = ml.reshape(HEADS, TILE, 128)
        acc_out[...] = acc_scr[...].reshape(HEADS, TILE, LAT)


FIRST, MIDDLE, LAST = 0, 1, 2


def attend(stage, scalars, qa, qr, local, pieces0, pieces1):
    n_pieces = len(pieces0)
    whole = lambda a: pl.BlockSpec(a.shape, lambda i, s: (0,) * a.ndim)
    tiled = lambda width: pl.BlockSpec((HEADS, TILE, width), lambda i, s: (0, i, 0))
    pieces = [*pieces0, *pieces1]
    local_specs = [whole(a) for a in local] if stage == FIRST else [tiled(128), tiled(LAT)]
    if stage == LAST:
        out_shape = jax.ShapeDtypeStruct((HEADS, TOK, LAT), bf16)
        out_specs = tiled(LAT)
    else:
        out_shape = (
            jax.ShapeDtypeStruct((HEADS, TOK, 128), f32),
            jax.ShapeDtypeStruct((HEADS, TOK, LAT), f32),
        )
        out_specs = [tiled(128), tiled(LAT)]
    keys = sum(a.shape[0] // BLK for a in pieces0)
    return pl.pallas_call(
        lambda *refs: attention_kernel(n_pieces, stage, *refs),
        out_shape=out_shape,
        grid_spec=pltpu.PrefetchScalarGridSpec(
            num_scalar_prefetch=1,
            grid=(TOK // TILE,),
            in_specs=[tiled(LAT), tiled(ROPE), *local_specs, *[whole(a) for a in pieces]],
            out_specs=out_specs,
            scratch_shapes=[
                pltpu.VMEM((max(keys // 4, 1), ROWS, 512), f32),
                pltpu.VMEM((ROWS, 128), f32),
                pltpu.VMEM((ROWS, 128), f32),
                pltpu.VMEM((ROWS, LAT), f32),
            ],
        ),
    )(scalars, qa, qr, *local, *pieces)


def project_kernel(sc_ref, o_ref, w_ref, wo_ref, res_ref, gain_ref, hid_ref, norm_ref, acc_ref):
    step = pl.program_id(0)

    @pl.when(step == 0)
    def _():
        acc_ref[...] = res_ref[...].astype(f32)

    back = sort_matrix(sc_ref, True)
    heads = [mm(o_ref[h], w_ref[:, h * 256 + 128 : h * 256 + 256]).astype(bf16) for h in range(HG)]
    head_out = mm(back, jnp.concatenate(heads, axis=1)).astype(bf16)
    acc_ref[...] += mm(head_out, wo_ref[...])

    @pl.when(step == HEADS // HG - 1)
    def _():
        hidden = acc_ref[...].astype(bf16)
        hid_ref[...] = hidden
        h32 = hidden.astype(f32)
        inverse = lax.rsqrt(jnp.mean(h32 * h32, axis=1, keepdims=True) + EPS)
        norm_ref[...] = (h32 * inverse * gain_ref[...].astype(f32)).astype(bf16)


def project(scalars, o_lat, w_ukv, w_out, residual, gain):
    return pl.pallas_call(
        project_kernel,
        out_shape=(
            jax.ShapeDtypeStruct((TOK, D), bf16),
            jax.ShapeDtypeStruct((TOK, D), bf16),
        ),
        grid_spec=pltpu.PrefetchScalarGridSpec(
            num_scalar_prefetch=1,
            grid=(HEADS // HG,),
            in_specs=[
                pl.BlockSpec((HG, TOK, LAT), lambda i, s: (i, 0, 0)),
                pl.BlockSpec((LAT, HG * 2 * NOPE), lambda i, s: (0, i)),
                pl.BlockSpec((HG * NOPE, D), lambda i, s: (i, 0)),
                pl.BlockSpec((TOK, D), lambda i, s: (0, 0)),
                pl.BlockSpec((1, D), lambda i, s: (0, 0)),
            ],
            out_specs=[
                pl.BlockSpec((TOK, D), lambda i, s: (0, 0)),
                pl.BlockSpec((TOK, D), lambda i, s: (0, 0)),
            ],
            scratch_shapes=[pltpu.VMEM((TOK, D), f32)],
        ),
        name="project",
    )(scalars, o_lat, w_ukv, w_out, residual, gain)


def rank_table(ids_ref):
    expert = lax.broadcasted_iota(jnp.int32, (EXPERTS, TOK), 0)
    named = ids_ref[0:1, :] == expert
    for k in range(1, TOP):
        named = named | (ids_ref[k : k + 1, :] == expert)
    earlier = lax.broadcasted_iota(jnp.int32, (TOK, TOK), 0) < lax.broadcasted_iota(
        jnp.int32, (TOK, TOK), 1
    )
    rank = mm(jnp.where(named, 1.0, 0.0).astype(bf16), jnp.where(earlier, 1.0, 0.0).astype(bf16))
    return jnp.where(named, rank, -1.0)


def gate_table(ids_ref, gates_ref):
    expert = lax.broadcasted_iota(jnp.int32, (EXPERTS, TOK), 0)
    gates = jnp.zeros((EXPERTS, TOK), f32)
    for k in range(TOP):
        gates = gates + jnp.where(ids_ref[k : k + 1, :] == expert, gates_ref[k : k + 1, :], 0.0)
    return gates


def whole_rows(ranks, experts, copies, values=None):
    slot = lax.broadcasted_iota(jnp.int32, (SLOTS_A, TOK), 0).astype(f32)
    rows = []
    for e in range(experts):
        on = 1.0 if values is None else values[e : e + 1, :]
        rows += [jnp.where(ranks[e : e + 1, :] == slot, on, 0.0)] * copies
    return jnp.concatenate(rows, axis=0)


def packed_rows(ranks, experts, copies, values=None):
    row = lax.broadcasted_iota(jnp.int32, (8, TOK), 0)
    slot = (SLOTS_A + row // 2).astype(f32)
    even = row % 2 == 0
    lower, upper, last = [], [], []
    for e in range(experts):
        rank = ranks[e : e + 1, :]
        on = 1.0 if values is None else values[e : e + 1, :]
        hit = jnp.where(rank == slot, on, 0.0)
        lower += [jnp.where(even, hit, 0.0)] * copies
        upper += [jnp.where(even, 0.0, hit)] * copies
        last += [jnp.where(jnp.broadcast_to(rank, (8, TOK)) == CAP - 1.0, on, 0.0)] * copies
    return [jnp.concatenate(part, axis=0) for part in (lower, upper, last)]


def pieces_of(last):
    row = lax.broadcasted_iota(jnp.int32, last.shape, 0) % 8
    return [jnp.where(row == q, last, 0.0) for q in range(8)]


EG = 16


def dispatch_kernel(ids_ref, norm_ref, out_ref, rank_scr):
    step = pl.program_id(0)

    @pl.when(step == 0)
    def _():
        rank_scr[...] = rank_table(ids_ref)

    ranks = rank_scr[pl.ds(step * EG, EG), :]
    sent = mm(whole_rows(ranks, EG, 1).astype(bf16), norm_ref[...]).astype(bf16)
    for e in range(EG):
        part = sent[e * SLOTS_A : (e + 1) * SLOTS_A]
        out_ref[2 * e] = part
        out_ref[2 * e + 1] = part


def dispatch_packed_kernel(ids_ref, norm_ref, out_ref, rank_scr):
    step = pl.program_id(0)

    @pl.when(step == 0)
    def _():
        rank_scr[...] = rank_table(ids_ref)

    ranks = rank_scr[pl.ds(step * EG, EG), :]
    lower, upper, last = packed_rows(ranks, EG, 1)
    sent = (
        mm(lower.astype(bf16), norm_ref[:, :HALF]) + mm(upper.astype(bf16), norm_ref[:, HALF:])
    ).astype(bf16)
    tail = jnp.zeros((EG * 8, PIECE), f32)
    for q, piece in enumerate(pieces_of(last)):
        tail = tail + mm(piece.astype(bf16), norm_ref[:, q * PIECE : (q + 1) * PIECE])
    tail = tail.astype(bf16)
    for e in range(EG):
        for copy in range(2):
            out_ref[2 * e + copy, :, :HALF] = sent[e * 8 : (e + 1) * 8]
            out_ref[2 * e + copy, :, HALF:] = tail[e * 8 : (e + 1) * 8]


def dispatch(kernel, width, ids_t, normed):
    return pl.pallas_call(
        kernel,
        out_shape=jax.ShapeDtypeStruct((2 * EXPERTS, 8, width), bf16),
        grid=(EXPERTS // EG,),
        in_specs=[
            pl.BlockSpec((TOP, TOK), lambda i: (0, 0)),
            pl.BlockSpec((TOK, D), lambda i: (0, 0)),
        ],
        out_specs=pl.BlockSpec((2 * EG, 8, width), lambda i: (i, 0, 0)),
        scratch_shapes=[pltpu.VMEM((EXPERTS, TOK), f32)],
    )(ids_t, normed)


def expert_rows(x, wg_ref, wd_ref):
    gate_up = mm(x, wg_ref[0])
    half = gate_up.shape[1] // 2
    gate, up = gate_up[:, :half], gate_up[:, half:]
    act = (gate / (1.0 + jnp.exp(-gate)) * up).astype(bf16)
    return mm(act, wd_ref[0]).astype(bf16)


def expert_kernel(x_ref, wg_ref, wd_ref, out_ref):
    x = x_ref[...].reshape(-1, D)
    out_ref[...] = expert_rows(x, wg_ref, wd_ref).reshape(out_ref.shape)


def select(rows, columns, stride, offset):
    r = lax.broadcasted_iota(jnp.int32, (rows, columns), 0)
    c = lax.broadcasted_iota(jnp.int32, (rows, columns), 1)
    return jnp.where(c == r * stride + offset, 1.0, 0.0).astype(bf16)


def expert_packed_kernel(x_ref, wg_ref, wd_ref, out_ref):
    n = x_ref.shape[0]
    x = x_ref[...].reshape(8 * n, WIDTH_B)
    even, odd = select(4 * n, 8 * n, 2, 0), select(4 * n, 8 * n, 2, 1)
    each = [select(n, 8 * n, 8, q) for q in range(8)]
    main = jnp.concatenate([mm(even, x[:, :HALF]), mm(odd, x[:, :HALF])], axis=1)
    last = jnp.concatenate([mm(pick, x[:, HALF:]) for pick in each], axis=1)
    y = expert_rows(jnp.concatenate([main, last], axis=0).astype(bf16), wg_ref, wd_ref)
    main, last = y[: 4 * n], y[4 * n :]
    out = mm_tn(even, main[:, :HALF]) + mm_tn(odd, main[:, HALF:])
    tail = jnp.zeros((8 * n, PIECE), f32)
    for q, pick in enumerate(each):
        tail = tail + mm_tn(pick, last[:, q * PIECE : (q + 1) * PIECE])
    out_ref[:, :, :HALF] = out.astype(bf16).reshape(n, 8, HALF)
    out_ref[:, :, HALF:] = tail.astype(bf16).reshape(n, 8, PIECE)


def run_expert(kernel, rows, w_gate_up, w_down):
    width = rows.shape[2]
    per = 32
    return pl.pallas_call(
        kernel,
        out_shape=jax.ShapeDtypeStruct(rows.shape, bf16),
        grid=(rows.shape[0] // per,),
        in_specs=[
            pl.BlockSpec((per, 8, width), lambda i: (i, 0, 0)),
            pl.BlockSpec(w_gate_up.shape, lambda i: (0, 0, 0), pipeline_mode=pl.Buffered(1)),
            pl.BlockSpec(w_down.shape, lambda i: (0, 0, 0), pipeline_mode=pl.Buffered(1)),
        ],
        out_specs=pl.BlockSpec((per, 8, width), lambda i: (i, 0, 0)),
    )(rows, w_gate_up, w_down)


def weighted(weight, back):
    high = weight.astype(bf16)
    low = (weight - high.astype(f32)).astype(bf16)
    both = mm_tn(jnp.concatenate([high, low], axis=1), back)
    return both[:TOK] + both[TOK:]


def combine_kernel(ids_ref, gates_ref, hid_ref, back_ref, out_ref, rank_scr, gate_scr):
    step = pl.program_id(0)

    @pl.when(step == 0)
    def _():
        rank_scr[...] = rank_table(ids_ref)
        gate_scr[...] = gate_table(ids_ref, gates_ref)
        out_ref[...] = hid_ref[...].astype(f32)

    ranks = rank_scr[pl.ds(step * EG, EG), :]
    gates = gate_scr[pl.ds(step * EG, EG), :]
    back = back_ref[...].reshape(2 * EG * SLOTS_A, D)
    out_ref[...] += weighted(whole_rows(ranks, EG, 2, gates), back)


def combine_packed_kernel(
    ids_ref, gates_ref, sum_ref, back_ref, out_ref, rank_scr, gate_scr, acc_ref
):
    step = pl.program_id(0)

    @pl.when(step == 0)
    def _():
        rank_scr[...] = rank_table(ids_ref)
        gate_scr[...] = gate_table(ids_ref, gates_ref)
        acc_ref[...] = sum_ref[...]

    ranks = rank_scr[pl.ds(step * EG, EG), :]
    gates = gate_scr[pl.ds(step * EG, EG), :]
    back = back_ref[...].reshape(2 * EG * 8, WIDTH_B)
    lower, upper, last = packed_rows(ranks, EG, 2, gates)
    acc_ref[:, :HALF] += weighted(lower, back[:, :HALF])
    acc_ref[:, HALF:] += weighted(upper, back[:, :HALF])
    for q, piece in enumerate(pieces_of(last)):
        acc_ref[:, q * PIECE : (q + 1) * PIECE] += weighted(piece, back[:, HALF:])

    @pl.when(step == EXPERTS // EG - 1)
    def _():
        out_ref[...] = acc_ref[...].astype(bf16)


def combine(kernel, ids_t, gates_t, base, back, out_type):
    scratch = [pltpu.VMEM((EXPERTS, TOK), f32), pltpu.VMEM((EXPERTS, TOK), f32)]
    if out_type == bf16:
        scratch.append(pltpu.VMEM((TOK, D), f32))
    return pl.pallas_call(
        kernel,
        out_shape=jax.ShapeDtypeStruct((TOK, D), out_type),
        grid=(EXPERTS // EG,),
        in_specs=[
            pl.BlockSpec((TOP, TOK), lambda i: (0, 0)),
            pl.BlockSpec((TOP, TOK), lambda i: (0, 0)),
            pl.BlockSpec((TOK, D), lambda i: (0, 0)),
            pl.BlockSpec((2 * EG, 8, back.shape[2]), lambda i: (i, 0, 0)),
        ],
        out_specs=pl.BlockSpec((TOK, D), lambda i: (0, 0)),
        scratch_shapes=scratch,
    )(ids_t, gates_t, base, back)


def shift(axis, k):
    pairs = []
    for x in range(4):
        for y in range(4):
            tx, ty = ((x + k) % 4, y) if axis == "x" else (x, (y + k) % 4)
            pairs.append((x * 4 + y, tx * 4 + ty))
    return pairs


def hop(a, axis, k):
    return lax.ppermute(a, "wide", shift(axis, k))


def gather_row(own, first):
    ahead, behind = hop(own, first, 1), hop(own, first, -1)
    far = hop(own, first, 2)
    return jnp.concatenate([own, ahead, behind, far], axis=0)


def gather_rest(row, second):
    ahead, behind = hop(row, second, 1), hop(row, second, -1)
    far = hop(row, second, 2)
    return ahead, behind, far


def pack_prefix(latent, rope):
    packed = rope.reshape(4, 16, TOK).transpose(1, 0, 2).reshape(16, 4 * TOK)
    return jnp.concatenate([latent, packed], axis=0)


def exchange(a):
    return lax.all_to_all(a, ("req", "wide"), split_axis=0, concat_axis=0, tiled=True)


def layer(
    queries,
    suffix_latent,
    suffix_rope,
    residual,
    prefix_latent,
    prefix_rope,
    suffix_lengths,
    prefix_ids,
    w_ukv,
    w_out,
    norm_gain,
    expert_ids,
    gate_values,
    expert_gate_up,
    expert_down,
):
    scalars = jnp.concatenate([suffix_lengths[0], prefix_ids[0]])
    row0 = gather_row(pack_prefix(prefix_latent[0, 0], prefix_rope[0, 0]), "x")
    row1 = gather_row(pack_prefix(prefix_latent[0, 1], prefix_rope[0, 1]), "y")
    qa, qr = prepare_queries(scalars, queries, w_ukv)
    ahead0, behind0, far0 = gather_rest(row0, "y")
    ahead1, behind1, far1 = gather_rest(row1, "x")
    state = attend(FIRST, scalars, qa, qr, (suffix_latent, suffix_rope), [row0], [row1])
    state = attend(MIDDLE, scalars, qa, qr, state, [ahead0, behind0], [ahead1, behind1])
    o_lat = attend(LAST, scalars, qa, qr, state, [far0], [far1])
    hidden, normed = project(scalars, o_lat, w_ukv, w_out, residual, norm_gain.reshape(1, D))
    ids_t = expert_ids.T
    gates_t = gate_values.T
    sent_a = dispatch(dispatch_kernel, D, ids_t, normed)
    sent_b = dispatch(dispatch_packed_kernel, WIDTH_B, ids_t, normed)
    rows_a = exchange(sent_a)
    rows_b = exchange(sent_b)
    made_a = run_expert(expert_kernel, rows_a, expert_gate_up, expert_down)
    made_b = run_expert(expert_packed_kernel, rows_b, expert_gate_up, expert_down)
    back_a = exchange(made_a)
    back_b = exchange(made_b)
    part = combine(combine_kernel, ids_t, gates_t, hidden, back_a, f32)
    return combine(combine_packed_kernel, ids_t, gates_t, part, back_b, bf16)


def solution(mesh):
    return jax.shard_map(
        layer,
        mesh=mesh,
        in_specs=(
            P(("req", "wide"), None),
            P(("req", "wide"), None),
            P(None, ("req", "wide")),
            P(("req", "wide"), None),
            P("req", None, "wide", None),
            P("req", None, None, "wide"),
            P(("req", "wide"), None),
            P(("req", "wide"), None),
            P(),
            P(),
            P(),
            P(("req", "wide"), None),
            P(("req", "wide"), None),
            P(("req", "wide"), None, None),
            P(("req", "wide"), None, None),
        ),
        out_specs=P(("req", "wide"), None),
        check_vma=False,
    )
```

profile of v0, /device:TPU:37, one launch (start us, length us, event | category | flops | bytes accessed | tf_op | source)
XLA Modules:
  0.0 312.7 jit_solution(12722306286319356701)
XLA Ops:
  7.2 2.1 collective-permute-done.2
  15.9 10.9 %collective-permute-done.3 = bf16[144,512]{1,0:T(8,128)(2,1)S(1)} collective-permute-done((bf16[144,512]{1,0:T(8,128)(2,1)S(1)}, bf16[144,512]{1,0:T(8,128)(2,1)S(1)}, u32[]{:S(2)}, u32[]{:S(2)}) %collective-permute-start.3) | collective-permute-done | bytes 147488 | tf_op jit(solution)/shard_map/ppermute | solution.py:531
  26.9 3.9 %collective-permute-done.5 = bf16[144,512]{1,0:T(8,128)(2,1)S(1)} collective-permute-done((bf16[144,512]{1,0:T(8,128)(2,1)S(1)}, bf16[144,512]{1,0:T(8,128)(2,1)S(1)}, u32[]{:S(2)}, u32[]{:S(2)}) %collective-permute-start.5) | collective-permute-done | bytes 147488 | tf_op jit(solution)/shard_map/ppermute | solution.py:531
  30.8 2.3 collective-permute-start.8
  33.7 3.5 %collective-permute-start.11 = (bf16[576,512]{1,0:T(8,128)(2,1)S(1)}, bf16[576,512]{1,0:T(8,128)(2,1)}, u32[]{:S(2)}, u32[]{:S(2)}) collective-permute-start(bf16[576,512]{1,0:T(8,128)(2,1)S(1)} %constant_dynamic-update-slice_fusion.5.refs_6_), channel_id=1, source_target_pairs={{0,8},{1,9},{2,10},{3,11},{4,12},{5,13},{6,14},{7,15},{8,0},{9,1},... | collective-permute-start | bytes 1769480 | tf_op jit(solution)/shard_map/ppermute | solution.py:531
  39.8 5.9 %query_prep.1 = (bf16[16,128,512]{2,1,0:T(8,128)(2,1)}, bf16[16,128,64]{2,1,0:T(8,128)(2,1)}) custom-call(s32[8]{0:T(128)} %pad_add_fusion.sc_ref.refs_0_, bf16[128,3072]{1,0:T(8,128)(2,1)} %qr_ref.1, bf16[128,3072]{1,0:T(8,128)(2,1)} %qr_ref.1, bf16[512,4096]{1,0:T(8,128)(2,1)} %w_ref.3), custom_call_target="tpu_custom_call" | custom-call | tf_op jit(solution)/shard_map/query_prep/pallas_call | solution.py:92
  45.7 14.7 %shard_map.145 = (f32[16,128,128]{2,1,0:T(8,128)}, f32[16,128,512]{2,1,0:T(8,128)}) custom-call(s32[8]{0:T(128)} %pad_add_fusion.sc_ref.refs_0_, bf16[16,128,512]{2,1,0:T(8,128)(2,1)} %get-tuple-element.13.refs_1_, bf16[16,128,64]{2,1,0:T(8,128)(2,1)} %get-tuple-element.14.refs_2_, bf16[128,512]{1,0:T(8,128)(2,1)} %refs_3_.1, bf16[64,128]{1,0:T(8,128)(2,1)} %refs_4_.1, ...), custom_call_target="tpu_custom_call" | custom-call | tf_op jit(solution)/shard_map/pallas_call | solution.py:234
  61.4 16.4 %shard_map.146 = (f32[16,128,128]{2,1,0:T(8,128)}, f32[16,128,512]{2,1,0:T(8,128)}) custom-call(s32[8]{0:T(128)} %pad_add_fusion.sc_ref.refs_0_, bf16[16,128,512]{2,1,0:T(8,128)(2,1)} %get-tuple-element.13.refs_1_, bf16[16,128,64]{2,1,0:T(8,128)(2,1)} %get-tuple-element.14.refs_2_, f32[16,128,128]{2,1,0:T(8,128)} %get-tuple-element.15.refs_3_, ...), custom_call_target="tpu_custom_call" | custom-call | tf_op jit(solution)/shard_map/pallas_call | solution.py:234
  78.6 13.3 %shard_map.147.o_ref = bf16[16,128,512]{2,1,0:T(8,128)(2,1)} custom-call(s32[8]{0:T(128)} %pad_add_fusion.sc_ref.refs_0_, bf16[16,128,512]{2,1,0:T(8,128)(2,1)} %get-tuple-element.13.refs_1_, bf16[16,128,64]{2,1,0:T(8,128)(2,1)} %get-tuple-element.14.refs_2_, f32[16,128,128]{2,1,0:T(8,128)} %get-tuple-element.17.refs_3_, ...), custom_call_target="tpu_custom_call" | custom-call | tf_op jit(solution)/shard_map/pallas_call | solution.py:234
  91.9 9.5 %project.1 = (bf16[128,2048]{1,0:T(8,128)(2,1)}, bf16[128,2048]{1,0:T(8,128)(2,1)}) custom-call(s32[8]{0:T(128)} %pad_add_fusion.sc_ref.refs_0_, bf16[16,128,512]{2,1,0:T(8,128)(2,1)} %shard_map.147.o_ref, bf16[512,4096]{1,0:T(8,128)(2,1)} %w_ref.3, bf16[2048,2048]{1,0:T(8,128)(2,1)} %wo_ref.1, bf16[128,2048]{1,0:T(8,128)(2,1)} %res_ref.1, ...), custom_call_target="tpu_custom_call" | custom-call | tf_op jit(solution)/shard_map/project/pallas_call | solution.py:274
  101.4 4.1 %shard_map.148 = bf16[128,8,2048]{2,1,0:T(8,128)(2,1)} custom-call(s32[6,128]{1,0:T(8,128)} %bitcast.36, bf16[128,2048]{1,0:T(8,128)(2,1)} %get-tuple-element.20.norm_ref), custom_call_target="tpu_custom_call" | custom-call | tf_op jit(solution)/shard_map/pallas_call | solution.py:390
  105.5 11.6 %all-to-all-start = ((bf16[128,8,2048]{2,1,0:T(8,128)(2,1)}), bf16[128,8,2048]{2,1,0:T(8,128)(2,1)}, u32[]{:S(2)}, u32[]{:S(2)}) async-start(bf16[128,8,2048]{2,1,0:T(8,128)(2,1)} %shard_map.148), calls=%async_computation | async-start | bytes 8388608 | tf_op jit(solution)/shard_map/all_to_all | solution.py:552
  117.2 4.3 %shard_map.151 = bf16[128,8,1280]{2,1,0:T(8,128)(2,1)} custom-call(s32[6,128]{1,0:T(8,128)} %bitcast.37, bf16[128,2048]{1,0:T(8,128)(2,1)} %get-tuple-element.20.norm_ref), custom_call_target="tpu_custom_call" | custom-call | tf_op jit(solution)/shard_map/pallas_call | solution.py:390
  121.5 44.5 %all-to-all-done.x_ref = bf16[128,8,2048]{2,1,0:T(8,128)(2,1)} async-done(((bf16[128,8,2048]{2,1,0:T(8,128)(2,1)}), bf16[128,8,2048]{2,1,0:T(8,128)(2,1)}, u32[]{:S(2)}, u32[]{:S(2)}) %all-to-all-start) | async-done | bytes 4194336 | tf_op jit(solution)/shard_map/all_to_all | solution.py:552
  166.0 7.7 %all-to-all-start.2 = ((bf16[128,8,1280]{2,1,0:T(8,128)(2,1)}), bf16[128,8,1280]{2,1,0:T(8,128)(2,1)S(1)}, u32[]{:S(2)}, u32[]{:S(2)}) async-start(bf16[128,8,1280]{2,1,0:T(8,128)(2,1)} %shard_map.151), calls=%async_computation.2 | async-start | bytes 5242880 | tf_op jit(solution)/shard_map/all_to_all | solution.py:552
  173.7 15.6 %shard_map.149 = bf16[128,8,2048]{2,1,0:T(8,128)(2,1)} custom-call(bf16[128,8,2048]{2,1,0:T(8,128)(2,1)} %all-to-all-done.x_ref, bf16[1,2048,1408]{2,1,0:T(8,128)(2,1)} %wg_ref.3, bf16[1,704,2048]{2,1,0:T(8,128)(2,1)} %wd_ref.3), custom_call_target="tpu_custom_call" | custom-call | tf_op jit(solution)/shard_map/pallas_call | solution.py:442
  189.3 16.9 %all-to-all-done.2.x_ref = bf16[128,8,1280]{2,1,0:T(8,128)(2,1)S(1)} async-done(((bf16[128,8,1280]{2,1,0:T(8,128)(2,1)}), bf16[128,8,1280]{2,1,0:T(8,128)(2,1)S(1)}, u32[]{:S(2)}, u32[]{:S(2)}) %all-to-all-start.2) | async-done | bytes 2621472 | tf_op jit(solution)/shard_map/all_to_all | solution.py:552
  207.8 8.5 %all-to-all-start.1 = ((bf16[128,8,2048]{2,1,0:T(8,128)(2,1)}), bf16[128,8,2048]{2,1,0:T(8,128)(2,1)}, u32[]{:S(2)}, u32[]{:S(2)}) async-start(bf16[128,8,2048]{2,1,0:T(8,128)(2,1)} %shard_map.149), calls=%async_computation.1 | async-start | bytes 8388608 | tf_op jit(solution)/shard_map/all_to_all | solution.py:552
  216.3 15.5 %shard_map.152 = bf16[128,8,1280]{2,1,0:T(8,128)(2,1)} custom-call(bf16[128,8,1280]{2,1,0:T(8,128)(2,1)} %copy-done.1, bf16[1,2048,1408]{2,1,0:T(8,128)(2,1)} %wg_ref.3, bf16[1,704,2048]{2,1,0:T(8,128)(2,1)} %wd_ref.3), custom_call_target="tpu_custom_call" | custom-call | tf_op jit(solution)/shard_map/pallas_call | solution.py:442
  231.8 33.3 %all-to-all-done.1.back_ref = bf16[128,8,2048]{2,1,0:T(8,128)(2,1)} async-done(((bf16[128,8,2048]{2,1,0:T(8,128)(2,1)}), bf16[128,8,2048]{2,1,0:T(8,128)(2,1)}, u32[]{:S(2)}, u32[]{:S(2)}) %all-to-all-start.1) | async-done | bytes 4194336 | tf_op jit(solution)/shard_map/all_to_all | solution.py:552
  265.1 7.7 %all-to-all-start.3 = ((bf16[128,8,1280]{2,1,0:T(8,128)(2,1)}), bf16[128,8,1280]{2,1,0:T(8,128)(2,1)S(1)}, u32[]{:S(2)}, u32[]{:S(2)}) async-start(bf16[128,8,1280]{2,1,0:T(8,128)(2,1)} %shard_map.152), calls=%async_computation.3 | async-start | bytes 5242880 | tf_op jit(solution)/shard_map/all_to_all | solution.py:552
  272.8 5.3 %shard_map.150.sum_ref = f32[128,2048]{1,0:T(8,128)} custom-call(s32[6,128]{1,0:T(8,128)} %bitcast.38, f32[6,128]{1,0:T(8,128)} %bitcast.40, bf16[128,2048]{1,0:T(8,128)(2,1)} %get-tuple-element.19.hid_ref, bf16[128,8,2048]{2,1,0:T(8,128)(2,1)} %all-to-all-done.1.back_ref), custom_call_target="tpu_custom_call" | custom-call | tf_op jit(solution)/shard_map/pallas_call | solution.py:506
  278.1 27.2 %all-to-all-done.3.back_ref = bf16[128,8,1280]{2,1,0:T(8,128)(2,1)S(1)} async-done(((bf16[128,8,1280]{2,1,0:T(8,128)(2,1)}), bf16[128,8,1280]{2,1,0:T(8,128)(2,1)S(1)}, u32[]{:S(2)}, u32[]{:S(2)}) %all-to-all-start.3) | async-done | bytes 2621472 | tf_op jit(solution)/shard_map/all_to_all | solution.py:552
  306.8 5.9 %shard_map.153 = bf16[128,2048]{1,0:T(8,128)(2,1)} custom-call(s32[6,128]{1,0:T(8,128)} %bitcast.39, f32[6,128]{1,0:T(8,128)} %bitcast.41, f32[128,2048]{1,0:T(8,128)} %shard_map.150.sum_ref, bf16[128,8,1280]{2,1,0:T(8,128)(2,1)} %copy-done), custom_call_target="tpu_custom_call" | custom-call | tf_op jit(solution)/shard_map/pallas_call | solution.py:506
  (54 shorter events, 21.9 us)
Async XLA Ops:
  1.8 4.8 %collective-permute-start = (bf16[144,512]{1,0:T(8,128)(2,1)S(1)}, bf16[144,512]{1,0:T(8,128)(2,1)S(1)}, u32[]{:S(2)}, u32[]{:S(2)}) collective-permute-start(bf16[144,512]{1,0:T(8,128)(2,1)S(1)} %pad_maximum_fusion), channel_id=1, source_target_pairs={{0,4},{1,5},{2,6},{3,7},{4,8},{5,9},{6,10},{7,11},{8,12},{9,13},{1... | collective-permute-start | bytes 442376 | tf_op jit(solution)/shard_map/ppermute | solution.py:531
  2.8 4.5 %collective-permute-start.1 = (bf16[144,512]{1,0:T(8,128)(2,1)S(1)}, bf16[144,512]{1,0:T(8,128)(2,1)S(1)}, u32[]{:S(2)}, u32[]{:S(2)}) collective-permute-start(bf16[144,512]{1,0:T(8,128)(2,1)S(1)} %pad_maximum_fusion), channel_id=1, source_target_pairs={{0,12},{1,13},{2,14},{3,15},{4,0},{5,1},{6,2},{7,3},{8,4},{9,5},{1... | collective-permute-start | bytes 442376 | tf_op jit(solution)/shard_map/ppermute | solution.py:531
  3.3 6.0 %collective-permute-start.2 = (bf16[144,512]{1,0:T(8,128)(2,1)S(1)}, bf16[144,512]{1,0:T(8,128)(2,1)S(1)}, u32[]{:S(2)}, u32[]{:S(2)}) collective-permute-start(bf16[144,512]{1,0:T(8,128)(2,1)S(1)} %pad_maximum_fusion), channel_id=1, source_target_pairs={{0,8},{1,9},{2,10},{3,11},{4,12},{5,13},{6,14},{7,15},{8,0},{9,1},... | collective-permute-start | bytes 442376 | tf_op jit(solution)/shard_map/ppermute | solution.py:531
  9.3 36.4 %copy-start.3 = (bf16[576,512]{1,0:T(8,128)(2,1)}, bf16[576,512]{1,0:T(8,128)(2,1)S(1)}, u32[]{:S(2)}) copy-start(bf16[576,512]{1,0:T(8,128)(2,1)S(1)} %constant_dynamic-update-slice_fusion.refs_5_) | copy-start | bytes 1769476
  9.3 24.4 %collective-permute-start.6 = (bf16[576,512]{1,0:T(8,128)(2,1)S(1)}, bf16[576,512]{1,0:T(8,128)(2,1)S(1)}, u32[]{:S(2)}, u32[]{:S(2)}) collective-permute-start(bf16[576,512]{1,0:T(8,128)(2,1)S(1)} %constant_dynamic-update-slice_fusion.refs_5_), channel_id=1, source_target_pairs={{0,1},{1,2},{2,3},{3,0},{4,5},{5,6},{6,7},{7,4},{8,9},{9,10},{10,1... | collective-permute-start | bytes 1769480 | tf_op jit(solution)/shard_map/ppermute | solution.py:531
  10.7 16.1 %collective-permute-start.3 = (bf16[144,512]{1,0:T(8,128)(2,1)S(1)}, bf16[144,512]{1,0:T(8,128)(2,1)S(1)}, u32[]{:S(2)}, u32[]{:S(2)}) collective-permute-start(bf16[144,512]{1,0:T(8,128)(2,1)S(1)} %pad_maximum_fusion.1), channel_id=1, source_target_pairs={{0,1},{1,2},{2,3},{3,0},{4,5},{5,6},{6,7},{7,4},{8,9},{9,10},{10,1... | collective-permute-start | bytes 442376 | tf_op jit(solution)/shard_map/ppermute | solution.py:531
  12.1 14.8 %collective-permute-start.4 = (bf16[144,512]{1,0:T(8,128)(2,1)S(1)}, bf16[144,512]{1,0:T(8,128)(2,1)S(1)}, u32[]{:S(2)}, u32[]{:S(2)}) collective-permute-start(bf16[144,512]{1,0:T(8,128)(2,1)S(1)} %pad_maximum_fusion.1), channel_id=1, source_target_pairs={{0,3},{1,0},{2,1},{3,2},{4,7},{5,4},{6,5},{7,6},{8,11},{9,8},{10,9... | collective-permute-start | bytes 442376 | tf_op jit(solution)/shard_map/ppermute | solution.py:531
  13.5 17.3 %collective-permute-start.5 = (bf16[144,512]{1,0:T(8,128)(2,1)S(1)}, bf16[144,512]{1,0:T(8,128)(2,1)S(1)}, u32[]{:S(2)}, u32[]{:S(2)}) collective-permute-start(bf16[144,512]{1,0:T(8,128)(2,1)S(1)} %pad_maximum_fusion.1), channel_id=1, source_target_pairs={{0,2},{1,3},{2,0},{3,1},{4,6},{5,7},{6,4},{7,5},{8,10},{9,11},{10,... | collective-permute-start | bytes 442376 | tf_op jit(solution)/shard_map/ppermute | solution.py:531
  14.9 45.5 %collective-permute-start.7 = (bf16[576,512]{1,0:T(8,128)(2,1)S(1)}, bf16[576,512]{1,0:T(8,128)(2,1)S(1)}, u32[]{:S(2)}, u32[]{:S(2)}) collective-permute-start(bf16[576,512]{1,0:T(8,128)(2,1)S(1)} %constant_dynamic-update-slice_fusion.refs_5_), channel_id=1, source_target_pairs={{0,3},{1,0},{2,1},{3,2},{4,7},{5,4},{6,5},{7,6},{8,11},{9,8},{10,9... | collective-permute-start | bytes 1769480 | tf_op jit(solution)/shard_map/ppermute | solution.py:531
  30.8 14.9 %copy-start.2 = (bf16[576,512]{1,0:T(8,128)(2,1)}, bf16[576,512]{1,0:T(8,128)(2,1)S(1)}, u32[]{:S(2)}) copy-start(bf16[576,512]{1,0:T(8,128)(2,1)S(1)} %constant_dynamic-update-slice_fusion.5.refs_6_) | copy-start | bytes 1769476
  30.8 29.6 %collective-permute-start.8 = (bf16[576,512]{1,0:T(8,128)(2,1)S(1)}, bf16[576,512]{1,0:T(8,128)(2,1)S(1)}, u32[]{:S(2)}, u32[]{:S(2)}) collective-permute-start(bf16[576,512]{1,0:T(8,128)(2,1)S(1)} %constant_dynamic-update-slice_fusion.5.refs_6_), channel_id=1, source_target_pairs={{0,4},{1,5},{2,6},{3,7},{4,8},{5,9},{6,10},{7,11},{8,12},{9,13},{1... | collective-permute-start | bytes 1769480 | tf_op jit(solution)/shard_map/ppermute | solution.py:531
  33.1 27.3 %collective-permute-start.9 = (bf16[576,512]{1,0:T(8,128)(2,1)S(1)}, bf16[576,512]{1,0:T(8,128)(2,1)}, u32[]{:S(2)}, u32[]{:S(2)}) collective-permute-start(bf16[576,512]{1,0:T(8,128)(2,1)S(1)} %constant_dynamic-update-slice_fusion.5.refs_6_), channel_id=1, source_target_pairs={{0,12},{1,13},{2,14},{3,15},{4,0},{5,1},{6,2},{7,3},{8,4},{9,5},{1... | collective-permute-start | bytes 1769480 | tf_op jit(solution)/shard_map/ppermute | solution.py:531
  33.4 44.4 %collective-permute-start.10 = (bf16[576,512]{1,0:T(8,128)(2,1)S(1)}, bf16[576,512]{1,0:T(8,128)(2,1)S(1)}, u32[]{:S(2)}, u32[]{:S(2)}) collective-permute-start(bf16[576,512]{1,0:T(8,128)(2,1)S(1)} %constant_dynamic-update-slice_fusion.refs_5_), channel_id=1, source_target_pairs={{0,2},{1,3},{2,0},{3,1},{4,6},{5,7},{6,4},{7,5},{8,10},{9,11},{10,... | collective-permute-start | bytes 1769480 | tf_op jit(solution)/shard_map/ppermute | solution.py:531
  33.7 26.6 %copy-start.4 = (bf16[576,512]{1,0:T(8,128)(2,1)}, bf16[576,512]{1,0:T(8,128)(2,1)S(1)}, u32[]{:S(2)}) copy-start(bf16[576,512]{1,0:T(8,128)(2,1)S(1)} %collective-permute-done.6.refs_5_) | copy-start | bytes 1769476
  33.7 44.1 %collective-permute-start.11 = (bf16[576,512]{1,0:T(8,128)(2,1)S(1)}, bf16[576,512]{1,0:T(8,128)(2,1)}, u32[]{:S(2)}, u32[]{:S(2)}) collective-permute-start(bf16[576,512]{1,0:T(8,128)(2,1)S(1)} %constant_dynamic-update-slice_fusion.5.refs_6_), channel_id=1, source_target_pairs={{0,8},{1,9},{2,10},{3,11},{4,12},{5,13},{6,14},{7,15},{8,0},{9,1},... | collective-permute-start | bytes 1769480 | tf_op jit(solution)/shard_map/ppermute | solution.py:531
  60.4 0.8 copy-start.5
  60.4 1.0 copy-start.7
  77.8 0.8 copy-start.6
  105.5 60.4 %all-to-all-start = ((bf16[128,8,2048]{2,1,0:T(8,128)(2,1)}), bf16[128,8,2048]{2,1,0:T(8,128)(2,1)}, u32[]{:S(2)}, u32[]{:S(2)}) async-start(bf16[128,8,2048]{2,1,0:T(8,128)(2,1)} %shard_map.148), calls=%async_computation | async-start | bytes 8388608 | tf_op jit(solution)/shard_map/all_to_all | solution.py:552
  166.0 40.2 %all-to-all-start.2 = ((bf16[128,8,1280]{2,1,0:T(8,128)(2,1)}), bf16[128,8,1280]{2,1,0:T(8,128)(2,1)S(1)}, u32[]{:S(2)}, u32[]{:S(2)}) async-start(bf16[128,8,1280]{2,1,0:T(8,128)(2,1)} %shard_map.151), calls=%async_computation.2 | async-start | bytes 5242880 | tf_op jit(solution)/shard_map/all_to_all | solution.py:552
  206.2 1.6 copy-start.1
  207.8 57.3 %all-to-all-start.1 = ((bf16[128,8,2048]{2,1,0:T(8,128)(2,1)}), bf16[128,8,2048]{2,1,0:T(8,128)(2,1)}, u32[]{:S(2)}, u32[]{:S(2)}) async-start(bf16[128,8,2048]{2,1,0:T(8,128)(2,1)} %shard_map.149), calls=%async_computation.1 | async-start | bytes 8388608 | tf_op jit(solution)/shard_map/all_to_all | solution.py:552
  265.1 40.2 %all-to-all-start.3 = ((bf16[128,8,1280]{2,1,0:T(8,128)(2,1)}), bf16[128,8,1280]{2,1,0:T(8,128)(2,1)S(1)}, u32[]{:S(2)}, u32[]{:S(2)}) async-start(bf16[128,8,1280]{2,1,0:T(8,128)(2,1)} %shard_map.152), calls=%async_computation.3 | async-start | bytes 5242880 | tf_op jit(solution)/shard_map/all_to_all | solution.py:552
  305.3 1.5 copy-start
where the time goes:
time: 318 us; the launch traced here: 313 us
  waiting for transfers between devices  140 us (44%)
  Pallas kernels  110 us (35%)
  starting transfers between devices  51.5 us (16%)
  local copies, waits for them, and re-layouts  9.01 us (3%)
    all_to_all x4, waiting for transfers between devices, exchange(): lax.all_to_all(a, ('req', 'wide'), split_axis=0, concat_axis=0, tiled=True)  122 us
    pallas_call x3, Pallas kernels, attend(): pl.pallas_call(lambda *refs: attention_kernel(n_pieces, stage, *refs), ou...  44.4 us
    all_to_all x4, starting transfers between devices, exchange(): lax.all_to_all(a, ('req', 'wide'), split_axis=0, concat_axis=0, tiled=True)  35.5 us
    pallas_call x2, Pallas kernels, run_expert(): pl.pallas_call(kernel, out_shape=jax.ShapeDtypeStruct(rows.shape, bf16),...  31.1 us
    ppermute x12, waiting for transfers between devices, hop(): return lax.ppermute(a, 'wide', shift(axis, k))  18.3 us
    ppermute x12, starting transfers between devices, hop(): return lax.ppermute(a, 'wide', shift(axis, k))  15.9 us
    pallas_call x2, Pallas kernels, combine(): pl.pallas_call(kernel, out_shape=jax.ShapeDtypeStruct((TOK, D), out_type)...  11.2 us
    pallas_call x1, Pallas kernels, project(): pl.pallas_call(project_kernel, out_shape=(jax.ShapeDtypeStruct((TOK, D),...  9.5 us
  transfers between devices with their start and end apart: 16, of which 9 were waited for; matrix products, arithmetic and copies ran while one was open for 1% of the time, Pallas kernels for 25%

commit v1 on v0

--- a/solution.py
+++ b/solution.py
@@ -63,6 +63,10 @@
     return jnp.where(place_of(tokens, starts, bases) == slots, 1.0, 0.0).astype(bf16)
 
 
+def grant(mib):
+    return pltpu.CompilerParams(vmem_limit_bytes=mib << 20)
+
+
 def mm(a, b):
     return jnp.dot(a, b, preferred_element_type=f32)
 
@@ -109,6 +113,7 @@
             ],
         ),
         name="query_prep",
+        compiler_params=grant(24),
     )(scalars, queries, queries, w_ukv)
 
 
@@ -212,7 +217,7 @@
         acc_out[...] = acc_scr[...].reshape(HEADS, TILE, LAT)
 
 
-FIRST, MIDDLE, LAST = 0, 1, 2
+FIRST, LAST = 0, 2
 
 
 def attend(stage, scalars, qa, qr, local, pieces0, pieces1):
@@ -237,7 +242,7 @@
         grid_spec=pltpu.PrefetchScalarGridSpec(
             num_scalar_prefetch=1,
             grid=(TOK // TILE,),
-            in_specs=[tiled(LAT), tiled(ROPE), *local_specs, *[whole(a) for a in pieces]],
+            in_specs=[tiled(LAT), tiled(ROPE), *local_specs, *[pl.BlockSpec(memory_space=pltpu.VMEM) for _ in pieces]],
             out_specs=out_specs,
             scratch_shapes=[
                 pltpu.VMEM((max(keys // 4, 1), ROWS, 512), f32),
@@ -246,6 +251,7 @@
                 pltpu.VMEM((ROWS, LAT), f32),
             ],
         ),
+        compiler_params=grant(24),
     )(scalars, qa, qr, *local, *pieces)
 
 
@@ -294,6 +300,7 @@
             scratch_shapes=[pltpu.VMEM((TOK, D), f32)],
         ),
         name="project",
+        compiler_params=grant(24),
     )(scalars, o_lat, w_ukv, w_out, residual, gain)
 
 
@@ -397,6 +404,7 @@
         ],
         out_specs=pl.BlockSpec((2 * EG, 8, width), lambda i: (i, 0, 0)),
         scratch_shapes=[pltpu.VMEM((EXPERTS, TOK), f32)],
+        compiler_params=grant(32),
     )(ids_t, normed)
 
 
@@ -449,6 +457,7 @@
             pl.BlockSpec(w_down.shape, lambda i: (0, 0, 0), pipeline_mode=pl.Buffered(1)),
         ],
         out_specs=pl.BlockSpec((per, 8, width), lambda i: (i, 0, 0)),
+        compiler_params=grant(32),
     )(rows, w_gate_up, w_down)
 
 
@@ -459,6 +468,9 @@
     return both[:TOK] + both[TOK:]
 
 
+CG = 16
+
+
 def combine_kernel(ids_ref, gates_ref, hid_ref, back_ref, out_ref, rank_scr, gate_scr):
     step = pl.program_id(0)
 
@@ -468,53 +480,51 @@
         gate_scr[...] = gate_table(ids_ref, gates_ref)
         out_ref[...] = hid_ref[...].astype(f32)
 
-    ranks = rank_scr[pl.ds(step * EG, EG), :]
-    gates = gate_scr[pl.ds(step * EG, EG), :]
-    back = back_ref[...].reshape(2 * EG * SLOTS_A, D)
-    out_ref[...] += weighted(whole_rows(ranks, EG, 2, gates), back)
-
-
-def combine_packed_kernel(
-    ids_ref, gates_ref, sum_ref, back_ref, out_ref, rank_scr, gate_scr, acc_ref
-):
-    step = pl.program_id(0)
-
-    @pl.when(step == 0)
-    def _():
-        rank_scr[...] = rank_table(ids_ref)
-        gate_scr[...] = gate_table(ids_ref, gates_ref)
-        acc_ref[...] = sum_ref[...]
-
-    ranks = rank_scr[pl.ds(step * EG, EG), :]
-    gates = gate_scr[pl.ds(step * EG, EG), :]
-    back = back_ref[...].reshape(2 * EG * 8, WIDTH_B)
-    lower, upper, last = packed_rows(ranks, EG, 2, gates)
-    acc_ref[:, :HALF] += weighted(lower, back[:, :HALF])
-    acc_ref[:, HALF:] += weighted(upper, back[:, :HALF])
-    for q, piece in enumerate(pieces_of(last)):
-        acc_ref[:, q * PIECE : (q + 1) * PIECE] += weighted(piece, back[:, HALF:])
-
-    @pl.when(step == EXPERTS // EG - 1)
-    def _():
-        out_ref[...] = acc_ref[...].astype(bf16)
-
-
-def combine(kernel, ids_t, gates_t, base, back, out_type):
-    scratch = [pltpu.VMEM((EXPERTS, TOK), f32), pltpu.VMEM((EXPERTS, TOK), f32)]
-    if out_type == bf16:
-        scratch.append(pltpu.VMEM((TOK, D), f32))
+    ranks = rank_scr[pl.ds(step * CG, CG), :]
+    gates = gate_scr[pl.ds(step * CG, CG), :]
+    back = back_ref[...].reshape(2 * CG * SLOTS_A, D)
+    out_ref[...] += weighted(whole_rows(ranks, CG, 2, gates), back)
+
+
+def combine(ids_t, gates_t, hidden, back):
     return pl.pallas_call(
-        kernel,
-        out_shape=jax.ShapeDtypeStruct((TOK, D), out_type),
-        grid=(EXPERTS // EG,),
+        combine_kernel,
+        out_shape=jax.ShapeDtypeStruct((TOK, D), f32),
+        grid=(EXPERTS // CG,),
         in_specs=[
             pl.BlockSpec((TOP, TOK), lambda i: (0, 0)),
             pl.BlockSpec((TOP, TOK), lambda i: (0, 0)),
             pl.BlockSpec((TOK, D), lambda i: (0, 0)),
-            pl.BlockSpec((2 * EG, 8, back.shape[2]), lambda i: (i, 0, 0)),
+            pl.BlockSpec((2 * CG, 8, D), lambda i: (i, 0, 0)),
         ],
         out_specs=pl.BlockSpec((TOK, D), lambda i: (0, 0)),
-        scratch_shapes=scratch,
+        scratch_shapes=[pltpu.VMEM((EXPERTS, TOK), f32), pltpu.VMEM((EXPERTS, TOK), f32)],
+        name="combine_a",
+        compiler_params=grant(32),
+    )(ids_t, gates_t, hidden, back)
+
+
+def combine_packed_kernel(ids_ref, gates_ref, sum_ref, back_ref, out_ref, acc_ref):
+    ranks = rank_table(ids_ref)
+    gates = gate_table(ids_ref, gates_ref)
+    back = back_ref[...].reshape(2 * EXPERTS * 8, WIDTH_B)
+    lower, upper, last = packed_rows(ranks, EXPERTS, 2, gates)
+    acc_ref[:, :HALF] = sum_ref[:, :HALF] + weighted(lower, back[:, :HALF])
+    acc_ref[:, HALF:] = sum_ref[:, HALF:] + weighted(upper, back[:, :HALF])
+    for q, piece in enumerate(pieces_of(last)):
+        acc_ref[:, q * PIECE : (q + 1) * PIECE] += weighted(piece, back[:, HALF:])
+    out_ref[...] = acc_ref[...].astype(bf16)
+
+
+def combine_packed(ids_t, gates_t, base, back):
+    return pl.pallas_call(
+        combine_packed_kernel,
+        out_shape=jax.ShapeDtypeStruct((TOK, D), bf16),
+        in_specs=[pl.BlockSpec(memory_space=pltpu.VMEM)] * 4,
+        out_specs=pl.BlockSpec(memory_space=pltpu.VMEM),
+        scratch_shapes=[pltpu.VMEM((TOK, D), f32)],
+        name="combine_b",
+        compiler_params=grant(24),
     )(ids_t, gates_t, base, back)
 
 
@@ -532,15 +542,14 @@
 
 
 def gather_row(own, first):
-    ahead, behind = hop(own, first, 1), hop(own, first, -1)
-    far = hop(own, first, 2)
-    return jnp.concatenate([own, ahead, behind, far], axis=0)
+    return jnp.concatenate([own, hop(own, first, 1), hop(own, first, -1), hop(own, first, 2)], axis=0)
 
 
 def gather_rest(row, second):
     ahead, behind = hop(row, second, 1), hop(row, second, -1)
-    far = hop(row, second, 2)
-    return ahead, behind, far
+    half = row.shape[0] // 2
+    far0, far1 = hop(ahead[:half], second, 1), hop(behind[half:], second, -1)
+    return [ahead, behind, far0, far1]
 
 
 def pack_prefix(latent, rope):
@@ -572,12 +581,11 @@
     scalars = jnp.concatenate([suffix_lengths[0], prefix_ids[0]])
     row0 = gather_row(pack_prefix(prefix_latent[0, 0], prefix_rope[0, 0]), "x")
     row1 = gather_row(pack_prefix(prefix_latent[0, 1], prefix_rope[0, 1]), "y")
+    rest0 = gather_rest(row0, "y")
+    rest1 = gather_rest(row1, "x")
     qa, qr = prepare_queries(scalars, queries, w_ukv)
-    ahead0, behind0, far0 = gather_rest(row0, "y")
-    ahead1, behind1, far1 = gather_rest(row1, "x")
     state = attend(FIRST, scalars, qa, qr, (suffix_latent, suffix_rope), [row0], [row1])
-    state = attend(MIDDLE, scalars, qa, qr, state, [ahead0, behind0], [ahead1, behind1])
-    o_lat = attend(LAST, scalars, qa, qr, state, [far0], [far1])
+    o_lat = attend(LAST, scalars, qa, qr, state, rest0, rest1)
     hidden, normed = project(scalars, o_lat, w_ukv, w_out, residual, norm_gain.reshape(1, D))
     ids_t = expert_ids.T
     gates_t = gate_values.T
@@ -589,8 +597,8 @@
     made_b = run_expert(expert_packed_kernel, rows_b, expert_gate_up, expert_down)
     back_a = exchange(made_a)
     back_b = exchange(made_b)
-    part = combine(combine_kernel, ids_t, gates_t, hidden, back_a, f32)
-    return combine(combine_packed_kernel, ids_t, gates_t, part, back_b, bf16)
+    part = combine(ids_t, gates_t, hidden, back_a)
+    return combine_packed(ids_t, gates_t, part, back_b)
 
 
 def solution(mesh):

time: 318 us -> 285 us (0.90)
  Pallas kernels: 110 us -> 72.2 us
  local copies, waits for them, and re-layouts: 9.01 us -> 18.9 us
  waiting for transfers between devices: 140 us -> 134 us
    pallas_call x3 -> x2, Pallas kernels: 44.4 us -> 30.2 us  [attend(): pl.pallas_call(lambda *refs: attention_kernel(n_pieces, stage, *refs), ou...]
    unnamed x25 -> x55, local copies, waits for them, and re-layouts: 5.96 us -> 16.4 us
    pallas_call x2, Pallas kernels: 31.1 us -> 24.1 us  [run_expert(): pl.pallas_call(kernel, out_shape=jax.ShapeDtypeStruct(rows.shape, bf16),...]
    ppermute x12 -> x14, waiting for transfers between devices: 18.3 us -> 13.1 us  [hop(): return lax.ppermute(a, 'wide', shift(axis, k))]
    pallas_call x2, Pallas kernels: 8.41 us -> 3.22 us  [dispatch(): pl.pallas_call(kernel, out_shape=jax.ShapeDtypeStruct((2 * EXPERTS, 8, wi...]
    pallas_call x1, Pallas kernels: 9.5 us -> 4.54 us  [project(): pl.pallas_call(project_kernel, out_shape=(jax.ShapeDtypeStruct((TOK, D),...]
    pallas_call x2, Pallas kernels: 11.2 us -> 7.46 us  [the longest x1 4.13 us: combine(): pl.pallas_call(combine_kernel, out_shape=jax.ShapeDtypeStruct((TOK, D), f...]
    pallas_call x1, Pallas kernels: 5.92 us -> 2.66 us  [prepare_queries(): pl.pallas_call(query_kernel, out_shape=(jax.ShapeDtypeStruct((HEADS, TOK,...]
  transfers between devices with their start and end apart: 16 -> 18, of which waited for: 9 -> 9; matrix products, arithmetic and copies ran while one was open for 1% -> 0% of each run, Pallas kernels for 25% -> 16%
where the time goes in v1:
time: 285 us; the launch traced here: 280 us
  waiting for transfers between devices  134 us (47%)
  Pallas kernels  72.2 us (25%)
  starting transfers between devices  54.6 us (19%)
  local copies, waits for them, and re-layouts  18.9 us (7%)
    all_to_all x4, waiting for transfers between devices, exchange(): lax.all_to_all(a, ('req', 'wide'), split_axis=0, concat_axis=0, tiled=True)  121 us
    all_to_all x4, starting transfers between devices, exchange(): lax.all_to_all(a, ('req', 'wide'), split_axis=0, concat_axis=0, tiled=True)  38.5 us
    pallas_call x2, Pallas kernels, attend(): pl.pallas_call(lambda *refs: attention_kernel(n_pieces, stage, *refs), ou...  30.2 us
    pallas_call x2, Pallas kernels, run_expert(): pl.pallas_call(kernel, out_shape=jax.ShapeDtypeStruct(rows.shape, bf16),...  24.1 us
    unnamed x55, local copies, waits for them, and re-layouts  16.4 us
    ppermute x14, starting transfers between devices, hop(): return lax.ppermute(a, 'wide', shift(axis, k))  16.1 us
    ppermute x14, waiting for transfers between devices, hop(): return lax.ppermute(a, 'wide', shift(axis, k))  13.1 us
  transfers between devices with their start and end apart: 18, of which 9 were waited for; matrix products, arithmetic and copies ran while one was open for 0% of the time, Pallas kernels for 16%

profile of v1, /device:TPU:37, one launch (start us, length us, event | category | flops | bytes accessed | tf_op | source)
XLA Modules:
  0.0 280.2 jit_solution(3986444012338695815)
XLA Ops:
  12.8 3.7 %collective-permute-done.5 = bf16[144,512]{1,0:T(8,128)(2,1)S(1)} collective-permute-done((bf16[144,512]{1,0:T(8,128)(2,1)S(1)}, bf16[144,512]{1,0:T(8,128)(2,1)S(1)}, u32[]{:S(2)}, u32[]{:S(2)}) %collective-permute-start.5) | collective-permute-done | bytes 147488 | tf_op jit(solution)/shard_map/ppermute | solution.py:541
  18.4 2.4 collective-permute-start.7
  20.9 7.0 %collective-permute-done.10.refs_9_ = bf16[576,512]{1,0:T(8,128)(2,1)S(1)} collective-permute-done((bf16[576,512]{1,0:T(8,128)(2,1)S(1)}, bf16[576,512]{1,0:T(8,128)(2,1)S(1)}, u32[]{:S(2)}, u32[]{:S(2)}) %collective-permute-start.10) | collective-permute-done | bytes 589856 | tf_op jit(solution)/shard_map/ppermute | solution.py:541
  30.3 2.7 collective-permute-start.9
  33.1 2.7 query_prep.1
  35.8 12.7 %shard_map.145 = (f32[16,128,128]{2,1,0:T(8,128)S(1)}, f32[16,128,512]{2,1,0:T(8,128)S(1)}) custom-call(s32[8]{0:T(128)S(1)} %pad_add_fusion.sc_ref.refs_0_, bf16[16,128,512]{2,1,0:T(8,128)(2,1)S(1)} %get-tuple-element.11.refs_1_, bf16[16,128,64]{2,1,0:T(8,128)(2,1)S(1)} %get-tuple-element.12.refs_2_, bf16[128,512]{1,0:T(8,128)(2,1)S(1)} %copy-done.14, ...), custom_call_target="tpu_custom_call" | custom-call | tf_op jit(solution)/shard_map/pallas_call | solution.py:239
  48.5 17.6 %shard_map.146.o_ref = bf16[16,128,512]{2,1,0:T(8,128)(2,1)S(1)} custom-call(s32[8]{0:T(128)S(1)} %pad_add_fusion.sc_ref.refs_0_, bf16[16,128,512]{2,1,0:T(8,128)(2,1)S(1)} %get-tuple-element.11.refs_1_, bf16[16,128,64]{2,1,0:T(8,128)(2,1)S(1)} %get-tuple-element.12.refs_2_, f32[16,128,128]{2,1,0:T(8,128)S(1)} %get-tuple-element.13.refs_3_, ...), custom_call_target="tpu_custom_call" | custom-call | tf_op jit(solution)/shard_map/pallas_call | solution.py:239
  66.1 4.5 %project.1 = (bf16[128,2048]{1,0:T(8,128)(2,1)S(1)}, bf16[128,2048]{1,0:T(8,128)(2,1)S(1)}) custom-call(s32[8]{0:T(128)S(1)} %pad_add_fusion.sc_ref.refs_0_, bf16[16,128,512]{2,1,0:T(8,128)(2,1)S(1)} %shard_map.146.o_ref, bf16[512,4096]{1,0:T(8,128)(2,1)S(1)} %copy-done.3, bf16[2048,2048]{1,0:T(8,128)(2,1)S(1)} %bitcast.29, ...), custom_call_target="tpu_custom_call" | custom-call | tf_op jit(solution)/shard_map/project/pallas_call | solution.py:280
  72.8 2.0 copy-done.2
  74.8 14.2 %all-to-all-start = ((bf16[128,8,2048]{2,1,0:T(8,128)(2,1)}), bf16[128,8,2048]{2,1,0:T(8,128)(2,1)}, u32[]{:S(2)}, u32[]{:S(2)}) async-start(bf16[128,8,2048]{2,1,0:T(8,128)(2,1)} %copy-done.2), calls=%async_computation | async-start | bytes 8388608 | tf_op jit(solution)/shard_map/all_to_all | solution.py:561
  92.5 45.3 %all-to-all-done.x_ref = bf16[128,8,2048]{2,1,0:T(8,128)(2,1)} async-done(((bf16[128,8,2048]{2,1,0:T(8,128)(2,1)}), bf16[128,8,2048]{2,1,0:T(8,128)(2,1)}, u32[]{:S(2)}, u32[]{:S(2)}) %all-to-all-start) | async-done | bytes 4194336 | tf_op jit(solution)/shard_map/all_to_all | solution.py:561
  137.8 8.1 %all-to-all-start.2 = ((bf16[128,8,1280]{2,1,0:T(8,128)(2,1)}), bf16[128,8,1280]{2,1,0:T(8,128)(2,1)}, u32[]{:S(2)}, u32[]{:S(2)}) async-start(bf16[128,8,1280]{2,1,0:T(8,128)(2,1)} %copy-done.6), calls=%async_computation.2 | async-start | bytes 5242880 | tf_op jit(solution)/shard_map/all_to_all | solution.py:561
  146.0 2.6 copy-done
  148.6 12.1 %shard_map.148 = bf16[128,8,2048]{2,1,0:T(8,128)(2,1)S(1)} custom-call(bf16[128,8,2048]{2,1,0:T(8,128)(2,1)} %all-to-all-done.x_ref, bf16[1,2048,1408]{2,1,0:T(8,128)(2,1)S(1)} %copy-done, bf16[1,704,2048]{2,1,0:T(8,128)(2,1)S(1)} %copy-done.5), custom_call_target="tpu_custom_call" | custom-call | tf_op jit(solution)/shard_map/pallas_call | solution.py:450
  160.7 2.0 copy-done.4
  162.7 15.5 %all-to-all-done.2.x_ref = bf16[128,8,1280]{2,1,0:T(8,128)(2,1)} async-done(((bf16[128,8,1280]{2,1,0:T(8,128)(2,1)}), bf16[128,8,1280]{2,1,0:T(8,128)(2,1)}, u32[]{:S(2)}, u32[]{:S(2)}) %all-to-all-start.2) | async-done | bytes 2621472 | tf_op jit(solution)/shard_map/all_to_all | solution.py:561
  178.1 8.5 %all-to-all-start.1 = ((bf16[128,8,2048]{2,1,0:T(8,128)(2,1)}), bf16[128,8,2048]{2,1,0:T(8,128)(2,1)}, u32[]{:S(2)}, u32[]{:S(2)}) async-start(bf16[128,8,2048]{2,1,0:T(8,128)(2,1)} %copy-done.4), calls=%async_computation.1 | async-start | bytes 8388608 | tf_op jit(solution)/shard_map/all_to_all | solution.py:561
  186.7 2.6 copy-done.1
  189.3 12.0 %shard_map.150 = bf16[128,8,1280]{2,1,0:T(8,128)(2,1)S(1)} custom-call(bf16[128,8,1280]{2,1,0:T(8,128)(2,1)} %all-to-all-done.2.x_ref, bf16[1,2048,1408]{2,1,0:T(8,128)(2,1)S(1)} %copy-done.1, bf16[1,704,2048]{2,1,0:T(8,128)(2,1)S(1)} %copy-done.5), custom_call_target="tpu_custom_call" | custom-call | tf_op jit(solution)/shard_map/pallas_call | solution.py:450
  202.8 32.7 %all-to-all-done.1.back_ref = bf16[128,8,2048]{2,1,0:T(8,128)(2,1)} async-done(((bf16[128,8,2048]{2,1,0:T(8,128)(2,1)}), bf16[128,8,2048]{2,1,0:T(8,128)(2,1)}, u32[]{:S(2)}, u32[]{:S(2)}) %all-to-all-start.1) | async-done | bytes 4194336 | tf_op jit(solution)/shard_map/all_to_all | solution.py:561
  235.5 7.7 %all-to-all-start.3 = ((bf16[128,8,1280]{2,1,0:T(8,128)(2,1)}), bf16[128,8,1280]{2,1,0:T(8,128)(2,1)S(1)}, u32[]{:S(2)}, u32[]{:S(2)}) async-start(bf16[128,8,1280]{2,1,0:T(8,128)(2,1)} %copy-done.7), calls=%async_computation.3 | async-start | bytes 5242880 | tf_op jit(solution)/shard_map/all_to_all | solution.py:561
  243.2 4.1 %combine_a.1.sum_ref = f32[128,2048]{1,0:T(8,128)S(1)} custom-call(s32[6,128]{1,0:T(8,128)S(1)} %bitcast.32, f32[6,128]{1,0:T(8,128)S(1)} %bitcast.34, bf16[128,2048]{1,0:T(8,128)(2,1)S(1)} %copy-done.13, bf16[128,8,2048]{2,1,0:T(8,128)(2,1)} %all-to-all-done.1.back_ref), custom_call_target="tpu_custom_call" | custom-call | tf_op jit(solution)/shard_map/combine_a/pallas_call | solution.py:490
  248.3 27.3 %all-to-all-done.3.back_ref = bf16[128,8,1280]{2,1,0:T(8,128)(2,1)S(1)} async-done(((bf16[128,8,1280]{2,1,0:T(8,128)(2,1)}), bf16[128,8,1280]{2,1,0:T(8,128)(2,1)S(1)}, u32[]{:S(2)}, u32[]{:S(2)}) %all-to-all-start.3) | async-done | bytes 2621472 | tf_op jit(solution)/shard_map/all_to_all | solution.py:561
  276.9 3.3 %combine_b.1 = bf16[128,2048]{1,0:T(8,128)(2,1)} custom-call(s32[6,128]{1,0:T(8,128)S(1)} %bitcast.33, f32[6,128]{1,0:T(8,128)S(1)} %bitcast.35, f32[128,2048]{1,0:T(8,128)S(1)} %copy-done.9, bf16[128,8,1280]{2,1,0:T(8,128)(2,1)S(1)} %all-to-all-done.3.back_ref), custom_call_target="tpu_custom_call" | custom-call | tf_op jit(solution)/shard_map/combine_b/pallas_call | solution.py:520
  (92 shorter events, 26.4 us)
Async XLA Ops:
  0.0 33.0 %copy-start.19 = (s32[1,4]{1,0:T(1,128)S(1)}, s32[1,4]{1,0:T(1,128)}, u32[]{:S(2)}) copy-start(s32[1,4]{1,0:T(1,128)} %param.22) | copy-start | bytes 52
  0.0 33.1 %copy-start.10 = (bf16[128,3072]{1,0:T(8,128)(2,1)S(1)}, bf16[128,3072]{1,0:T(8,128)(2,1)}, u32[]{:S(2)}) copy-start(bf16[128,3072]{1,0:T(8,128)(2,1)} %qr_ref.1) | copy-start | bytes 2359300
  0.0 33.1 %copy-start.3 = (bf16[512,4096]{1,0:T(8,128)(2,1)S(1)}, bf16[512,4096]{1,0:T(8,128)(2,1)}, u32[]{:S(2)}) copy-start(bf16[512,4096]{1,0:T(8,128)(2,1)} %w_ref.3) | copy-start | bytes 12582916
  2.5 15.5 %collective-permute-start = (bf16[144,512]{1,0:T(8,128)(2,1)S(1)}, bf16[144,512]{1,0:T(8,128)(2,1)S(1)}, u32[]{:S(2)}, u32[]{:S(2)}) collective-permute-start(bf16[144,512]{1,0:T(8,128)(2,1)S(1)} %pad_maximum_fusion), channel_id=1, source_target_pairs={{0,4},{1,5},{2,6},{3,7},{4,8},{5,9},{6,10},{7,11},{8,12},{9,13},{1... | collective-permute-start | bytes 442376 | tf_op jit(solution)/shard_map/ppermute | solution.py:541
  3.5 14.6 %collective-permute-start.1 = (bf16[144,512]{1,0:T(8,128)(2,1)S(1)}, bf16[144,512]{1,0:T(8,128)(2,1)S(1)}, u32[]{:S(2)}, u32[]{:S(2)}) collective-permute-start(bf16[144,512]{1,0:T(8,128)(2,1)S(1)} %pad_maximum_fusion), channel_id=1, source_target_pairs={{0,12},{1,13},{2,14},{3,15},{4,0},{5,1},{6,2},{7,3},{8,4},{9,5},{1... | collective-permute-start | bytes 442376 | tf_op jit(solution)/shard_map/ppermute | solution.py:541
  4.0 14.1 %collective-permute-start.2 = (bf16[144,512]{1,0:T(8,128)(2,1)S(1)}, bf16[144,512]{1,0:T(8,128)(2,1)S(1)}, u32[]{:S(2)}, u32[]{:S(2)}) collective-permute-start(bf16[144,512]{1,0:T(8,128)(2,1)S(1)} %pad_maximum_fusion), channel_id=1, source_target_pairs={{0,8},{1,9},{2,10},{3,11},{4,12},{5,13},{6,14},{7,15},{8,0},{9,1},... | collective-permute-start | bytes 442376 | tf_op jit(solution)/shard_map/ppermute | solution.py:541
  5.5 5.5 %collective-permute-start.3 = (bf16[144,512]{1,0:T(8,128)(2,1)S(1)}, bf16[144,512]{1,0:T(8,128)(2,1)S(1)}, u32[]{:S(2)}, u32[]{:S(2)}) collective-permute-start(bf16[144,512]{1,0:T(8,128)(2,1)S(1)} %pad_maximum_fusion.1), channel_id=1, source_target_pairs={{0,1},{1,2},{2,3},{3,0},{4,5},{5,6},{6,7},{7,4},{8,9},{9,10},{10,1... | collective-permute-start | bytes 442376 | tf_op jit(solution)/shard_map/ppermute | solution.py:541
  6.9 5.9 %collective-permute-start.4 = (bf16[144,512]{1,0:T(8,128)(2,1)S(1)}, bf16[144,512]{1,0:T(8,128)(2,1)S(1)}, u32[]{:S(2)}, u32[]{:S(2)}) collective-permute-start(bf16[144,512]{1,0:T(8,128)(2,1)S(1)} %pad_maximum_fusion.1), channel_id=1, source_target_pairs={{0,3},{1,0},{2,1},{3,2},{4,7},{5,4},{6,5},{7,6},{8,11},{9,8},{10,9... | collective-permute-start | bytes 442376 | tf_op jit(solution)/shard_map/ppermute | solution.py:541
  11.0 5.5 %collective-permute-start.5 = (bf16[144,512]{1,0:T(8,128)(2,1)S(1)}, bf16[144,512]{1,0:T(8,128)(2,1)S(1)}, u32[]{:S(2)}, u32[]{:S(2)}) collective-permute-start(bf16[144,512]{1,0:T(8,128)(2,1)S(1)} %pad_maximum_fusion.1), channel_id=1, source_target_pairs={{0,2},{1,3},{2,0},{3,1},{4,6},{5,7},{6,4},{7,5},{8,10},{9,11},{10,... | collective-permute-start | bytes 442376 | tf_op jit(solution)/shard_map/ppermute | solution.py:541
  16.5 11.3 %collective-permute-start.10 = (bf16[576,512]{1,0:T(8,128)(2,1)S(1)}, bf16[576,512]{1,0:T(8,128)(2,1)S(1)}, u32[]{:S(2)}, u32[]{:S(2)}) collective-permute-start(bf16[576,512]{1,0:T(8,128)(2,1)S(1)} %constant_dynamic-update-slice_fusion.5.refs_6_), channel_id=1, source_target_pairs={{0,4},{1,5},{2,6},{3,7},{4,8},{5,9},{6,10},{7,11},{8,12},{9,13},{1... | collective-permute-start | bytes 1769480 | tf_op jit(solution)/shard_map/ppermute | solution.py:541
  17.3 11.8 %collective-permute-start.11 = (bf16[576,512]{1,0:T(8,128)(2,1)S(1)}, bf16[576,512]{1,0:T(8,128)(2,1)S(1)}, u32[]{:S(2)}, u32[]{:S(2)}) collective-permute-start(bf16[576,512]{1,0:T(8,128)(2,1)S(1)} %constant_dynamic-update-slice_fusion.5.refs_6_), channel_id=1, source_target_pairs={{0,12},{1,13},{2,14},{3,15},{4,0},{5,1},{6,2},{7,3},{8,4},{9,5},{1... | collective-permute-start | bytes 1769480 | tf_op jit(solution)/shard_map/ppermute | solution.py:541
  18.1 12.0 %collective-permute-start.6 = (bf16[576,512]{1,0:T(8,128)(2,1)S(1)}, bf16[576,512]{1,0:T(8,128)(2,1)S(1)}, u32[]{:S(2)}, u32[]{:S(2)}) collective-permute-start(bf16[576,512]{1,0:T(8,128)(2,1)S(1)} %constant_dynamic-update-slice_fusion.refs_5_), channel_id=1, source_target_pairs={{0,1},{1,2},{2,3},{3,0},{4,5},{5,6},{6,7},{7,4},{8,9},{9,10},{10,1... | collective-permute-start | bytes 1769480 | tf_op jit(solution)/shard_map/ppermute | solution.py:541
  18.4 11.8 %collective-permute-start.7 = (bf16[576,512]{1,0:T(8,128)(2,1)S(1)}, bf16[576,512]{1,0:T(8,128)(2,1)S(1)}, u32[]{:S(2)}, u32[]{:S(2)}) collective-permute-start(bf16[576,512]{1,0:T(8,128)(2,1)S(1)} %constant_dynamic-update-slice_fusion.refs_5_), channel_id=1, source_target_pairs={{0,3},{1,0},{2,1},{3,2},{4,7},{5,4},{6,5},{7,6},{8,11},{9,8},{10,9... | collective-permute-start | bytes 1769480 | tf_op jit(solution)/shard_map/ppermute | solution.py:541
  27.8 20.6 %collective-permute-start.12 = (bf16[288,512]{1,0:T(8,128)(2,1)S(1)}, bf16[288,512]{1,0:T(8,128)(2,1)S(1)}, u32[]{:S(2)}, u32[]{:S(2)}) collective-permute-start(bf16[288,512]{1,0:T(8,128)(2,1)S(1)} %slice.34), channel_id=1, source_target_pairs={{0,4},{1,5},{2,6},{3,7},{4,8},{5,9},{6,10},{7,11},{8,12},{9,13},{1... | collective-permute-start | bytes 884744 | tf_op jit(solution)/shard_map/ppermute | solution.py:541
  29.1 19.4 %collective-permute-start.13 = (bf16[288,512]{1,0:T(8,128)(2,1)S(1)}, bf16[288,512]{1,0:T(8,128)(2,1)S(1)}, u32[]{:S(2)}, u32[]{:S(2)}) collective-permute-start(bf16[288,512]{1,0:T(8,128)(2,1)S(1)} %slice.35), channel_id=1, source_target_pairs={{0,12},{1,13},{2,14},{3,15},{4,0},{5,1},{6,2},{7,3},{8,4},{9,5},{1... | collective-permute-start | bytes 884744 | tf_op jit(solution)/shard_map/ppermute | solution.py:541
  30.1 18.4 %collective-permute-start.8 = (bf16[288,512]{1,0:T(8,128)(2,1)S(1)}, bf16[288,512]{1,0:T(8,128)(2,1)S(1)}, u32[]{:S(2)}, u32[]{:S(2)}) collective-permute-start(bf16[288,512]{1,0:T(8,128)(2,1)S(1)} %slice.32), channel_id=1, source_target_pairs={{0,1},{1,2},{2,3},{3,0},{4,5},{5,6},{6,7},{7,4},{8,9},{9,10},{10,1... | collective-permute-start | bytes 884744 | tf_op jit(solution)/shard_map/ppermute | solution.py:541
  30.3 18.2 %collective-permute-start.9 = (bf16[288,512]{1,0:T(8,128)(2,1)S(1)}, bf16[288,512]{1,0:T(8,128)(2,1)S(1)}, u32[]{:S(2)}, u32[]{:S(2)}) collective-permute-start(bf16[288,512]{1,0:T(8,128)(2,1)S(1)} %slice.33), channel_id=1, source_target_pairs={{0,3},{1,0},{2,1},{3,2},{4,7},{5,4},{6,5},{7,6},{8,11},{9,8},{10,9... | collective-permute-start | bytes 884744 | tf_op jit(solution)/shard_map/ppermute | solution.py:541
  74.8 63.0 %all-to-all-start = ((bf16[128,8,2048]{2,1,0:T(8,128)(2,1)}), bf16[128,8,2048]{2,1,0:T(8,128)(2,1)}, u32[]{:S(2)}, u32[]{:S(2)}) async-start(bf16[128,8,2048]{2,1,0:T(8,128)(2,1)} %copy-done.2), calls=%async_computation | async-start | bytes 8388608 | tf_op jit(solution)/shard_map/all_to_all | solution.py:561
  89.0 56.9 %copy-start.5 = (bf16[1,704,2048]{2,1,0:T(8,128)(2,1)S(1)}, bf16[1,704,2048]{2,1,0:T(8,128)(2,1)}, u32[]{:S(2)}) copy-start(bf16[1,704,2048]{2,1,0:T(8,128)(2,1)} %wd_ref.3) | copy-start | bytes 8650756
  137.8 40.3 %all-to-all-start.2 = ((bf16[128,8,1280]{2,1,0:T(8,128)(2,1)}), bf16[128,8,1280]{2,1,0:T(8,128)(2,1)}, u32[]{:S(2)}, u32[]{:S(2)}) async-start(bf16[128,8,1280]{2,1,0:T(8,128)(2,1)} %copy-done.6), calls=%async_computation.2 | async-start | bytes 5242880 | tf_op jit(solution)/shard_map/all_to_all | solution.py:561
  178.1 57.3 %all-to-all-start.1 = ((bf16[128,8,2048]{2,1,0:T(8,128)(2,1)}), bf16[128,8,2048]{2,1,0:T(8,128)(2,1)}, u32[]{:S(2)}, u32[]{:S(2)}) async-start(bf16[128,8,2048]{2,1,0:T(8,128)(2,1)} %copy-done.4), calls=%async_computation.1 | async-start | bytes 8388608 | tf_op jit(solution)/shard_map/all_to_all | solution.py:561
  202.8 40.4 %copy-start.13 = (bf16[128,2048]{1,0:T(8,128)(2,1)S(1)}, bf16[128,2048]{1,0:T(8,128)(2,1)}, u32[]{:S(2)}) copy-start(bf16[128,2048]{1,0:T(8,128)(2,1)} %copy-done.12) | copy-start | bytes 1572868
  202.8 40.4 %copy-start.17 = (f32[128,6]{0,1:T(8,128)S(1)}, f32[128,6]{0,1:T(8,128)}, u32[]{:S(2)}) copy-start(f32[128,6]{0,1:T(8,128)} %param.27) | copy-start | bytes 9220
  235.5 40.2 %all-to-all-start.3 = ((bf16[128,8,1280]{2,1,0:T(8,128)(2,1)}), bf16[128,8,1280]{2,1,0:T(8,128)(2,1)S(1)}, u32[]{:S(2)}, u32[]{:S(2)}) async-start(bf16[128,8,1280]{2,1,0:T(8,128)(2,1)} %copy-done.7), calls=%async_computation.3 | async-start | bytes 5242880 | tf_op jit(solution)/shard_map/all_to_all | solution.py:561
  (17 other events, 187.5 us)

commit v2 on v1

--- a/solution.py
+++ b/solution.py
@@ -128,131 +128,87 @@
     return views
 
 
-def attention_kernel(n_pieces, stage, sc_ref, qa_ref, qr_ref, *rest):
-    rest = list(rest)
-    local = [rest.pop(0), rest.pop(0)]
+def unpack_rope(ref, at):
+    return jnp.concatenate(
+        [ref[at + 128 : at + 144, j * 128 : (j + 1) * 128] for j in range(4)], axis=0
+    )
+
+
+def attention_kernel(n_pieces, sc_ref, qa_ref, qr_ref, ll_ref, lr_ref, *rest):
     pieces = (rest[:n_pieces], rest[n_pieces : 2 * n_pieces])
-    rest = rest[2 * n_pieces :]
-    if stage == LAST:
-        o_ref, s_scr, m_scr, l_scr, acc_scr = rest
-    else:
-        ml_ref, acc_out, s_scr, m_scr, l_scr, acc_scr = rest
+    o_ref, s_scr, n_scr = rest[2 * n_pieces :]
     lens, starts, bases, zero_count = request_scalars(sc_ref)
     first = pl.program_id(0) * TILE
     c = SCALE * LOG2E
-    q = qa_ref[...].reshape(ROWS, LAT)
-    qr = qr_ref[...].reshape(ROWS, ROPE)
-
-    if stage == FIRST:
-        ll_ref, lr_ref = local
-        places = first + lax.broadcasted_iota(jnp.int32, (TILE, TOK), 0)
-        keys_at = lax.broadcasted_iota(jnp.int32, (TILE, TOK), 1)
-        bias = jnp.full((TILE, TOK), NEG, f32)
-        for r in range(REQS):
-            mine = (places >= bases[r]) & (places < bases[r] + lens[r])
-            tok = places - bases[r] + starts[r]
-            ok = mine & (keys_at >= starts[r]) & (keys_at <= tok)
-            bias = jnp.where(ok, 0.0, bias)
-        local_lat = ll_ref[...]
-        s = mm_nt(q, local_lat) + mm(qr, lr_ref[...])
-        s = (s.reshape(HEADS, TILE, TOK) + bias[None]).reshape(ROWS, TOK)
-        m = jnp.max(s, axis=1, keepdims=True)
-        p = jnp.exp2((s - m) * c)
-        m_scr[...] = jnp.broadcast_to(m, (ROWS, 128))
-        l_scr[...] = jnp.broadcast_to(jnp.sum(p, axis=1, keepdims=True), (ROWS, 128))
-        acc_scr[...] = mm(p.astype(bf16), local_lat)
-    else:
-        ml_in, acc_in = local
-        ml = ml_in[...].reshape(ROWS, 128)
-        m_scr[...] = jnp.broadcast_to(ml[:, :1], (ROWS, 128))
-        l_scr[...] = jnp.broadcast_to(ml[:, 1:2], (ROWS, 128))
-        acc_scr[...] = acc_in[...].reshape(ROWS, LAT)
 
     for pre in range(PREF):
         needed = (first < zero_count) if pre == 0 else (first + TILE > zero_count)
 
         @pl.when(needed)
         def _(pre=pre):
+            q = qa_ref[...].reshape(ROWS, LAT)
+            qr = qr_ref[...].reshape(ROWS, ROPE)
+            places = first + lax.broadcasted_iota(jnp.int32, (TILE, TOK), 0)
+            keys_at = lax.broadcasted_iota(jnp.int32, (TILE, TOK), 1)
+            bias = jnp.full((TILE, TOK), NEG, f32)
+            for r in range(REQS):
+                mine = (places >= bases[r]) & (places < bases[r] + lens[r])
+                tok = places - bases[r] + starts[r]
+                ok = mine & (keys_at >= starts[r]) & (keys_at <= tok)
+                bias = jnp.where(ok, 0.0, bias)
+            local_lat = ll_ref[...]
+            s = mm_nt(q, local_lat) + mm(qr, lr_ref[...])
+            s = (s.reshape(HEADS, TILE, TOK) + bias[None]).reshape(ROWS, TOK)
+            n_scr[...] = s
+            m = jnp.max(s, axis=1, keepdims=True)
             views = block_views(pieces[pre])
-            place = first + lax.broadcasted_iota(jnp.int32, (ROWS, 1), 0) % TILE
-            mine = (place < zero_count) if pre == 0 else (place >= zero_count)
-            row_bias = jnp.where(mine, 0.0, NEG)
             chunks = [views[k : k + 4] for k in range(0, len(views), 4)]
-            m_old = m_scr[:, :1]
-            m_new = m_old
             for k, chunk in enumerate(chunks):
                 lat = jnp.concatenate([ref[at : at + 128, :] for ref, at in chunk], axis=0)
-                rope = jnp.concatenate(
-                    [
-                        jnp.concatenate(
-                            [ref[at + 128 : at + 144, j * 128 : (j + 1) * 128] for j in range(4)],
-                            axis=0,
-                        )
-                        for ref, at in chunk
-                    ],
-                    axis=1,
-                )
-                s = mm_nt(q, lat) + mm(qr, rope) + row_bias
+                rope = jnp.concatenate([unpack_rope(ref, at) for ref, at in chunk], axis=1)
+                s = mm_nt(q, lat) + mm(qr, rope)
                 s_scr[k] = s
-                m_new = jnp.maximum(m_new, jnp.max(s, axis=1, keepdims=True))
-            scale_old = jnp.exp2((m_old - m_new) * c)
-            total = l_scr[:, :1] * scale_old
-            acc = acc_scr[...] * scale_old
+                m = jnp.maximum(m, jnp.max(s, axis=1, keepdims=True))
+            p = jnp.exp2((n_scr[...] - m) * c)
+            total = jnp.sum(p, axis=1, keepdims=True)
+            acc = mm(p.astype(bf16), local_lat)
             for k, chunk in enumerate(chunks):
                 lat = jnp.concatenate([ref[at : at + 128, :] for ref, at in chunk], axis=0)
-                p = jnp.exp2((s_scr[k] - m_new) * c)
+                p = jnp.exp2((s_scr[k] - m) * c)
                 total = total + jnp.sum(p, axis=1, keepdims=True)
                 acc = acc + mm(p.astype(bf16), lat)
-            m_scr[...] = jnp.broadcast_to(m_new, (ROWS, 128))
-            l_scr[...] = jnp.broadcast_to(total, (ROWS, 128))
-            acc_scr[...] = acc
-
-    if stage == LAST:
-        out = acc_scr[...] / l_scr[:, :1]
-        o_ref[...] = out.astype(bf16).reshape(HEADS, TILE, LAT)
-    else:
-        lane = lax.broadcasted_iota(jnp.int32, (ROWS, 128), 1)
-        ml = jnp.where(lane == 0, m_scr[...], l_scr[...])
-        ml_ref[...] = ml.reshape(HEADS, TILE, 128)
-        acc_out[...] = acc_scr[...].reshape(HEADS, TILE, LAT)
-
-
-FIRST, LAST = 0, 2
-
-
-def attend(stage, scalars, qa, qr, local, pieces0, pieces1):
+            out = (acc / total).astype(bf16).reshape(HEADS, TILE, LAT)
+            if pre == 0:
+                o_ref[...] = out
+            else:
+                place = first + lax.broadcasted_iota(jnp.int32, (HEADS, TILE, LAT), 1)
+                o_ref[...] = jnp.where(place >= zero_count, out, o_ref[...])
+
+
+def attend(scalars, qa, qr, local_lat, local_rope, pieces0, pieces1):
     n_pieces = len(pieces0)
     whole = lambda a: pl.BlockSpec(a.shape, lambda i, s: (0,) * a.ndim)
     tiled = lambda width: pl.BlockSpec((HEADS, TILE, width), lambda i, s: (0, i, 0))
     pieces = [*pieces0, *pieces1]
-    local_specs = [whole(a) for a in local] if stage == FIRST else [tiled(128), tiled(LAT)]
-    if stage == LAST:
-        out_shape = jax.ShapeDtypeStruct((HEADS, TOK, LAT), bf16)
-        out_specs = tiled(LAT)
-    else:
-        out_shape = (
-            jax.ShapeDtypeStruct((HEADS, TOK, 128), f32),
-            jax.ShapeDtypeStruct((HEADS, TOK, LAT), f32),
-        )
-        out_specs = [tiled(128), tiled(LAT)]
-    keys = sum(a.shape[0] // BLK for a in pieces0)
-    return pl.pallas_call(
-        lambda *refs: attention_kernel(n_pieces, stage, *refs),
-        out_shape=out_shape,
+    return pl.pallas_call(
+        lambda *refs: attention_kernel(n_pieces, *refs),
+        out_shape=jax.ShapeDtypeStruct((HEADS, TOK, LAT), bf16),
         grid_spec=pltpu.PrefetchScalarGridSpec(
             num_scalar_prefetch=1,
             grid=(TOK // TILE,),
-            in_specs=[tiled(LAT), tiled(ROPE), *local_specs, *[pl.BlockSpec(memory_space=pltpu.VMEM) for _ in pieces]],
-            out_specs=out_specs,
-            scratch_shapes=[
-                pltpu.VMEM((max(keys // 4, 1), ROWS, 512), f32),
-                pltpu.VMEM((ROWS, 128), f32),
-                pltpu.VMEM((ROWS, 128), f32),
-                pltpu.VMEM((ROWS, LAT), f32),
+            in_specs=[
+                tiled(LAT),
+                tiled(ROPE),
+                whole(local_lat),
+                whole(local_rope),
+                *[pl.BlockSpec(memory_space=pltpu.VMEM) for _ in pieces],
             ],
+            out_specs=tiled(LAT),
+            scratch_shapes=[pltpu.VMEM((4, ROWS, 512), f32), pltpu.VMEM((ROWS, TOK), f32)],
         ),
+        name="attention",
         compiler_params=grant(24),
-    )(scalars, qa, qr, *local, *pieces)
+    )(scalars, qa, qr, local_lat, local_rope, *pieces)
 
 
 def project_kernel(sc_ref, o_ref, w_ref, wo_ref, res_ref, gain_ref, hid_ref, norm_ref, acc_ref):
@@ -542,7 +498,9 @@
 
 
 def gather_row(own, first):
-    return jnp.concatenate([own, hop(own, first, 1), hop(own, first, -1), hop(own, first, 2)], axis=0)
+    far = hop(own, first, 2)
+    near = [hop(own, first, 1), hop(own, first, -1)]
+    return jnp.concatenate([own, *near, far], axis=0)
 
 
 def gather_rest(row, second):
@@ -584,8 +542,7 @@
     rest0 = gather_rest(row0, "y")
     rest1 = gather_rest(row1, "x")
     qa, qr = prepare_queries(scalars, queries, w_ukv)
-    state = attend(FIRST, scalars, qa, qr, (suffix_latent, suffix_rope), [row0], [row1])
-    o_lat = attend(LAST, scalars, qa, qr, state, rest0, rest1)
+    o_lat = attend(scalars, qa, qr, suffix_latent, suffix_rope, [row0, *rest0], [row1, *rest1])
     hidden, normed = project(scalars, o_lat, w_ukv, w_out, residual, norm_gain.reshape(1, D))
     ids_t = expert_ids.T
     gates_t = gate_values.T

time: 285 us -> 275 us (0.965)
  Pallas kernels: 72.2 us -> 61 us
  waiting for transfers between devices: 134 us -> 138 us
    pallas_call x2 -> x1, Pallas kernels: 30.2 us -> 19 us  [attend(): pl.pallas_call(lambda *refs: attention_kernel(n_pieces, *refs), out_shape...]
    ppermute x14, waiting for transfers between devices: 13.1 us -> 17.1 us  [hop(): return lax.ppermute(a, 'wide', shift(axis, k))]
  transfers between devices with their start and end apart: 18 -> 18, of which waited for: 9 -> 9; matrix products, arithmetic and copies ran while one was open for 0% -> 0% of each run, Pallas kernels for 16% -> 12%
where the time goes in v2:
time: 275 us; the launch traced here: 271 us
  waiting for transfers between devices  138 us (50%)
  Pallas kernels  61 us (22%)
  starting transfers between devices  52.4 us (19%)
  local copies, waits for them, and re-layouts  18.9 us (7%)
    all_to_all x4, waiting for transfers between devices, exchange(): lax.all_to_all(a, ('req', 'wide'), split_axis=0, concat_axis=0, tiled=True)  121 us
    all_to_all x4, starting transfers between devices, exchange(): lax.all_to_all(a, ('req', 'wide'), split_axis=0, concat_axis=0, tiled=True)  36.2 us
    pallas_call x2, Pallas kernels, run_expert(): pl.pallas_call(kernel, out_shape=jax.ShapeDtypeStruct(rows.shape, bf16),...  24.1 us
    pallas_call x1, Pallas kernels, attend(): pl.pallas_call(lambda *refs: attention_kernel(n_pieces, *refs), out_shape...  19 us
    ppermute x14, waiting for transfers between devices, hop(): return lax.ppermute(a, 'wide', shift(axis, k))  17.1 us
    unnamed x55, local copies, waits for them, and re-layouts  16.4 us
    ppermute x14, starting transfers between devices, hop(): return lax.ppermute(a, 'wide', shift(axis, k))  16.2 us
  transfers between devices with their start and end apart: 18, of which 9 were waited for; matrix products, arithmetic and copies ran while one was open for 0% of the time, Pallas kernels for 12%

profile of v2, /device:TPU:37, one launch (start us, length us, event | category | flops | bytes accessed | tf_op | source)
XLA Modules:
  0.0 270.8 jit_solution(8658572333132667001)
XLA Ops:
  11.6 2.3 collective-permute-start.4
  13.9 1.7 collective-permute-done.9
  17.2 11.7 %collective-permute-done.3.refs_6_ = bf16[576,512]{1,0:T(8,128)(2,1)S(1)} collective-permute-done((bf16[576,512]{1,0:T(8,128)(2,1)S(1)}, bf16[576,512]{1,0:T(8,128)(2,1)S(1)}, u32[]{:S(2)}, u32[]{:S(2)}) %collective-permute-start.3) | collective-permute-done | bytes 589856 | tf_op jit(solution)/shard_map/ppermute | solution.py:497
  29.1 2.7 %collective-permute-start.6 = (bf16[288,512]{1,0:T(8,128)(2,1)S(1)}, bf16[288,512]{1,0:T(8,128)(2,1)S(1)}, u32[]{:S(2)}, u32[]{:S(2)}) collective-permute-start(bf16[288,512]{1,0:T(8,128)(2,1)S(1)} %slice.33), channel_id=1, source_target_pairs={{0,3},{1,0},{2,1},{3,2},{4,7},{5,4},{6,5},{7,6},{8,11},{9,8},{10,9... | collective-permute-start | bytes 884744 | tf_op jit(solution)/shard_map/ppermute | solution.py:497
  33.6 2.7 query_prep.1
  39.9 19.0 %attention.1.o_ref = bf16[16,128,512]{2,1,0:T(8,128)(2,1)S(1)} custom-call(s32[8]{0:T(128)S(1)} %pad_add_fusion.sc_ref.refs_0_, bf16[16,128,512]{2,1,0:T(8,128)(2,1)S(1)} %get-tuple-element.9.refs_1_, bf16[16,128,64]{2,1,0:T(8,128)(2,1)S(1)} %get-tuple-element.10.refs_2_, bf16[128,512]{1,0:T(8,128)(2,1)S(1)} %copy-done.14, bf16[64,128]{1,0:T(8,128)(2,1)S(1)} %copy-done.16, ...), custom_call_target="tpu_custom_call" | custom-call | tf_op jit(solution)/shard_map/attention/pallas_call | solution.py:193
  58.9 4.5 %project.1 = (bf16[128,2048]{1,0:T(8,128)(2,1)S(1)}, bf16[128,2048]{1,0:T(8,128)(2,1)S(1)}) custom-call(s32[8]{0:T(128)S(1)} %pad_add_fusion.sc_ref.refs_0_, bf16[16,128,512]{2,1,0:T(8,128)(2,1)S(1)} %attention.1.o_ref, bf16[512,4096]{1,0:T(8,128)(2,1)S(1)} %copy-done.3, bf16[2048,2048]{1,0:T(8,128)(2,1)S(1)} %bitcast.29, bf16[128,2048]{1,0:T(8,128)(2,1)S(1)} %copy-done.11, ...), custom_call_target="tpu_custom_call" | custom-call | tf_op jit(solution)/shard_map/project/pallas_call | solution.py:236
  65.6 2.0 copy-done.2
  67.6 11.8 %all-to-all-start = ((bf16[128,8,2048]{2,1,0:T(8,128)(2,1)}), bf16[128,8,2048]{2,1,0:T(8,128)(2,1)}, u32[]{:S(2)}, u32[]{:S(2)}) async-start(bf16[128,8,2048]{2,1,0:T(8,128)(2,1)} %copy-done.2), calls=%async_computation | async-start | bytes 8388608 | tf_op jit(solution)/shard_map/all_to_all | solution.py:519
  79.5 1.9 shard_map.147
  83.0 45.3 %all-to-all-done.x_ref = bf16[128,8,2048]{2,1,0:T(8,128)(2,1)} async-done(((bf16[128,8,2048]{2,1,0:T(8,128)(2,1)}), bf16[128,8,2048]{2,1,0:T(8,128)(2,1)}, u32[]{:S(2)}, u32[]{:S(2)}) %all-to-all-start) | async-done | bytes 4194336 | tf_op jit(solution)/shard_map/all_to_all | solution.py:519
  128.3 8.2 %all-to-all-start.2 = ((bf16[128,8,1280]{2,1,0:T(8,128)(2,1)}), bf16[128,8,1280]{2,1,0:T(8,128)(2,1)}, u32[]{:S(2)}, u32[]{:S(2)}) async-start(bf16[128,8,1280]{2,1,0:T(8,128)(2,1)} %copy-done.6), calls=%async_computation.2 | async-start | bytes 5242880 | tf_op jit(solution)/shard_map/all_to_all | solution.py:519
  136.5 2.6 copy-done
  139.1 12.1 %shard_map.146 = bf16[128,8,2048]{2,1,0:T(8,128)(2,1)S(1)} custom-call(bf16[128,8,2048]{2,1,0:T(8,128)(2,1)} %all-to-all-done.x_ref, bf16[1,2048,1408]{2,1,0:T(8,128)(2,1)S(1)} %copy-done, bf16[1,704,2048]{2,1,0:T(8,128)(2,1)S(1)} %copy-done.5), custom_call_target="tpu_custom_call" | custom-call | tf_op jit(solution)/shard_map/pallas_call | solution.py:406
  151.2 2.0 copy-done.4
  153.2 15.5 %all-to-all-done.2.x_ref = bf16[128,8,1280]{2,1,0:T(8,128)(2,1)} async-done(((bf16[128,8,1280]{2,1,0:T(8,128)(2,1)}), bf16[128,8,1280]{2,1,0:T(8,128)(2,1)}, u32[]{:S(2)}, u32[]{:S(2)}) %all-to-all-start.2) | async-done | bytes 2621472 | tf_op jit(solution)/shard_map/all_to_all | solution.py:519
  168.7 8.5 %all-to-all-start.1 = ((bf16[128,8,2048]{2,1,0:T(8,128)(2,1)}), bf16[128,8,2048]{2,1,0:T(8,128)(2,1)}, u32[]{:S(2)}, u32[]{:S(2)}) async-start(bf16[128,8,2048]{2,1,0:T(8,128)(2,1)} %copy-done.4), calls=%async_computation.1 | async-start | bytes 8388608 | tf_op jit(solution)/shard_map/all_to_all | solution.py:519
  177.2 2.6 copy-done.1
  179.8 12.0 %shard_map.148 = bf16[128,8,1280]{2,1,0:T(8,128)(2,1)S(1)} custom-call(bf16[128,8,1280]{2,1,0:T(8,128)(2,1)} %all-to-all-done.2.x_ref, bf16[1,2048,1408]{2,1,0:T(8,128)(2,1)S(1)} %copy-done.1, bf16[1,704,2048]{2,1,0:T(8,128)(2,1)S(1)} %copy-done.5), custom_call_target="tpu_custom_call" | custom-call | tf_op jit(solution)/shard_map/pallas_call | solution.py:406
  193.3 32.7 %all-to-all-done.1.back_ref = bf16[128,8,2048]{2,1,0:T(8,128)(2,1)} async-done(((bf16[128,8,2048]{2,1,0:T(8,128)(2,1)}), bf16[128,8,2048]{2,1,0:T(8,128)(2,1)}, u32[]{:S(2)}, u32[]{:S(2)}) %all-to-all-start.1) | async-done | bytes 4194336 | tf_op jit(solution)/shard_map/all_to_all | solution.py:519
  226.0 7.7 %all-to-all-start.3 = ((bf16[128,8,1280]{2,1,0:T(8,128)(2,1)}), bf16[128,8,1280]{2,1,0:T(8,128)(2,1)S(1)}, u32[]{:S(2)}, u32[]{:S(2)}) async-start(bf16[128,8,1280]{2,1,0:T(8,128)(2,1)} %copy-done.7), calls=%async_computation.3 | async-start | bytes 5242880 | tf_op jit(solution)/shard_map/all_to_all | solution.py:519
  233.7 4.1 %combine_a.1.sum_ref = f32[128,2048]{1,0:T(8,128)S(1)} custom-call(s32[6,128]{1,0:T(8,128)S(1)} %bitcast.32, f32[6,128]{1,0:T(8,128)S(1)} %bitcast.34, bf16[128,2048]{1,0:T(8,128)(2,1)S(1)} %copy-done.13, bf16[128,8,2048]{2,1,0:T(8,128)(2,1)} %all-to-all-done.1.back_ref), custom_call_target="tpu_custom_call" | custom-call | tf_op jit(solution)/shard_map/combine_a/pallas_call | solution.py:446
  238.8 27.4 %all-to-all-done.3.back_ref = bf16[128,8,1280]{2,1,0:T(8,128)(2,1)S(1)} async-done(((bf16[128,8,1280]{2,1,0:T(8,128)(2,1)}), bf16[128,8,1280]{2,1,0:T(8,128)(2,1)S(1)}, u32[]{:S(2)}, u32[]{:S(2)}) %all-to-all-start.3) | async-done | bytes 2621472 | tf_op jit(solution)/shard_map/all_to_all | solution.py:519
  267.4 3.3 %combine_b.1 = bf16[128,2048]{1,0:T(8,128)(2,1)} custom-call(s32[6,128]{1,0:T(8,128)S(1)} %bitcast.33, f32[6,128]{1,0:T(8,128)S(1)} %bitcast.35, f32[128,2048]{1,0:T(8,128)S(1)} %copy-done.9, bf16[128,8,1280]{2,1,0:T(8,128)(2,1)S(1)} %all-to-all-done.3.back_ref), custom_call_target="tpu_custom_call" | custom-call | tf_op jit(solution)/shard_map/combine_b/pallas_call | solution.py:476
  (91 shorter events, 26.0 us)
Async XLA Ops:
  0.0 33.5 %copy-start.20 = (s32[1,4]{1,0:T(1,128)S(1)}, s32[1,4]{1,0:T(1,128)}, u32[]{:S(2)}) copy-start(s32[1,4]{1,0:T(1,128)} %param.21) | copy-start | bytes 52
  0.0 33.5 %copy-start.10 = (bf16[128,3072]{1,0:T(8,128)(2,1)S(1)}, bf16[128,3072]{1,0:T(8,128)(2,1)}, u32[]{:S(2)}) copy-start(bf16[128,3072]{1,0:T(8,128)(2,1)} %qr_ref.1) | copy-start | bytes 2359300
  0.0 33.5 %copy-start.3 = (bf16[512,4096]{1,0:T(8,128)(2,1)S(1)}, bf16[512,4096]{1,0:T(8,128)(2,1)}, u32[]{:S(2)}) copy-start(bf16[512,4096]{1,0:T(8,128)(2,1)} %w_ref.3) | copy-start | bytes 12582916
  2.5 6.9 %collective-permute-start = (bf16[144,512]{1,0:T(8,128)(2,1)S(1)}, bf16[144,512]{1,0:T(8,128)(2,1)S(1)}, u32[]{:S(2)}, u32[]{:S(2)}) collective-permute-start(bf16[144,512]{1,0:T(8,128)(2,1)S(1)} %pad_maximum_fusion), channel_id=1, source_target_pairs={{0,4},{1,5},{2,6},{3,7},{4,8},{5,9},{6,10},{7,11},{8,12},{9,13},{1... | collective-permute-start | bytes 442376 | tf_op jit(solution)/shard_map/ppermute | solution.py:497
  3.5 7.6 %collective-permute-start.1 = (bf16[144,512]{1,0:T(8,128)(2,1)S(1)}, bf16[144,512]{1,0:T(8,128)(2,1)S(1)}, u32[]{:S(2)}, u32[]{:S(2)}) collective-permute-start(bf16[144,512]{1,0:T(8,128)(2,1)S(1)} %pad_maximum_fusion), channel_id=1, source_target_pairs={{0,12},{1,13},{2,14},{3,15},{4,0},{5,1},{6,2},{7,3},{8,4},{9,5},{1... | collective-permute-start | bytes 442376 | tf_op jit(solution)/shard_map/ppermute | solution.py:497
  4.0 7.1 %collective-permute-start.2 = (bf16[144,512]{1,0:T(8,128)(2,1)S(1)}, bf16[144,512]{1,0:T(8,128)(2,1)S(1)}, u32[]{:S(2)}, u32[]{:S(2)}) collective-permute-start(bf16[144,512]{1,0:T(8,128)(2,1)S(1)} %pad_maximum_fusion), channel_id=1, source_target_pairs={{0,8},{1,9},{2,10},{3,11},{4,12},{5,13},{6,14},{7,15},{8,0},{9,1},... | collective-permute-start | bytes 442376 | tf_op jit(solution)/shard_map/ppermute | solution.py:497
  5.5 8.4 %collective-permute-start.7 = (bf16[144,512]{1,0:T(8,128)(2,1)S(1)}, bf16[144,512]{1,0:T(8,128)(2,1)S(1)}, u32[]{:S(2)}, u32[]{:S(2)}) collective-permute-start(bf16[144,512]{1,0:T(8,128)(2,1)S(1)} %pad_maximum_fusion.1), channel_id=1, source_target_pairs={{0,1},{1,2},{2,3},{3,0},{4,5},{5,6},{6,7},{7,4},{8,9},{9,10},{10,1... | collective-permute-start | bytes 442376 | tf_op jit(solution)/shard_map/ppermute | solution.py:497
  6.9 7.0 %collective-permute-start.8 = (bf16[144,512]{1,0:T(8,128)(2,1)S(1)}, bf16[144,512]{1,0:T(8,128)(2,1)S(1)}, u32[]{:S(2)}, u32[]{:S(2)}) collective-permute-start(bf16[144,512]{1,0:T(8,128)(2,1)S(1)} %pad_maximum_fusion.1), channel_id=1, source_target_pairs={{0,3},{1,0},{2,1},{3,2},{4,7},{5,4},{6,5},{7,6},{8,11},{9,8},{10,9... | collective-permute-start | bytes 442376 | tf_op jit(solution)/shard_map/ppermute | solution.py:497
  9.4 6.2 %collective-permute-start.9 = (bf16[144,512]{1,0:T(8,128)(2,1)S(1)}, bf16[144,512]{1,0:T(8,128)(2,1)S(1)}, u32[]{:S(2)}, u32[]{:S(2)}) collective-permute-start(bf16[144,512]{1,0:T(8,128)(2,1)S(1)} %pad_maximum_fusion.1), channel_id=1, source_target_pairs={{0,2},{1,3},{2,0},{3,1},{4,6},{5,7},{6,4},{7,5},{8,10},{9,11},{10,... | collective-permute-start | bytes 442376 | tf_op jit(solution)/shard_map/ppermute | solution.py:497
  11.1 17.8 %collective-permute-start.3 = (bf16[576,512]{1,0:T(8,128)(2,1)S(1)}, bf16[576,512]{1,0:T(8,128)(2,1)S(1)}, u32[]{:S(2)}, u32[]{:S(2)}) collective-permute-start(bf16[576,512]{1,0:T(8,128)(2,1)S(1)} %constant_dynamic-update-slice_fusion.refs_5_), channel_id=1, source_target_pairs={{0,1},{1,2},{2,3},{3,0},{4,5},{5,6},{6,7},{7,4},{8,9},{9,10},{10,1... | collective-permute-start | bytes 1769480 | tf_op jit(solution)/shard_map/ppermute | solution.py:497
  11.6 17.4 %collective-permute-start.4 = (bf16[576,512]{1,0:T(8,128)(2,1)S(1)}, bf16[576,512]{1,0:T(8,128)(2,1)S(1)}, u32[]{:S(2)}, u32[]{:S(2)}) collective-permute-start(bf16[576,512]{1,0:T(8,128)(2,1)S(1)} %constant_dynamic-update-slice_fusion.refs_5_), channel_id=1, source_target_pairs={{0,3},{1,0},{2,1},{3,2},{4,7},{5,4},{6,5},{7,6},{8,11},{9,8},{10,9... | collective-permute-start | bytes 1769480 | tf_op jit(solution)/shard_map/ppermute | solution.py:497
  15.6 16.1 %collective-permute-start.10 = (bf16[576,512]{1,0:T(8,128)(2,1)S(1)}, bf16[576,512]{1,0:T(8,128)(2,1)S(1)}, u32[]{:S(2)}, u32[]{:S(2)}) collective-permute-start(bf16[576,512]{1,0:T(8,128)(2,1)S(1)} %constant_dynamic-update-slice_fusion.5.refs_10_), channel_id=1, source_target_pairs={{0,4},{1,5},{2,6},{3,7},{4,8},{5,9},{6,10},{7,11},{8,12},{9,13},{1... | collective-permute-start | bytes 1769480 | tf_op jit(solution)/shard_map/ppermute | solution.py:497
  16.2 16.5 %collective-permute-start.11 = (bf16[576,512]{1,0:T(8,128)(2,1)S(1)}, bf16[576,512]{1,0:T(8,128)(2,1)S(1)}, u32[]{:S(2)}, u32[]{:S(2)}) collective-permute-start(bf16[576,512]{1,0:T(8,128)(2,1)S(1)} %constant_dynamic-update-slice_fusion.5.refs_10_), channel_id=1, source_target_pairs={{0,12},{1,13},{2,14},{3,15},{4,0},{5,1},{6,2},{7,3},{8,4},{9,5},{1... | collective-permute-start | bytes 1769480 | tf_op jit(solution)/shard_map/ppermute | solution.py:497
  28.9 8.3 %collective-permute-start.5 = (bf16[288,512]{1,0:T(8,128)(2,1)S(1)}, bf16[288,512]{1,0:T(8,128)(2,1)S(1)}, u32[]{:S(2)}, u32[]{:S(2)}) collective-permute-start(bf16[288,512]{1,0:T(8,128)(2,1)S(1)} %slice.32), channel_id=1, source_target_pairs={{0,1},{1,2},{2,3},{3,0},{4,5},{5,6},{6,7},{7,4},{8,9},{9,10},{10,1... | collective-permute-start | bytes 884744 | tf_op jit(solution)/shard_map/ppermute | solution.py:497
  29.1 8.2 %collective-permute-start.6 = (bf16[288,512]{1,0:T(8,128)(2,1)S(1)}, bf16[288,512]{1,0:T(8,128)(2,1)S(1)}, u32[]{:S(2)}, u32[]{:S(2)}) collective-permute-start(bf16[288,512]{1,0:T(8,128)(2,1)S(1)} %slice.33), channel_id=1, source_target_pairs={{0,3},{1,0},{2,1},{3,2},{4,7},{5,4},{6,5},{7,6},{8,11},{9,8},{10,9... | collective-permute-start | bytes 884744 | tf_op jit(solution)/shard_map/ppermute | solution.py:497
  31.8 6.5 %collective-permute-start.12 = (bf16[288,512]{1,0:T(8,128)(2,1)S(1)}, bf16[288,512]{1,0:T(8,128)(2,1)S(1)}, u32[]{:S(2)}, u32[]{:S(2)}) collective-permute-start(bf16[288,512]{1,0:T(8,128)(2,1)S(1)} %slice.34), channel_id=1, source_target_pairs={{0,4},{1,5},{2,6},{3,7},{4,8},{5,9},{6,10},{7,11},{8,12},{9,13},{1... | collective-permute-start | bytes 884744 | tf_op jit(solution)/shard_map/ppermute | solution.py:497
  32.8 7.1 %collective-permute-start.13 = (bf16[288,512]{1,0:T(8,128)(2,1)S(1)}, bf16[288,512]{1,0:T(8,128)(2,1)S(1)}, u32[]{:S(2)}, u32[]{:S(2)}) collective-permute-start(bf16[288,512]{1,0:T(8,128)(2,1)S(1)} %slice.35), channel_id=1, source_target_pairs={{0,12},{1,13},{2,14},{3,15},{4,0},{5,1},{6,2},{7,3},{8,4},{9,5},{1... | collective-permute-start | bytes 884744 | tf_op jit(solution)/shard_map/ppermute | solution.py:497
  67.6 60.7 %all-to-all-start = ((bf16[128,8,2048]{2,1,0:T(8,128)(2,1)}), bf16[128,8,2048]{2,1,0:T(8,128)(2,1)}, u32[]{:S(2)}, u32[]{:S(2)}) async-start(bf16[128,8,2048]{2,1,0:T(8,128)(2,1)} %copy-done.2), calls=%async_computation | async-start | bytes 8388608 | tf_op jit(solution)/shard_map/all_to_all | solution.py:519
  79.5 57.0 %copy-start.5 = (bf16[1,704,2048]{2,1,0:T(8,128)(2,1)S(1)}, bf16[1,704,2048]{2,1,0:T(8,128)(2,1)}, u32[]{:S(2)}) copy-start(bf16[1,704,2048]{2,1,0:T(8,128)(2,1)} %wd_ref.3) | copy-start | bytes 8650756
  128.3 40.4 %all-to-all-start.2 = ((bf16[128,8,1280]{2,1,0:T(8,128)(2,1)}), bf16[128,8,1280]{2,1,0:T(8,128)(2,1)}, u32[]{:S(2)}, u32[]{:S(2)}) async-start(bf16[128,8,1280]{2,1,0:T(8,128)(2,1)} %copy-done.6), calls=%async_computation.2 | async-start | bytes 5242880 | tf_op jit(solution)/shard_map/all_to_all | solution.py:519
  168.7 57.3 %all-to-all-start.1 = ((bf16[128,8,2048]{2,1,0:T(8,128)(2,1)}), bf16[128,8,2048]{2,1,0:T(8,128)(2,1)}, u32[]{:S(2)}, u32[]{:S(2)}) async-start(bf16[128,8,2048]{2,1,0:T(8,128)(2,1)} %copy-done.4), calls=%async_computation.1 | async-start | bytes 8388608 | tf_op jit(solution)/shard_map/all_to_all | solution.py:519
  193.3 40.4 %copy-start.13 = (bf16[128,2048]{1,0:T(8,128)(2,1)S(1)}, bf16[128,2048]{1,0:T(8,128)(2,1)}, u32[]{:S(2)}) copy-start(bf16[128,2048]{1,0:T(8,128)(2,1)} %copy-done.12) | copy-start | bytes 1572868
  193.3 40.4 %copy-start.17 = (f32[128,6]{0,1:T(8,128)S(1)}, f32[128,6]{0,1:T(8,128)}, u32[]{:S(2)}) copy-start(f32[128,6]{0,1:T(8,128)} %param.27) | copy-start | bytes 9220
  226.0 40.2 %all-to-all-start.3 = ((bf16[128,8,1280]{2,1,0:T(8,128)(2,1)}), bf16[128,8,1280]{2,1,0:T(8,128)(2,1)S(1)}, u32[]{:S(2)}, u32[]{:S(2)}) async-start(bf16[128,8,1280]{2,1,0:T(8,128)(2,1)} %copy-done.7), calls=%async_computation.3 | async-start | bytes 5242880 | tf_op jit(solution)/shard_map/all_to_all | solution.py:519
  (17 other events, 202.9 us)

commit v3 on v2

--- a/solution.py
+++ b/solution.py
@@ -211,12 +211,16 @@
     )(scalars, qa, qr, local_lat, local_rope, *pieces)
 
 
-def project_kernel(sc_ref, o_ref, w_ref, wo_ref, res_ref, gain_ref, hid_ref, norm_ref, acc_ref):
+def project_kernel(
+    sc_ref, o_ref, w_ref, wo_ref, res_ref, gain_ref, ids_ref,
+    hid_ref, norm_ref, sent_ref, acc_ref, rank_scr, sent_scr, sems,
+):
     step = pl.program_id(0)
 
     @pl.when(step == 0)
     def _():
         acc_ref[...] = res_ref[...].astype(f32)
+        rank_scr[...] = rank_table(ids_ref)
 
     back = sort_matrix(sc_ref, True)
     heads = [mm(o_ref[h], w_ref[:, h * 256 + 128 : h * 256 + 256]).astype(bf16) for h in range(HG)]
@@ -230,14 +234,29 @@
         h32 = hidden.astype(f32)
         inverse = lax.rsqrt(jnp.mean(h32 * h32, axis=1, keepdims=True) + EPS)
         norm_ref[...] = (h32 * inverse * gain_ref[...].astype(f32)).astype(bf16)
-
-
-def project(scalars, o_lat, w_ukv, w_out, residual, gain):
+        copies = []
+        for g in range(EXPERTS // EG):
+            part = pl.ds(g * EG, EG)
+            rows = whole_rows(rank_scr[g * EG : (g + 1) * EG, :], EG, 1).astype(bf16)
+            sent = mm(rows, norm_ref[...]).astype(bf16)
+            sent_scr[part] = sent.reshape(EG, SLOTS_A, D)
+            for half in range(2):
+                copy = pltpu.make_async_copy(
+                    sent_scr.at[part], sent_ref.at[part, half], sems.at[g, half]
+                )
+                copy.start()
+                copies.append(copy)
+        for copy in copies:
+            copy.wait()
+
+
+def project(scalars, o_lat, w_ukv, w_out, residual, gain, ids_t):
     return pl.pallas_call(
         project_kernel,
         out_shape=(
+            pltpu.HBM((TOK, D), bf16),
             jax.ShapeDtypeStruct((TOK, D), bf16),
-            jax.ShapeDtypeStruct((TOK, D), bf16),
+            pltpu.HBM((EXPERTS, 2, SLOTS_A, D), bf16),
         ),
         grid_spec=pltpu.PrefetchScalarGridSpec(
             num_scalar_prefetch=1,
@@ -248,16 +267,23 @@
                 pl.BlockSpec((HG * NOPE, D), lambda i, s: (i, 0)),
                 pl.BlockSpec((TOK, D), lambda i, s: (0, 0)),
                 pl.BlockSpec((1, D), lambda i, s: (0, 0)),
+                pl.BlockSpec((TOP, TOK), lambda i, s: (0, 0)),
             ],
             out_specs=[
                 pl.BlockSpec((TOK, D), lambda i, s: (0, 0)),
                 pl.BlockSpec((TOK, D), lambda i, s: (0, 0)),
+                pl.BlockSpec(memory_space=pltpu.HBM),
             ],
-            scratch_shapes=[pltpu.VMEM((TOK, D), f32)],
+            scratch_shapes=[
+                pltpu.VMEM((TOK, D), f32),
+                pltpu.VMEM((EXPERTS, TOK), f32),
+                pltpu.VMEM((EXPERTS, SLOTS_A, D), bf16),
+                pltpu.SemaphoreType.DMA((EXPERTS // EG, 2)),
+            ],
         ),
         name="project",
         compiler_params=grant(24),
-    )(scalars, o_lat, w_ukv, w_out, residual, gain)
+    )(scalars, o_lat, w_ukv, w_out, residual, gain, ids_t)
 
 
 def rank_table(ids_ref):
@@ -310,21 +336,6 @@
 
 
 EG = 16
-
-
-def dispatch_kernel(ids_ref, norm_ref, out_ref, rank_scr):
-    step = pl.program_id(0)
-
-    @pl.when(step == 0)
-    def _():
-        rank_scr[...] = rank_table(ids_ref)
-
-    ranks = rank_scr[pl.ds(step * EG, EG), :]
-    sent = mm(whole_rows(ranks, EG, 1).astype(bf16), norm_ref[...]).astype(bf16)
-    for e in range(EG):
-        part = sent[e * SLOTS_A : (e + 1) * SLOTS_A]
-        out_ref[2 * e] = part
-        out_ref[2 * e + 1] = part
 
 
 def dispatch_packed_kernel(ids_ref, norm_ref, out_ref, rank_scr):
@@ -445,7 +456,7 @@
 def combine(ids_t, gates_t, hidden, back):
     return pl.pallas_call(
         combine_kernel,
-        out_shape=jax.ShapeDtypeStruct((TOK, D), f32),
+        out_shape=pltpu.VMEM((TOK, D), f32),
         grid=(EXPERTS // CG,),
         in_specs=[
             pl.BlockSpec((TOP, TOK), lambda i: (0, 0)),
@@ -460,16 +471,27 @@
     )(ids_t, gates_t, hidden, back)
 
 
-def combine_packed_kernel(ids_ref, gates_ref, sum_ref, back_ref, out_ref, acc_ref):
+def last_rows(ranks, values):
+    hit = jnp.where(ranks == CAP - 1.0, values, 0.0)
+    return jnp.broadcast_to(hit[:, None, :], (EXPERTS, 2, TOK)).reshape(2 * EXPERTS, TOK)
+
+
+def combine_packed_kernel(ids_ref, gates_ref, sum_ref, back_ref, out_ref, acc_ref, tail_ref):
     ranks = rank_table(ids_ref)
     gates = gate_table(ids_ref, gates_ref)
     back = back_ref[...].reshape(2 * EXPERTS * 8, WIDTH_B)
-    lower, upper, last = packed_rows(ranks, EXPERTS, 2, gates)
+    for j in range(PIECE // 128):
+        tail_ref[j] = back[:, HALF + j * 128 : HALF + (j + 1) * 128].astype(f32)
+    lower, upper = packed_rows(ranks, EXPERTS, 2, gates)[:2]
     acc_ref[:, :HALF] = sum_ref[:, :HALF] + weighted(lower, back[:, :HALF])
     acc_ref[:, HALF:] = sum_ref[:, HALF:] + weighted(upper, back[:, :HALF])
-    for q, piece in enumerate(pieces_of(last)):
-        acc_ref[:, q * PIECE : (q + 1) * PIECE] += weighted(piece, back[:, HALF:])
-    out_ref[...] = acc_ref[...].astype(bf16)
+    fifth = [
+        tail_ref[j, pl.ds(q, 2 * EXPERTS, stride=8), :].astype(bf16)
+        for q in range(8)
+        for j in range(PIECE // 128)
+    ]
+    acc = acc_ref[...] + weighted(last_rows(ranks, gates), jnp.concatenate(fifth, axis=1))
+    out_ref[...] = acc.astype(bf16)
 
 
 def combine_packed(ids_t, gates_t, base, back):
@@ -478,7 +500,10 @@
         out_shape=jax.ShapeDtypeStruct((TOK, D), bf16),
         in_specs=[pl.BlockSpec(memory_space=pltpu.VMEM)] * 4,
         out_specs=pl.BlockSpec(memory_space=pltpu.VMEM),
-        scratch_shapes=[pltpu.VMEM((TOK, D), f32)],
+        scratch_shapes=[
+            pltpu.VMEM((TOK, D), f32),
+            pltpu.VMEM((PIECE // 128, 2 * EXPERTS * 8, 128), f32),
+        ],
         name="combine_b",
         compiler_params=grant(24),
     )(ids_t, gates_t, base, back)
@@ -543,10 +568,12 @@
     rest1 = gather_rest(row1, "x")
     qa, qr = prepare_queries(scalars, queries, w_ukv)
     o_lat = attend(scalars, qa, qr, suffix_latent, suffix_rope, [row0, *rest0], [row1, *rest1])
-    hidden, normed = project(scalars, o_lat, w_ukv, w_out, residual, norm_gain.reshape(1, D))
     ids_t = expert_ids.T
     gates_t = gate_values.T
-    sent_a = dispatch(dispatch_kernel, D, ids_t, normed)
+    hidden, normed, sent_a = project(
+        scalars, o_lat, w_ukv, w_out, residual, norm_gain.reshape(1, D), ids_t
+    )
+    sent_a = sent_a.reshape(2 * EXPERTS, SLOTS_A, D)
     sent_b = dispatch(dispatch_packed_kernel, WIDTH_B, ids_t, normed)
     rows_a = exchange(sent_a)
     rows_b = exchange(sent_b)

time: 275 us -> 274 us (level)
  local copies, waits for them, and re-layouts: 18.9 us -> 16.1 us
    pallas_call x2, Pallas kernels: 8.66 us -> 11.9 us  [the longest x1 7.73 us: project(): pl.pallas_call(project_kernel, out_shape=(pltpu.HBM((TOK, D), bf16), jax....]
    unnamed x55 -> x51, local copies, waits for them, and re-layouts: 16.4 us -> 13.6 us
where the time goes in v3:
time: 274 us; the launch traced here: 269 us
  waiting for transfers between devices  138 us (50%)
  Pallas kernels  62.2 us (23%)
  starting transfers between devices  52.4 us (19%)
  local copies, waits for them, and re-layouts  16.1 us (6%)
    all_to_all x4, waiting for transfers between devices, exchange(): lax.all_to_all(a, ('req', 'wide'), split_axis=0, concat_axis=0, tiled=True)  121 us
    all_to_all x4, starting transfers between devices, exchange(): lax.all_to_all(a, ('req', 'wide'), split_axis=0, concat_axis=0, tiled=True)  36.2 us
    pallas_call x2, Pallas kernels, run_expert(): pl.pallas_call(kernel, out_shape=jax.ShapeDtypeStruct(rows.shape, bf16),...  24.1 us
    pallas_call x1, Pallas kernels, attend(): pl.pallas_call(lambda *refs: attention_kernel(n_pieces, *refs), out_shape...  19.2 us
    ppermute x14, waiting for transfers between devices, hop(): return lax.ppermute(a, 'wide', shift(axis, k))  17.1 us
    ppermute x14, starting transfers between devices, hop(): return lax.ppermute(a, 'wide', shift(axis, k))  16.2 us
    unnamed x51, local copies, waits for them, and re-layouts  13.6 us
    pallas_call x1, Pallas kernels, project(): pl.pallas_call(project_kernel, out_shape=(pltpu.HBM((TOK, D), bf16), jax....  7.73 us
  transfers between devices with their start and end apart: 18, of which 9 were waited for; matrix products, arithmetic and copies ran while one was open for 0% of the time, Pallas kernels for 12%

profile of v3, /device:TPU:37, one launch (start us, length us, event | category | flops | bytes accessed | tf_op | source)
XLA Modules:
  0.0 269.1 jit_solution(8635739755624152448)
XLA Ops:
  9.4 1.6 collective-permute-start.9
  11.6 2.3 collective-permute-start.4
  13.9 1.7 collective-permute-done.9
  17.2 11.7 %collective-permute-done.3.refs_6_ = bf16[576,512]{1,0:T(8,128)(2,1)S(1)} collective-permute-done((bf16[576,512]{1,0:T(8,128)(2,1)S(1)}, bf16[576,512]{1,0:T(8,128)(2,1)S(1)}, u32[]{:S(2)}, u32[]{:S(2)}) %collective-permute-start.3) | collective-permute-done | bytes 589856 | tf_op jit(solution)/shard_map/ppermute | solution.py:522
  29.1 2.7 %collective-permute-start.6 = (bf16[288,512]{1,0:T(8,128)(2,1)S(1)}, bf16[288,512]{1,0:T(8,128)(2,1)S(1)}, u32[]{:S(2)}, u32[]{:S(2)}) collective-permute-start(bf16[288,512]{1,0:T(8,128)(2,1)S(1)} %slice.33), channel_id=1, source_target_pairs={{0,3},{1,0},{2,1},{3,2},{4,7},{5,4},{6,5},{7,6},{8,11},{9,8},{10,9... | collective-permute-start | bytes 884744 | tf_op jit(solution)/shard_map/ppermute | solution.py:522
  33.6 2.7 query_prep.1
  39.9 19.2 %attention.1.o_ref = bf16[16,128,512]{2,1,0:T(8,128)(2,1)S(1)} custom-call(s32[8]{0:T(128)S(1)} %pad_add_fusion.sc_ref.refs_0_, bf16[16,128,512]{2,1,0:T(8,128)(2,1)S(1)} %get-tuple-element.10.refs_1_, bf16[16,128,64]{2,1,0:T(8,128)(2,1)S(1)} %get-tuple-element.11.refs_2_, bf16[128,512]{1,0:T(8,128)(2,1)S(1)} %copy-done.12, bf16[64,128]{1,0:T(8,128)(2,1)S(1)} %copy-done.14, ...), custom_call_target="tpu_custom_call" | custom-call | tf_op jit(solution)/shard_map/attention/pallas_call | solution.py:193
  59.1 7.7 %project.1 = (bf16[128,2048]{1,0:T(8,128)(2,1)}, bf16[128,2048]{1,0:T(8,128)(2,1)S(1)}, bf16[64,2,8,2048]{3,2,1,0:T(8,128)(2,1)}) custom-call(s32[8]{0:T(128)S(1)} %pad_add_fusion.sc_ref.refs_0_, bf16[16,128,512]{2,1,0:T(8,128)(2,1)S(1)} %attention.1.o_ref, bf16[512,4096]{1,0:T(8,128)(2,1)S(1)} %copy-done.2, bf16[2048,2048]{1,0:T(8,128)(2,1)S(1)} %bitcast.30, ...), custom_call_target="tpu_custom_call" | custom-call | tf_op jit(solution)/shard_map/project/pallas_call | solution.py:254
  66.8 11.9 %all-to-all-start = ((bf16[128,8,2048]{2,1,0:T(8,128)(2,1)}), bf16[128,8,2048]{2,1,0:T(8,128)(2,1)}, u32[]{:S(2)}, u32[]{:S(2)}) async-start(bf16[128,8,2048]{2,1,0:T(8,128)(2,1)} %bitcast.37), calls=%async_computation | async-start | bytes 8388608 | tf_op jit(solution)/shard_map/all_to_all | solution.py:544
  78.8 1.9 shard_map.146
  82.2 45.3 %all-to-all-done.x_ref = bf16[128,8,2048]{2,1,0:T(8,128)(2,1)} async-done(((bf16[128,8,2048]{2,1,0:T(8,128)(2,1)}), bf16[128,8,2048]{2,1,0:T(8,128)(2,1)}, u32[]{:S(2)}, u32[]{:S(2)}) %all-to-all-start) | async-done | bytes 4194336 | tf_op jit(solution)/shard_map/all_to_all | solution.py:544
  127.5 8.1 %all-to-all-start.2 = ((bf16[128,8,1280]{2,1,0:T(8,128)(2,1)}), bf16[128,8,1280]{2,1,0:T(8,128)(2,1)}, u32[]{:S(2)}, u32[]{:S(2)}) async-start(bf16[128,8,1280]{2,1,0:T(8,128)(2,1)} %copy-done.5), calls=%async_computation.2 | async-start | bytes 5242880 | tf_op jit(solution)/shard_map/all_to_all | solution.py:544
  135.7 2.6 copy-done
  138.3 12.1 %shard_map.145 = bf16[128,8,2048]{2,1,0:T(8,128)(2,1)S(1)} custom-call(bf16[128,8,2048]{2,1,0:T(8,128)(2,1)} %all-to-all-done.x_ref, bf16[1,2048,1408]{2,1,0:T(8,128)(2,1)S(1)} %copy-done, bf16[1,704,2048]{2,1,0:T(8,128)(2,1)S(1)} %copy-done.4), custom_call_target="tpu_custom_call" | custom-call | tf_op jit(solution)/shard_map/pallas_call | solution.py:417
  150.4 1.9 copy-done.3
  152.4 15.5 %all-to-all-done.2.x_ref = bf16[128,8,1280]{2,1,0:T(8,128)(2,1)} async-done(((bf16[128,8,1280]{2,1,0:T(8,128)(2,1)}), bf16[128,8,1280]{2,1,0:T(8,128)(2,1)}, u32[]{:S(2)}, u32[]{:S(2)}) %all-to-all-start.2) | async-done | bytes 2621472 | tf_op jit(solution)/shard_map/all_to_all | solution.py:544
  167.9 8.5 %all-to-all-start.1 = ((bf16[128,8,2048]{2,1,0:T(8,128)(2,1)}), bf16[128,8,2048]{2,1,0:T(8,128)(2,1)}, u32[]{:S(2)}, u32[]{:S(2)}) async-start(bf16[128,8,2048]{2,1,0:T(8,128)(2,1)} %copy-done.3), calls=%async_computation.1 | async-start | bytes 8388608 | tf_op jit(solution)/shard_map/all_to_all | solution.py:544
  176.4 2.6 copy-done.1
  179.0 12.0 %shard_map.147 = bf16[128,8,1280]{2,1,0:T(8,128)(2,1)S(1)} custom-call(bf16[128,8,1280]{2,1,0:T(8,128)(2,1)} %all-to-all-done.2.x_ref, bf16[1,2048,1408]{2,1,0:T(8,128)(2,1)S(1)} %copy-done.1, bf16[1,704,2048]{2,1,0:T(8,128)(2,1)S(1)} %copy-done.4), custom_call_target="tpu_custom_call" | custom-call | tf_op jit(solution)/shard_map/pallas_call | solution.py:417
  192.5 32.7 %all-to-all-done.1.back_ref = bf16[128,8,2048]{2,1,0:T(8,128)(2,1)} async-done(((bf16[128,8,2048]{2,1,0:T(8,128)(2,1)}), bf16[128,8,2048]{2,1,0:T(8,128)(2,1)}, u32[]{:S(2)}, u32[]{:S(2)}) %all-to-all-start.1) | async-done | bytes 4194336 | tf_op jit(solution)/shard_map/all_to_all | solution.py:544
  225.2 7.7 %all-to-all-start.3 = ((bf16[128,8,1280]{2,1,0:T(8,128)(2,1)}), bf16[128,8,1280]{2,1,0:T(8,128)(2,1)S(1)}, u32[]{:S(2)}, u32[]{:S(2)}) async-start(bf16[128,8,1280]{2,1,0:T(8,128)(2,1)} %copy-done.6), calls=%async_computation.3 | async-start | bytes 5242880 | tf_op jit(solution)/shard_map/all_to_all | solution.py:544
  232.9 4.1 %combine_a.1.sum_ref = f32[128,2048]{1,0:T(8,128)S(1)} custom-call(s32[6,128]{1,0:T(8,128)S(1)} %bitcast.33, f32[6,128]{1,0:T(8,128)S(1)} %bitcast.35, bf16[128,2048]{1,0:T(8,128)(2,1)S(1)} %copy-done.11, bf16[128,8,2048]{2,1,0:T(8,128)(2,1)} %all-to-all-done.1.back_ref), custom_call_target="tpu_custom_call" | custom-call | tf_op jit(solution)/shard_map/combine_a/pallas_call | solution.py:457
  238.0 27.3 %all-to-all-done.3.back_ref = bf16[128,8,1280]{2,1,0:T(8,128)(2,1)S(1)} async-done(((bf16[128,8,1280]{2,1,0:T(8,128)(2,1)}), bf16[128,8,1280]{2,1,0:T(8,128)(2,1)S(1)}, u32[]{:S(2)}, u32[]{:S(2)}) %all-to-all-start.3) | async-done | bytes 2621472 | tf_op jit(solution)/shard_map/all_to_all | solution.py:544
  266.6 2.5 combine_b.1
  (86 shorter events, 22.2 us)
Async XLA Ops:
  0.0 33.5 %copy-start.18 = (s32[1,4]{1,0:T(1,128)S(1)}, s32[1,4]{1,0:T(1,128)}, u32[]{:S(2)}) copy-start(s32[1,4]{1,0:T(1,128)} %param.21) | copy-start | bytes 52
  0.0 33.5 %copy-start.9 = (bf16[128,3072]{1,0:T(8,128)(2,1)S(1)}, bf16[128,3072]{1,0:T(8,128)(2,1)}, u32[]{:S(2)}) copy-start(bf16[128,3072]{1,0:T(8,128)(2,1)} %qr_ref.1) | copy-start | bytes 2359300
  0.0 33.5 %copy-start.2 = (bf16[512,4096]{1,0:T(8,128)(2,1)S(1)}, bf16[512,4096]{1,0:T(8,128)(2,1)}, u32[]{:S(2)}) copy-start(bf16[512,4096]{1,0:T(8,128)(2,1)} %w_ref.3) | copy-start | bytes 12582916
  2.5 6.9 %collective-permute-start = (bf16[144,512]{1,0:T(8,128)(2,1)S(1)}, bf16[144,512]{1,0:T(8,128)(2,1)S(1)}, u32[]{:S(2)}, u32[]{:S(2)}) collective-permute-start(bf16[144,512]{1,0:T(8,128)(2,1)S(1)} %pad_maximum_fusion), channel_id=1, source_target_pairs={{0,4},{1,5},{2,6},{3,7},{4,8},{5,9},{6,10},{7,11},{8,12},{9,13},{1... | collective-permute-start | bytes 442376 | tf_op jit(solution)/shard_map/ppermute | solution.py:522
  3.5 7.6 %collective-permute-start.1 = (bf16[144,512]{1,0:T(8,128)(2,1)S(1)}, bf16[144,512]{1,0:T(8,128)(2,1)S(1)}, u32[]{:S(2)}, u32[]{:S(2)}) collective-permute-start(bf16[144,512]{1,0:T(8,128)(2,1)S(1)} %pad_maximum_fusion), channel_id=1, source_target_pairs={{0,12},{1,13},{2,14},{3,15},{4,0},{5,1},{6,2},{7,3},{8,4},{9,5},{1... | collective-permute-start | bytes 442376 | tf_op jit(solution)/shard_map/ppermute | solution.py:522
  4.0 7.1 %collective-permute-start.2 = (bf16[144,512]{1,0:T(8,128)(2,1)S(1)}, bf16[144,512]{1,0:T(8,128)(2,1)S(1)}, u32[]{:S(2)}, u32[]{:S(2)}) collective-permute-start(bf16[144,512]{1,0:T(8,128)(2,1)S(1)} %pad_maximum_fusion), channel_id=1, source_target_pairs={{0,8},{1,9},{2,10},{3,11},{4,12},{5,13},{6,14},{7,15},{8,0},{9,1},... | collective-permute-start | bytes 442376 | tf_op jit(solution)/shard_map/ppermute | solution.py:522
  5.5 8.4 %collective-permute-start.7 = (bf16[144,512]{1,0:T(8,128)(2,1)S(1)}, bf16[144,512]{1,0:T(8,128)(2,1)S(1)}, u32[]{:S(2)}, u32[]{:S(2)}) collective-permute-start(bf16[144,512]{1,0:T(8,128)(2,1)S(1)} %pad_maximum_fusion.1), channel_id=1, source_target_pairs={{0,1},{1,2},{2,3},{3,0},{4,5},{5,6},{6,7},{7,4},{8,9},{9,10},{10,1... | collective-permute-start | bytes 442376 | tf_op jit(solution)/shard_map/ppermute | solution.py:522
  6.9 7.0 %collective-permute-start.8 = (bf16[144,512]{1,0:T(8,128)(2,1)S(1)}, bf16[144,512]{1,0:T(8,128)(2,1)S(1)}, u32[]{:S(2)}, u32[]{:S(2)}) collective-permute-start(bf16[144,512]{1,0:T(8,128)(2,1)S(1)} %pad_maximum_fusion.1), channel_id=1, source_target_pairs={{0,3},{1,0},{2,1},{3,2},{4,7},{5,4},{6,5},{7,6},{8,11},{9,8},{10,9... | collective-permute-start | bytes 442376 | tf_op jit(solution)/shard_map/ppermute | solution.py:522
  9.4 6.2 %collective-permute-start.9 = (bf16[144,512]{1,0:T(8,128)(2,1)S(1)}, bf16[144,512]{1,0:T(8,128)(2,1)S(1)}, u32[]{:S(2)}, u32[]{:S(2)}) collective-permute-start(bf16[144,512]{1,0:T(8,128)(2,1)S(1)} %pad_maximum_fusion.1), channel_id=1, source_target_pairs={{0,2},{1,3},{2,0},{3,1},{4,6},{5,7},{6,4},{7,5},{8,10},{9,11},{10,... | collective-permute-start | bytes 442376 | tf_op jit(solution)/shard_map/ppermute | solution.py:522
  11.1 17.8 %collective-permute-start.3 = (bf16[576,512]{1,0:T(8,128)(2,1)S(1)}, bf16[576,512]{1,0:T(8,128)(2,1)S(1)}, u32[]{:S(2)}, u32[]{:S(2)}) collective-permute-start(bf16[576,512]{1,0:T(8,128)(2,1)S(1)} %constant_dynamic-update-slice_fusion.refs_5_), channel_id=1, source_target_pairs={{0,1},{1,2},{2,3},{3,0},{4,5},{5,6},{6,7},{7,4},{8,9},{9,10},{10,1... | collective-permute-start | bytes 1769480 | tf_op jit(solution)/shard_map/ppermute | solution.py:522
  11.6 17.4 %collective-permute-start.4 = (bf16[576,512]{1,0:T(8,128)(2,1)S(1)}, bf16[576,512]{1,0:T(8,128)(2,1)S(1)}, u32[]{:S(2)}, u32[]{:S(2)}) collective-permute-start(bf16[576,512]{1,0:T(8,128)(2,1)S(1)} %constant_dynamic-update-slice_fusion.refs_5_), channel_id=1, source_target_pairs={{0,3},{1,0},{2,1},{3,2},{4,7},{5,4},{6,5},{7,6},{8,11},{9,8},{10,9... | collective-permute-start | bytes 1769480 | tf_op jit(solution)/shard_map/ppermute | solution.py:522
  15.6 16.1 %collective-permute-start.10 = (bf16[576,512]{1,0:T(8,128)(2,1)S(1)}, bf16[576,512]{1,0:T(8,128)(2,1)S(1)}, u32[]{:S(2)}, u32[]{:S(2)}) collective-permute-start(bf16[576,512]{1,0:T(8,128)(2,1)S(1)} %constant_dynamic-update-slice_fusion.5.refs_10_), channel_id=1, source_target_pairs={{0,4},{1,5},{2,6},{3,7},{4,8},{5,9},{6,10},{7,11},{8,12},{9,13},{1... | collective-permute-start | bytes 1769480 | tf_op jit(solution)/shard_map/ppermute | solution.py:522
  16.2 16.5 %collective-permute-start.11 = (bf16[576,512]{1,0:T(8,128)(2,1)S(1)}, bf16[576,512]{1,0:T(8,128)(2,1)S(1)}, u32[]{:S(2)}, u32[]{:S(2)}) collective-permute-start(bf16[576,512]{1,0:T(8,128)(2,1)S(1)} %constant_dynamic-update-slice_fusion.5.refs_10_), channel_id=1, source_target_pairs={{0,12},{1,13},{2,14},{3,15},{4,0},{5,1},{6,2},{7,3},{8,4},{9,5},{1... | collective-permute-start | bytes 1769480 | tf_op jit(solution)/shard_map/ppermute | solution.py:522
  28.9 8.3 %collective-permute-start.5 = (bf16[288,512]{1,0:T(8,128)(2,1)S(1)}, bf16[288,512]{1,0:T(8,128)(2,1)S(1)}, u32[]{:S(2)}, u32[]{:S(2)}) collective-permute-start(bf16[288,512]{1,0:T(8,128)(2,1)S(1)} %slice.32), channel_id=1, source_target_pairs={{0,1},{1,2},{2,3},{3,0},{4,5},{5,6},{6,7},{7,4},{8,9},{9,10},{10,1... | collective-permute-start | bytes 884744 | tf_op jit(solution)/shard_map/ppermute | solution.py:522
  29.1 8.2 %collective-permute-start.6 = (bf16[288,512]{1,0:T(8,128)(2,1)S(1)}, bf16[288,512]{1,0:T(8,128)(2,1)S(1)}, u32[]{:S(2)}, u32[]{:S(2)}) collective-permute-start(bf16[288,512]{1,0:T(8,128)(2,1)S(1)} %slice.33), channel_id=1, source_target_pairs={{0,3},{1,0},{2,1},{3,2},{4,7},{5,4},{6,5},{7,6},{8,11},{9,8},{10,9... | collective-permute-start | bytes 884744 | tf_op jit(solution)/shard_map/ppermute | solution.py:522
  31.8 6.5 %collective-permute-start.12 = (bf16[288,512]{1,0:T(8,128)(2,1)S(1)}, bf16[288,512]{1,0:T(8,128)(2,1)S(1)}, u32[]{:S(2)}, u32[]{:S(2)}) collective-permute-start(bf16[288,512]{1,0:T(8,128)(2,1)S(1)} %slice.34), channel_id=1, source_target_pairs={{0,4},{1,5},{2,6},{3,7},{4,8},{5,9},{6,10},{7,11},{8,12},{9,13},{1... | collective-permute-start | bytes 884744 | tf_op jit(solution)/shard_map/ppermute | solution.py:522
  32.8 7.1 %collective-permute-start.13 = (bf16[288,512]{1,0:T(8,128)(2,1)S(1)}, bf16[288,512]{1,0:T(8,128)(2,1)S(1)}, u32[]{:S(2)}, u32[]{:S(2)}) collective-permute-start(bf16[288,512]{1,0:T(8,128)(2,1)S(1)} %slice.35), channel_id=1, source_target_pairs={{0,12},{1,13},{2,14},{3,15},{4,0},{5,1},{6,2},{7,3},{8,4},{9,5},{1... | collective-permute-start | bytes 884744 | tf_op jit(solution)/shard_map/ppermute | solution.py:522
  66.8 60.7 %all-to-all-start = ((bf16[128,8,2048]{2,1,0:T(8,128)(2,1)}), bf16[128,8,2048]{2,1,0:T(8,128)(2,1)}, u32[]{:S(2)}, u32[]{:S(2)}) async-start(bf16[128,8,2048]{2,1,0:T(8,128)(2,1)} %bitcast.37), calls=%async_computation | async-start | bytes 8388608 | tf_op jit(solution)/shard_map/all_to_all | solution.py:544
  78.7 56.9 %copy-start.4 = (bf16[1,704,2048]{2,1,0:T(8,128)(2,1)S(1)}, bf16[1,704,2048]{2,1,0:T(8,128)(2,1)}, u32[]{:S(2)}) copy-start(bf16[1,704,2048]{2,1,0:T(8,128)(2,1)} %wd_ref.3) | copy-start | bytes 8650756
  127.5 40.3 %all-to-all-start.2 = ((bf16[128,8,1280]{2,1,0:T(8,128)(2,1)}), bf16[128,8,1280]{2,1,0:T(8,128)(2,1)}, u32[]{:S(2)}, u32[]{:S(2)}) async-start(bf16[128,8,1280]{2,1,0:T(8,128)(2,1)} %copy-done.5), calls=%async_computation.2 | async-start | bytes 5242880 | tf_op jit(solution)/shard_map/all_to_all | solution.py:544
  167.9 57.3 %all-to-all-start.1 = ((bf16[128,8,2048]{2,1,0:T(8,128)(2,1)}), bf16[128,8,2048]{2,1,0:T(8,128)(2,1)}, u32[]{:S(2)}, u32[]{:S(2)}) async-start(bf16[128,8,2048]{2,1,0:T(8,128)(2,1)} %copy-done.3), calls=%async_computation.1 | async-start | bytes 8388608 | tf_op jit(solution)/shard_map/all_to_all | solution.py:544
  192.5 40.4 %copy-start.11 = (bf16[128,2048]{1,0:T(8,128)(2,1)S(1)}, bf16[128,2048]{1,0:T(8,128)(2,1)}, u32[]{:S(2)}) copy-start(bf16[128,2048]{1,0:T(8,128)(2,1)} %get-tuple-element.12.hid_ref) | copy-start | bytes 1572868
  192.5 40.4 %copy-start.15 = (f32[128,6]{0,1:T(8,128)S(1)}, f32[128,6]{0,1:T(8,128)}, u32[]{:S(2)}) copy-start(f32[128,6]{0,1:T(8,128)} %param.27) | copy-start | bytes 9220
  225.2 40.2 %all-to-all-start.3 = ((bf16[128,8,1280]{2,1,0:T(8,128)(2,1)}), bf16[128,8,1280]{2,1,0:T(8,128)(2,1)S(1)}, u32[]{:S(2)}, u32[]{:S(2)}) async-start(bf16[128,8,1280]{2,1,0:T(8,128)(2,1)} %copy-done.6), calls=%async_computation.3 | async-start | bytes 5242880 | tf_op jit(solution)/shard_map/all_to_all | solution.py:544
  (15 other events, 214.5 us)

commit v4 on v3

--- a/solution.py
+++ b/solution.py
@@ -65,6 +65,10 @@
 
 def grant(mib):
     return pltpu.CompilerParams(vmem_limit_bytes=mib << 20)
+
+
+def in_hbm(a):
+    return pltpu.with_memory_space_constraint(a, pltpu.HBM)
 
 
 def mm(a, b):
@@ -211,6 +215,9 @@
     )(scalars, qa, qr, local_lat, local_rope, *pieces)
 
 
+DG = 32
+
+
 def project_kernel(
     sc_ref, o_ref, w_ref, wo_ref, res_ref, gain_ref, ids_ref,
     hid_ref, norm_ref, sent_ref, acc_ref, rank_scr, sent_scr, sems,
@@ -235,11 +242,11 @@
         inverse = lax.rsqrt(jnp.mean(h32 * h32, axis=1, keepdims=True) + EPS)
         norm_ref[...] = (h32 * inverse * gain_ref[...].astype(f32)).astype(bf16)
         copies = []
-        for g in range(EXPERTS // EG):
-            part = pl.ds(g * EG, EG)
-            rows = whole_rows(rank_scr[g * EG : (g + 1) * EG, :], EG, 1).astype(bf16)
+        for g in range(EXPERTS // DG):
+            part = pl.ds(g * DG, DG)
+            rows = whole_rows(rank_scr[g * DG : (g + 1) * DG, :], DG, 1).astype(bf16)
             sent = mm(rows, norm_ref[...]).astype(bf16)
-            sent_scr[part] = sent.reshape(EG, SLOTS_A, D)
+            sent_scr[part] = sent.reshape(DG, SLOTS_A, D)
             for half in range(2):
                 copy = pltpu.make_async_copy(
                     sent_scr.at[part], sent_ref.at[part, half], sems.at[g, half]
@@ -278,7 +285,7 @@
                 pltpu.VMEM((TOK, D), f32),
                 pltpu.VMEM((EXPERTS, TOK), f32),
                 pltpu.VMEM((EXPERTS, SLOTS_A, D), bf16),
-                pltpu.SemaphoreType.DMA((EXPERTS // EG, 2)),
+                pltpu.SemaphoreType.DMA((EXPERTS // DG, 2)),
             ],
         ),
         name="project",
@@ -456,7 +463,7 @@
 def combine(ids_t, gates_t, hidden, back):
     return pl.pallas_call(
         combine_kernel,
-        out_shape=pltpu.VMEM((TOK, D), f32),
+        out_shape=pltpu.HBM((TOK, D), f32),
         grid=(EXPERTS // CG,),
         in_specs=[
             pl.BlockSpec((TOP, TOK), lambda i: (0, 0)),
@@ -476,37 +483,49 @@
     return jnp.broadcast_to(hit[:, None, :], (EXPERTS, 2, TOK)).reshape(2 * EXPERTS, TOK)
 
 
-def combine_packed_kernel(ids_ref, gates_ref, sum_ref, back_ref, out_ref, acc_ref, tail_ref):
+def combine_packed_kernel(
+    ids_ref, gates_ref, sum_hbm, back_ref, out_ref, acc_ref, tail_ref, sum_ref, sem
+):
+    fetch = pltpu.make_async_copy(sum_hbm, sum_ref, sem)
+    fetch.start()
     ranks = rank_table(ids_ref)
     gates = gate_table(ids_ref, gates_ref)
     back = back_ref[...].reshape(2 * EXPERTS * 8, WIDTH_B)
     for j in range(PIECE // 128):
         tail_ref[j] = back[:, HALF + j * 128 : HALF + (j + 1) * 128].astype(f32)
     lower, upper = packed_rows(ranks, EXPERTS, 2, gates)[:2]
-    acc_ref[:, :HALF] = sum_ref[:, :HALF] + weighted(lower, back[:, :HALF])
-    acc_ref[:, HALF:] = sum_ref[:, HALF:] + weighted(upper, back[:, :HALF])
+    acc_ref[:, :HALF] = weighted(lower, back[:, :HALF])
+    acc_ref[:, HALF:] = weighted(upper, back[:, :HALF])
     fifth = [
         tail_ref[j, pl.ds(q, 2 * EXPERTS, stride=8), :].astype(bf16)
         for q in range(8)
         for j in range(PIECE // 128)
     ]
     acc = acc_ref[...] + weighted(last_rows(ranks, gates), jnp.concatenate(fifth, axis=1))
-    out_ref[...] = acc.astype(bf16)
+    fetch.wait()
+    out_ref[...] = (acc + sum_ref[...]).astype(bf16)
 
 
 def combine_packed(ids_t, gates_t, base, back):
     return pl.pallas_call(
         combine_packed_kernel,
         out_shape=jax.ShapeDtypeStruct((TOK, D), bf16),
-        in_specs=[pl.BlockSpec(memory_space=pltpu.VMEM)] * 4,
+        in_specs=[
+            pl.BlockSpec(memory_space=pltpu.VMEM),
+            pl.BlockSpec(memory_space=pltpu.VMEM),
+            pl.BlockSpec(memory_space=pltpu.HBM),
+            pl.BlockSpec(memory_space=pltpu.VMEM),
+        ],
         out_specs=pl.BlockSpec(memory_space=pltpu.VMEM),
         scratch_shapes=[
             pltpu.VMEM((TOK, D), f32),
             pltpu.VMEM((PIECE // 128, 2 * EXPERTS * 8, 128), f32),
+            pltpu.VMEM((TOK, D), f32),
+            pltpu.SemaphoreType.DMA,
         ],
         name="combine_b",
         compiler_params=grant(24),
-    )(ids_t, gates_t, base, back)
+    )(ids_t, gates_t, in_hbm(base), back)
 
 
 def shift(axis, k):
@@ -535,9 +554,31 @@
     return [ahead, behind, far0, far1]
 
 
-def pack_prefix(latent, rope):
-    packed = rope.reshape(4, 16, TOK).transpose(1, 0, 2).reshape(16, 4 * TOK)
-    return jnp.concatenate([latent, packed], axis=0)
+def pack_kernel(lat_ref, rope_ref, out0_ref, out1_ref, sems):
+    copies = []
+    for pre, out_ref in enumerate((out0_ref, out1_ref)):
+        pairs = [(lat_ref.at[0, pre], out_ref.at[pl.ds(0, TOK)])]
+        for j in range(4):
+            source = rope_ref.at[0, pre, pl.ds(j * 16, 16)]
+            pairs.append((source, out_ref.at[pl.ds(TOK, 16), pl.ds(j * TOK, TOK)]))
+        for k, (source, target) in enumerate(pairs):
+            copy = pltpu.make_async_copy(source, target, sems.at[pre, k])
+            copy.start()
+            copies.append(copy)
+    for copy in copies:
+        copy.wait()
+
+
+def pack_prefixes(latent, rope):
+    return pl.pallas_call(
+        pack_kernel,
+        out_shape=(pltpu.VMEM((BLK, LAT), bf16),) * PREF,
+        in_specs=[pl.BlockSpec(memory_space=pltpu.HBM)] * 2,
+        out_specs=[pl.BlockSpec(memory_space=pltpu.VMEM)] * 2,
+        scratch_shapes=[pltpu.SemaphoreType.DMA((PREF, 5))],
+        name="pack",
+        compiler_params=grant(8),
+    )(in_hbm(latent), in_hbm(rope))
 
 
 def exchange(a):
@@ -562,8 +603,9 @@
     expert_down,
 ):
     scalars = jnp.concatenate([suffix_lengths[0], prefix_ids[0]])
-    row0 = gather_row(pack_prefix(prefix_latent[0, 0], prefix_rope[0, 0]), "x")
-    row1 = gather_row(pack_prefix(prefix_latent[0, 1], prefix_rope[0, 1]), "y")
+    shard0, shard1 = pack_prefixes(prefix_latent, prefix_rope)
+    row0 = gather_row(shard0, "x")
+    row1 = gather_row(shard1, "y")
     rest0 = gather_rest(row0, "y")
     rest1 = gather_rest(row1, "x")
     qa, qr = prepare_queries(scalars, queries, w_ukv)

time: 274 us -> 272 us (level)
  local copies, waits for them, and re-layouts: 16.1 us -> 10.5 us
  Pallas kernels: 62.2 us -> 65.4 us
    unnamed x51 -> x44, local copies, waits for them, and re-layouts: 13.6 us -> 10.3 us
    pallas_call x1 -> x2, Pallas kernels: 4.13 us -> 6.39 us  [the longest x1 5.11 us: combine(): pl.pallas_call(combine_kernel, out_shape=pltpu.HBM((TOK, D), f32), grid=(...]
  transfers between devices with their start and end apart: 18 -> 18, of which waited for: 9 -> 9; matrix products, arithmetic and copies ran while one was open for 0% -> 0% of each run, Pallas kernels for 12% -> 13%
where the time goes in v4:
time: 272 us; the launch traced here: 268 us
  waiting for transfers between devices  138 us (51%)
  Pallas kernels  65.4 us (24%)
  starting transfers between devices  53 us (19%)
  local copies, waits for them, and re-layouts  10.5 us (4%)
    all_to_all x4, waiting for transfers between devices, exchange(): lax.all_to_all(a, ('req', 'wide'), split_axis=0, concat_axis=0, tiled=True)  121 us
    all_to_all x4, starting transfers between devices, exchange(): lax.all_to_all(a, ('req', 'wide'), split_axis=0, concat_axis=0, tiled=True)  36 us
    pallas_call x2, Pallas kernels, run_expert(): pl.pallas_call(kernel, out_shape=jax.ShapeDtypeStruct(rows.shape, bf16),...  24.1 us
    pallas_call x1, Pallas kernels, attend(): pl.pallas_call(lambda *refs: attention_kernel(n_pieces, *refs), out_shape...  19.2 us
    ppermute x14, waiting for transfers between devices, hop(): return lax.ppermute(a, 'wide', shift(axis, k))  17.6 us
    ppermute x14, starting transfers between devices, hop(): return lax.ppermute(a, 'wide', shift(axis, k))  17 us
    unnamed x44, local copies, waits for them, and re-layouts  10.3 us
    pallas_call x1, Pallas kernels, project(): pl.pallas_call(project_kernel, out_shape=(pltpu.HBM((TOK, D), bf16), jax....  7.82 us
  transfers between devices with their start and end apart: 18, of which 9 were waited for; matrix products, arithmetic and copies ran while one was open for 0% of the time, Pallas kernels for 13%

profile of v4, /device:TPU:37, one launch (start us, length us, event | category | flops | bytes accessed | tf_op | source)
XLA Modules:
  0.0 267.9 jit_solution(4218611392683575717)
XLA Ops:
  7.1 2.0 collective-permute-start.9
  11.9 2.2 collective-permute-done.9
  15.7 10.9 %collective-permute-done.3.refs_6_ = bf16[576,512]{1,0:T(8,128)(2,1)S(1)} collective-permute-done((bf16[576,512]{1,0:T(8,128)(2,1)S(1)}, bf16[576,512]{1,0:T(8,128)(2,1)S(1)}, u32[]{:S(2)}, u32[]{:S(2)}) %collective-permute-start.3) | collective-permute-done | bytes 589856 | tf_op jit(solution)/shard_map/ppermute | solution.py:541
  26.8 2.7 %collective-permute-start.6 = (bf16[288,512]{1,0:T(8,128)(2,1)S(1)}, bf16[288,512]{1,0:T(8,128)(2,1)S(1)}, u32[]{:S(2)}, u32[]{:S(2)}) collective-permute-start(bf16[288,512]{1,0:T(8,128)(2,1)S(1)} %slice.17), channel_id=1, source_target_pairs={{0,3},{1,0},{2,1},{3,2},{4,7},{5,4},{6,5},{7,6},{8,11},{9,8},{10,9... | collective-permute-start | bytes 884744 | tf_op jit(solution)/shard_map/ppermute | solution.py:541
  32.0 2.7 query_prep.1
  34.8 2.4 collective-permute-done.12.refs_13_
  39.0 19.2 %attention.1.o_ref = bf16[16,128,512]{2,1,0:T(8,128)(2,1)S(1)} custom-call(s32[8]{0:T(128)S(1)} %pad_add_fusion.sc_ref.refs_0_, bf16[16,128,512]{2,1,0:T(8,128)(2,1)S(1)} %get-tuple-element.12.refs_1_, bf16[16,128,64]{2,1,0:T(8,128)(2,1)S(1)} %get-tuple-element.13.refs_2_, bf16[128,512]{1,0:T(8,128)(2,1)S(1)} %copy-done.10, bf16[64,128]{1,0:T(8,128)(2,1)S(1)} %copy-done.12, ...), custom_call_target="tpu_custom_call" | custom-call | tf_op jit(solution)/shard_map/attention/pallas_call | solution.py:197
  58.2 7.8 %project.1 = (bf16[128,2048]{1,0:T(8,128)(2,1)}, bf16[128,2048]{1,0:T(8,128)(2,1)S(1)}, bf16[64,2,8,2048]{3,2,1,0:T(8,128)(2,1)}) custom-call(s32[8]{0:T(128)S(1)} %pad_add_fusion.sc_ref.refs_0_, bf16[16,128,512]{2,1,0:T(8,128)(2,1)S(1)} %attention.1.o_ref, bf16[512,4096]{1,0:T(8,128)(2,1)S(1)} %copy-done.2, bf16[2048,2048]{1,0:T(8,128)(2,1)S(1)} %bitcast.6, ...), custom_call_target="tpu_custom_call" | custom-call | tf_op jit(solution)/shard_map/project/pallas_call | solution.py:261
  66.1 11.6 %all-to-all-start = ((bf16[128,8,2048]{2,1,0:T(8,128)(2,1)}), bf16[128,8,2048]{2,1,0:T(8,128)(2,1)}, u32[]{:S(2)}, u32[]{:S(2)}) async-start(bf16[128,8,2048]{2,1,0:T(8,128)(2,1)} %bitcast.13), calls=%async_computation | async-start | bytes 8388608 | tf_op jit(solution)/shard_map/all_to_all | solution.py:585
  77.7 1.9 shard_map.146
  81.1 45.4 %all-to-all-done.x_ref = bf16[128,8,2048]{2,1,0:T(8,128)(2,1)} async-done(((bf16[128,8,2048]{2,1,0:T(8,128)(2,1)}), bf16[128,8,2048]{2,1,0:T(8,128)(2,1)}, u32[]{:S(2)}, u32[]{:S(2)}) %all-to-all-start) | async-done | bytes 4194336 | tf_op jit(solution)/shard_map/all_to_all | solution.py:585
  126.5 8.1 %all-to-all-start.2 = ((bf16[128,8,1280]{2,1,0:T(8,128)(2,1)}), bf16[128,8,1280]{2,1,0:T(8,128)(2,1)}, u32[]{:S(2)}, u32[]{:S(2)}) async-start(bf16[128,8,1280]{2,1,0:T(8,128)(2,1)} %copy-done.5), calls=%async_computation.2 | async-start | bytes 5242880 | tf_op jit(solution)/shard_map/all_to_all | solution.py:585
  134.6 2.6 copy-done
  137.3 12.1 %shard_map.145 = bf16[128,8,2048]{2,1,0:T(8,128)(2,1)S(1)} custom-call(bf16[128,8,2048]{2,1,0:T(8,128)(2,1)} %all-to-all-done.x_ref, bf16[1,2048,1408]{2,1,0:T(8,128)(2,1)S(1)} %copy-done, bf16[1,704,2048]{2,1,0:T(8,128)(2,1)S(1)} %copy-done.4), custom_call_target="tpu_custom_call" | custom-call | tf_op jit(solution)/shard_map/pallas_call | solution.py:424
  149.4 2.0 copy-done.3
  151.4 15.4 %all-to-all-done.2.x_ref = bf16[128,8,1280]{2,1,0:T(8,128)(2,1)} async-done(((bf16[128,8,1280]{2,1,0:T(8,128)(2,1)}), bf16[128,8,1280]{2,1,0:T(8,128)(2,1)}, u32[]{:S(2)}, u32[]{:S(2)}) %all-to-all-start.2) | async-done | bytes 2621472 | tf_op jit(solution)/shard_map/all_to_all | solution.py:585
  166.8 8.5 %all-to-all-start.1 = ((bf16[128,8,2048]{2,1,0:T(8,128)(2,1)}), bf16[128,8,2048]{2,1,0:T(8,128)(2,1)}, u32[]{:S(2)}, u32[]{:S(2)}) async-start(bf16[128,8,2048]{2,1,0:T(8,128)(2,1)} %copy-done.3), calls=%async_computation.1 | async-start | bytes 8388608 | tf_op jit(solution)/shard_map/all_to_all | solution.py:585
  175.3 2.6 copy-done.1
  178.0 12.0 %shard_map.147 = bf16[128,8,1280]{2,1,0:T(8,128)(2,1)S(1)} custom-call(bf16[128,8,1280]{2,1,0:T(8,128)(2,1)} %all-to-all-done.2.x_ref, bf16[1,2048,1408]{2,1,0:T(8,128)(2,1)S(1)} %copy-done.1, bf16[1,704,2048]{2,1,0:T(8,128)(2,1)S(1)} %copy-done.4), custom_call_target="tpu_custom_call" | custom-call | tf_op jit(solution)/shard_map/pallas_call | solution.py:424
  191.5 32.7 %all-to-all-done.1.back_ref = bf16[128,8,2048]{2,1,0:T(8,128)(2,1)} async-done(((bf16[128,8,2048]{2,1,0:T(8,128)(2,1)}), bf16[128,8,2048]{2,1,0:T(8,128)(2,1)}, u32[]{:S(2)}, u32[]{:S(2)}) %all-to-all-start.1) | async-done | bytes 4194336 | tf_op jit(solution)/shard_map/all_to_all | solution.py:585
  224.1 7.7 %all-to-all-start.3 = ((bf16[128,8,1280]{2,1,0:T(8,128)(2,1)}), bf16[128,8,1280]{2,1,0:T(8,128)(2,1)S(1)}, u32[]{:S(2)}, u32[]{:S(2)}) async-start(bf16[128,8,1280]{2,1,0:T(8,128)(2,1)} %copy-done.6), calls=%async_computation.3 | async-start | bytes 5242880 | tf_op jit(solution)/shard_map/all_to_all | solution.py:585
  231.9 5.1 %combine_a.1.sum_hbm = f32[128,2048]{1,0:T(8,128)} custom-call(s32[6,128]{1,0:T(8,128)S(1)} %bitcast.9, f32[6,128]{1,0:T(8,128)S(1)} %bitcast.11, bf16[128,2048]{1,0:T(8,128)(2,1)S(1)} %copy-done.9, bf16[128,8,2048]{2,1,0:T(8,128)(2,1)} %all-to-all-done.1.back_ref), custom_call_target="tpu_custom_call" | custom-call | tf_op jit(solution)/shard_map/combine_a/pallas_call | solution.py:464
  237.0 27.4 %all-to-all-done.3.back_ref = bf16[128,8,1280]{2,1,0:T(8,128)(2,1)S(1)} async-done(((bf16[128,8,1280]{2,1,0:T(8,128)(2,1)}), bf16[128,8,1280]{2,1,0:T(8,128)(2,1)S(1)}, u32[]{:S(2)}, u32[]{:S(2)}) %all-to-all-start.3) | async-done | bytes 2621472 | tf_op jit(solution)/shard_map/all_to_all | solution.py:585
  264.3 3.3 %combine_b.1 = bf16[128,2048]{1,0:T(8,128)(2,1)} custom-call(s32[6,128]{1,0:T(8,128)S(1)} %bitcast.10, f32[6,128]{1,0:T(8,128)S(1)} %bitcast.12, f32[128,2048]{1,0:T(8,128)} %combine_a.1.sum_hbm, bf16[128,8,1280]{2,1,0:T(8,128)(2,1)S(1)} %all-to-all-done.3.back_ref), custom_call_target="tpu_custom_call" | custom-call | tf_op jit(solution)/shard_map/combine_b/pallas_call | solution.py:510
  (74 shorter events, 18.9 us)
Async XLA Ops:
  0.0 31.9 %copy-start.16 = (s32[1,4]{1,0:T(1,128)S(1)}, s32[1,4]{1,0:T(1,128)}, u32[]{:S(2)}) copy-start(s32[1,4]{1,0:T(1,128)} %param.21) | copy-start | bytes 52
  0.0 31.9 %copy-start.7 = (bf16[128,3072]{1,0:T(8,128)(2,1)S(1)}, bf16[128,3072]{1,0:T(8,128)(2,1)}, u32[]{:S(2)}) copy-start(bf16[128,3072]{1,0:T(8,128)(2,1)} %qr_ref.1) | copy-start | bytes 2359300
  0.0 31.9 %copy-start.2 = (bf16[512,4096]{1,0:T(8,128)(2,1)S(1)}, bf16[512,4096]{1,0:T(8,128)(2,1)}, u32[]{:S(2)}) copy-start(bf16[512,4096]{1,0:T(8,128)(2,1)} %w_ref.3) | copy-start | bytes 12582916
  1.3 5.7 %collective-permute-start = (bf16[144,512]{1,0:T(8,128)(2,1)S(1)}, bf16[144,512]{1,0:T(8,128)(2,1)S(1)}, u32[]{:S(2)}, u32[]{:S(2)}) collective-permute-start(bf16[144,512]{1,0:T(8,128)(2,1)S(1)} %get-tuple-element.14), channel_id=1, source_target_pairs={{0,4},{1,5},{2,6},{3,7},{4,8},{5,9},{6,10},{7,11},{8,12},{9,13},{1... | collective-permute-start | bytes 442376 | tf_op jit(solution)/shard_map/ppermute | solution.py:541
  2.3 6.7 %collective-permute-start.1 = (bf16[144,512]{1,0:T(8,128)(2,1)S(1)}, bf16[144,512]{1,0:T(8,128)(2,1)S(1)}, u32[]{:S(2)}, u32[]{:S(2)}) collective-permute-start(bf16[144,512]{1,0:T(8,128)(2,1)S(1)} %get-tuple-element.14), channel_id=1, source_target_pairs={{0,12},{1,13},{2,14},{3,15},{4,0},{5,1},{6,2},{7,3},{8,4},{9,5},{1... | collective-permute-start | bytes 442376 | tf_op jit(solution)/shard_map/ppermute | solution.py:541
  2.9 6.2 %collective-permute-start.2 = (bf16[144,512]{1,0:T(8,128)(2,1)S(1)}, bf16[144,512]{1,0:T(8,128)(2,1)S(1)}, u32[]{:S(2)}, u32[]{:S(2)}) collective-permute-start(bf16[144,512]{1,0:T(8,128)(2,1)S(1)} %get-tuple-element.14), channel_id=1, source_target_pairs={{0,8},{1,9},{2,10},{3,11},{4,12},{5,13},{6,14},{7,15},{8,0},{9,1},... | collective-permute-start | bytes 442376 | tf_op jit(solution)/shard_map/ppermute | solution.py:541
  4.3 7.6 %collective-permute-start.7 = (bf16[144,512]{1,0:T(8,128)(2,1)S(1)}, bf16[144,512]{1,0:T(8,128)(2,1)S(1)}, u32[]{:S(2)}, u32[]{:S(2)}) collective-permute-start(bf16[144,512]{1,0:T(8,128)(2,1)S(1)} %get-tuple-element.15), channel_id=1, source_target_pairs={{0,1},{1,2},{2,3},{3,0},{4,5},{5,6},{6,7},{7,4},{8,9},{9,10},{10,1... | collective-permute-start | bytes 442376 | tf_op jit(solution)/shard_map/ppermute | solution.py:541
  5.6 6.3 %collective-permute-start.8 = (bf16[144,512]{1,0:T(8,128)(2,1)S(1)}, bf16[144,512]{1,0:T(8,128)(2,1)S(1)}, u32[]{:S(2)}, u32[]{:S(2)}) collective-permute-start(bf16[144,512]{1,0:T(8,128)(2,1)S(1)} %get-tuple-element.15), channel_id=1, source_target_pairs={{0,3},{1,0},{2,1},{3,2},{4,7},{5,4},{6,5},{7,6},{8,11},{9,8},{10,9... | collective-permute-start | bytes 442376 | tf_op jit(solution)/shard_map/ppermute | solution.py:541
  7.1 7.1 %collective-permute-start.9 = (bf16[144,512]{1,0:T(8,128)(2,1)S(1)}, bf16[144,512]{1,0:T(8,128)(2,1)S(1)}, u32[]{:S(2)}, u32[]{:S(2)}) collective-permute-start(bf16[144,512]{1,0:T(8,128)(2,1)S(1)} %get-tuple-element.15), channel_id=1, source_target_pairs={{0,2},{1,3},{2,0},{3,1},{4,6},{5,7},{6,4},{7,5},{8,10},{9,11},{10,... | collective-permute-start | bytes 442376 | tf_op jit(solution)/shard_map/ppermute | solution.py:541
  9.1 17.5 %collective-permute-start.3 = (bf16[576,512]{1,0:T(8,128)(2,1)S(1)}, bf16[576,512]{1,0:T(8,128)(2,1)S(1)}, u32[]{:S(2)}, u32[]{:S(2)}) collective-permute-start(bf16[576,512]{1,0:T(8,128)(2,1)S(1)} %constant_dynamic-update-slice_fusion.refs_5_), channel_id=1, source_target_pairs={{0,1},{1,2},{2,3},{3,0},{4,5},{5,6},{6,7},{7,4},{8,9},{9,10},{10,1... | collective-permute-start | bytes 1769480 | tf_op jit(solution)/shard_map/ppermute | solution.py:541
  10.2 16.5 %collective-permute-start.4 = (bf16[576,512]{1,0:T(8,128)(2,1)S(1)}, bf16[576,512]{1,0:T(8,128)(2,1)S(1)}, u32[]{:S(2)}, u32[]{:S(2)}) collective-permute-start(bf16[576,512]{1,0:T(8,128)(2,1)S(1)} %constant_dynamic-update-slice_fusion.refs_5_), channel_id=1, source_target_pairs={{0,3},{1,0},{2,1},{3,2},{4,7},{5,4},{6,5},{7,6},{8,11},{9,8},{10,9... | collective-permute-start | bytes 1769480 | tf_op jit(solution)/shard_map/ppermute | solution.py:541
  14.2 15.4 %collective-permute-start.10 = (bf16[576,512]{1,0:T(8,128)(2,1)S(1)}, bf16[576,512]{1,0:T(8,128)(2,1)S(1)}, u32[]{:S(2)}, u32[]{:S(2)}) collective-permute-start(bf16[576,512]{1,0:T(8,128)(2,1)S(1)} %constant_dynamic-update-slice_fusion.4.refs_10_), channel_id=1, source_target_pairs={{0,4},{1,5},{2,6},{3,7},{4,8},{5,9},{6,10},{7,11},{8,12},{9,13},{1... | collective-permute-start | bytes 1769480 | tf_op jit(solution)/shard_map/ppermute | solution.py:541
  14.8 16.5 %collective-permute-start.11 = (bf16[576,512]{1,0:T(8,128)(2,1)S(1)}, bf16[576,512]{1,0:T(8,128)(2,1)S(1)}, u32[]{:S(2)}, u32[]{:S(2)}) collective-permute-start(bf16[576,512]{1,0:T(8,128)(2,1)S(1)} %constant_dynamic-update-slice_fusion.4.refs_10_), channel_id=1, source_target_pairs={{0,12},{1,13},{2,14},{3,15},{4,0},{5,1},{6,2},{7,3},{8,4},{9,5},{1... | collective-permute-start | bytes 1769480 | tf_op jit(solution)/shard_map/ppermute | solution.py:541
  26.7 8.1 %collective-permute-start.5 = (bf16[288,512]{1,0:T(8,128)(2,1)S(1)}, bf16[288,512]{1,0:T(8,128)(2,1)S(1)}, u32[]{:S(2)}, u32[]{:S(2)}) collective-permute-start(bf16[288,512]{1,0:T(8,128)(2,1)S(1)} %slice.16), channel_id=1, source_target_pairs={{0,1},{1,2},{2,3},{3,0},{4,5},{5,6},{6,7},{7,4},{8,9},{9,10},{10,1... | collective-permute-start | bytes 884744 | tf_op jit(solution)/shard_map/ppermute | solution.py:541
  26.8 8.0 %collective-permute-start.6 = (bf16[288,512]{1,0:T(8,128)(2,1)S(1)}, bf16[288,512]{1,0:T(8,128)(2,1)S(1)}, u32[]{:S(2)}, u32[]{:S(2)}) collective-permute-start(bf16[288,512]{1,0:T(8,128)(2,1)S(1)} %slice.17), channel_id=1, source_target_pairs={{0,3},{1,0},{2,1},{3,2},{4,7},{5,4},{6,5},{7,6},{8,11},{9,8},{10,9... | collective-permute-start | bytes 884744 | tf_op jit(solution)/shard_map/ppermute | solution.py:541
  29.6 7.6 %collective-permute-start.12 = (bf16[288,512]{1,0:T(8,128)(2,1)S(1)}, bf16[288,512]{1,0:T(8,128)(2,1)S(1)}, u32[]{:S(2)}, u32[]{:S(2)}) collective-permute-start(bf16[288,512]{1,0:T(8,128)(2,1)S(1)} %slice.18), channel_id=1, source_target_pairs={{0,4},{1,5},{2,6},{3,7},{4,8},{5,9},{6,10},{7,11},{8,12},{9,13},{1... | collective-permute-start | bytes 884744 | tf_op jit(solution)/shard_map/ppermute | solution.py:541
  31.4 7.6 %collective-permute-start.13 = (bf16[288,512]{1,0:T(8,128)(2,1)S(1)}, bf16[288,512]{1,0:T(8,128)(2,1)S(1)}, u32[]{:S(2)}, u32[]{:S(2)}) collective-permute-start(bf16[288,512]{1,0:T(8,128)(2,1)S(1)} %slice.19), channel_id=1, source_target_pairs={{0,12},{1,13},{2,14},{3,15},{4,0},{5,1},{6,2},{7,3},{8,4},{9,5},{1... | collective-permute-start | bytes 884744 | tf_op jit(solution)/shard_map/ppermute | solution.py:541
  66.1 60.4 %all-to-all-start = ((bf16[128,8,2048]{2,1,0:T(8,128)(2,1)}), bf16[128,8,2048]{2,1,0:T(8,128)(2,1)}, u32[]{:S(2)}, u32[]{:S(2)}) async-start(bf16[128,8,2048]{2,1,0:T(8,128)(2,1)} %bitcast.13), calls=%async_computation | async-start | bytes 8388608 | tf_op jit(solution)/shard_map/all_to_all | solution.py:585
  77.7 56.9 %copy-start.4 = (bf16[1,704,2048]{2,1,0:T(8,128)(2,1)S(1)}, bf16[1,704,2048]{2,1,0:T(8,128)(2,1)}, u32[]{:S(2)}) copy-start(bf16[1,704,2048]{2,1,0:T(8,128)(2,1)} %wd_ref.3) | copy-start | bytes 8650756
  126.5 40.3 %all-to-all-start.2 = ((bf16[128,8,1280]{2,1,0:T(8,128)(2,1)}), bf16[128,8,1280]{2,1,0:T(8,128)(2,1)}, u32[]{:S(2)}, u32[]{:S(2)}) async-start(bf16[128,8,1280]{2,1,0:T(8,128)(2,1)} %copy-done.5), calls=%async_computation.2 | async-start | bytes 5242880 | tf_op jit(solution)/shard_map/all_to_all | solution.py:585
  166.8 57.3 %all-to-all-start.1 = ((bf16[128,8,2048]{2,1,0:T(8,128)(2,1)}), bf16[128,8,2048]{2,1,0:T(8,128)(2,1)}, u32[]{:S(2)}, u32[]{:S(2)}) async-start(bf16[128,8,2048]{2,1,0:T(8,128)(2,1)} %copy-done.3), calls=%async_computation.1 | async-start | bytes 8388608 | tf_op jit(solution)/shard_map/all_to_all | solution.py:585
  191.5 40.4 %copy-start.9 = (bf16[128,2048]{1,0:T(8,128)(2,1)S(1)}, bf16[128,2048]{1,0:T(8,128)(2,1)}, u32[]{:S(2)}) copy-start(bf16[128,2048]{1,0:T(8,128)(2,1)} %get-tuple-element.16.hid_ref) | copy-start | bytes 1572868
  191.5 40.4 %copy-start.13 = (f32[128,6]{0,1:T(8,128)S(1)}, f32[128,6]{0,1:T(8,128)}, u32[]{:S(2)}) copy-start(f32[128,6]{0,1:T(8,128)} %param.27) | copy-start | bytes 9220
  224.1 40.2 %all-to-all-start.3 = ((bf16[128,8,1280]{2,1,0:T(8,128)(2,1)}), bf16[128,8,1280]{2,1,0:T(8,128)(2,1)S(1)}, u32[]{:S(2)}, u32[]{:S(2)}) async-start(bf16[128,8,1280]{2,1,0:T(8,128)(2,1)} %copy-done.6), calls=%async_computation.3 | async-start | bytes 5242880 | tf_op jit(solution)/shard_map/all_to_all | solution.py:585
  (13 other events, 211.9 us)

commit v5 on v4

--- a/solution.py
+++ b/solution.py
@@ -549,9 +549,8 @@
 
 def gather_rest(row, second):
     ahead, behind = hop(row, second, 1), hop(row, second, -1)
-    half = row.shape[0] // 2
-    far0, far1 = hop(ahead[:half], second, 1), hop(behind[half:], second, -1)
-    return [ahead, behind, far0, far1]
+    far = hop(row, second, 2)
+    return [ahead, behind, far]
 
 
 def pack_kernel(lat_ref, rope_ref, out0_ref, out1_ref, sems):

time: 272 us -> 292 us (1.074)
  starting transfers between devices: 53 us -> 62.6 us
  waiting for transfers between devices: 138 us -> 144 us
  local copies, waits for them, and re-layouts: 10.5 us -> 14.4 us
    all_to_all x4, starting transfers between devices: 36 us -> 45.3 us  [exchange(): lax.all_to_all(a, ('req', 'wide'), split_axis=0, concat_axis=0, tiled=True)]
    ppermute x14 -> x12, waiting for transfers between devices: 17.6 us -> 23.5 us  [hop(): return lax.ppermute(a, 'wide', shift(axis, k))]
    unnamed x44 -> x38, local copies, waits for them, and re-layouts: 10.3 us -> 13.7 us
    ppermute x14 -> x12, starting transfers between devices: 17 us -> 17.3 us  [hop(): return lax.ppermute(a, 'wide', shift(axis, k))]
  transfers between devices with their start and end apart: 18 -> 16, of which waited for: 9 -> 10; matrix products, arithmetic and copies ran while one was open for 0% -> 1% of each run, Pallas kernels for 13% -> 12%
where the time goes in v5:
time: 292 us; the launch traced here: 288 us
  waiting for transfers between devices  144 us (49%)
  Pallas kernels  65.2 us (22%)
  starting transfers between devices  62.6 us (21%)
  local copies, waits for them, and re-layouts  14.4 us (5%)
    all_to_all x4, waiting for transfers between devices, exchange(): lax.all_to_all(a, ('req', 'wide'), split_axis=0, concat_axis=0, tiled=True)  121 us
    all_to_all x4, starting transfers between devices, exchange(): lax.all_to_all(a, ('req', 'wide'), split_axis=0, concat_axis=0, tiled=True)  45.3 us
    pallas_call x2, Pallas kernels, run_expert(): pl.pallas_call(kernel, out_shape=jax.ShapeDtypeStruct(rows.shape, bf16),...  24.1 us
    ppermute x12, waiting for transfers between devices, hop(): return lax.ppermute(a, 'wide', shift(axis, k))  23.5 us
    pallas_call x1, Pallas kernels, attend(): pl.pallas_call(lambda *refs: attention_kernel(n_pieces, *refs), out_shape...  19 us
    ppermute x12, starting transfers between devices, hop(): return lax.ppermute(a, 'wide', shift(axis, k))  17.3 us
    unnamed x38, local copies, waits for them, and re-layouts  13.7 us
    pallas_call x1, Pallas kernels, project(): pl.pallas_call(project_kernel, out_shape=(pltpu.HBM((TOK, D), bf16), jax....  7.86 us
  transfers between devices with their start and end apart: 16, of which 10 were waited for; matrix products, arithmetic and copies ran while one was open for 1% of the time, Pallas kernels for 12%

profile of v5, /device:TPU:37, one launch (start us, length us, event | category | flops | bytes accessed | tf_op | source)
XLA Modules:
  0.0 287.7 jit_solution(1330772941189968575)
XLA Ops:
  6.6 2.1 collective-permute-done.2
  15.3 10.9 %collective-permute-done.6 = bf16[144,512]{1,0:T(8,128)(2,1)S(1)} collective-permute-done((bf16[144,512]{1,0:T(8,128)(2,1)S(1)}, bf16[144,512]{1,0:T(8,128)(2,1)S(1)}, u32[]{:S(2)}, u32[]{:S(2)}) %collective-permute-start.6) | collective-permute-done | bytes 147488 | tf_op jit(solution)/shard_map/ppermute | solution.py:541
  27.9 2.3 collective-permute-done.8
  30.2 2.3 collective-permute-start.9
  32.8 3.5 %collective-permute-start.11 = (bf16[576,512]{1,0:T(8,128)(2,1)S(1)}, bf16[576,512]{1,0:T(8,128)(2,1)S(1)}, u32[]{:S(2)}, u32[]{:S(2)}) collective-permute-start(bf16[576,512]{1,0:T(8,128)(2,1)S(1)} %constant_dynamic-update-slice_fusion.4.refs_9_), channel_id=1, source_target_pairs={{0,8},{1,9},{2,10},{3,11},{4,12},{5,13},{6,14},{7,15},{8,0},{9,1},... | collective-permute-start | bytes 1769480 | tf_op jit(solution)/shard_map/ppermute | solution.py:541
  37.7 2.2 copy-done.2
  41.0 2.7 query_prep.1
  43.7 5.8 %collective-permute-done.11.refs_12_ = bf16[576,512]{1,0:T(8,128)(2,1)S(1)} collective-permute-done((bf16[576,512]{1,0:T(8,128)(2,1)S(1)}, bf16[576,512]{1,0:T(8,128)(2,1)S(1)}, u32[]{:S(2)}, u32[]{:S(2)}) %collective-permute-start.11) | collective-permute-done | bytes 589856 | tf_op jit(solution)/shard_map/ppermute | solution.py:541
  49.6 19.0 %attention.1.o_ref = bf16[16,128,512]{2,1,0:T(8,128)(2,1)S(1)} custom-call(s32[8]{0:T(128)S(1)} %pad_add_fusion.sc_ref.refs_0_, bf16[16,128,512]{2,1,0:T(8,128)(2,1)S(1)} %get-tuple-element.12.refs_1_, bf16[16,128,64]{2,1,0:T(8,128)(2,1)S(1)} %get-tuple-element.13.refs_2_, bf16[128,512]{1,0:T(8,128)(2,1)S(1)} %copy-done.12, bf16[64,128]{1,0:T(8,128)(2,1)S(1)} %copy-done.14, ...), custom_call_target="tpu_custom_call" | custom-call | tf_op jit(solution)/shard_map/attention/pallas_call | solution.py:197
  68.7 7.9 %project.1 = (bf16[128,2048]{1,0:T(8,128)(2,1)}, bf16[128,2048]{1,0:T(8,128)(2,1)S(1)}, bf16[64,2,8,2048]{3,2,1,0:T(8,128)(2,1)}) custom-call(s32[8]{0:T(128)S(1)} %pad_add_fusion.sc_ref.refs_0_, bf16[16,128,512]{2,1,0:T(8,128)(2,1)S(1)} %attention.1.o_ref, bf16[512,4096]{1,0:T(8,128)(2,1)S(1)} %copy-done.3, bf16[2048,2048]{1,0:T(8,128)(2,1)S(1)} %copy-done.8, ...), custom_call_target="tpu_custom_call" | custom-call | tf_op jit(solution)/shard_map/project/pallas_call | solution.py:261
  76.5 21.0 %all-to-all-start = ((bf16[128,8,2048]{2,1,0:T(8,128)(2,1)}), bf16[128,8,2048]{2,1,0:T(8,128)(2,1)}, u32[]{:S(2)}, u32[]{:S(2)}) async-start(bf16[128,8,2048]{2,1,0:T(8,128)(2,1)} %bitcast.11), calls=%async_computation | async-start | bytes 8388608 | tf_op jit(solution)/shard_map/all_to_all | solution.py:584
  100.9 45.4 %all-to-all-done.x_ref = bf16[128,8,2048]{2,1,0:T(8,128)(2,1)} async-done(((bf16[128,8,2048]{2,1,0:T(8,128)(2,1)}), bf16[128,8,2048]{2,1,0:T(8,128)(2,1)}, u32[]{:S(2)}, u32[]{:S(2)}) %all-to-all-start) | async-done | bytes 4194336 | tf_op jit(solution)/shard_map/all_to_all | solution.py:584
  146.3 8.1 %all-to-all-start.2 = ((bf16[128,8,1280]{2,1,0:T(8,128)(2,1)}), bf16[128,8,1280]{2,1,0:T(8,128)(2,1)}, u32[]{:S(2)}, u32[]{:S(2)}) async-start(bf16[128,8,1280]{2,1,0:T(8,128)(2,1)} %copy-done.6), calls=%async_computation.2 | async-start | bytes 5242880 | tf_op jit(solution)/shard_map/all_to_all | solution.py:584
  154.5 2.6 copy-done
  157.1 12.1 %shard_map.145 = bf16[128,8,2048]{2,1,0:T(8,128)(2,1)S(1)} custom-call(bf16[128,8,2048]{2,1,0:T(8,128)(2,1)} %all-to-all-done.x_ref, bf16[1,2048,1408]{2,1,0:T(8,128)(2,1)S(1)} %copy-done, bf16[1,704,2048]{2,1,0:T(8,128)(2,1)S(1)} %copy-done.5), custom_call_target="tpu_custom_call" | custom-call | tf_op jit(solution)/shard_map/pallas_call | solution.py:424
  171.2 15.4 %all-to-all-done.2.x_ref = bf16[128,8,1280]{2,1,0:T(8,128)(2,1)} async-done(((bf16[128,8,1280]{2,1,0:T(8,128)(2,1)}), bf16[128,8,1280]{2,1,0:T(8,128)(2,1)}, u32[]{:S(2)}, u32[]{:S(2)}) %all-to-all-start.2) | async-done | bytes 2621472 | tf_op jit(solution)/shard_map/all_to_all | solution.py:584
  186.6 8.5 %all-to-all-start.1 = ((bf16[128,8,2048]{2,1,0:T(8,128)(2,1)}), bf16[128,8,2048]{2,1,0:T(8,128)(2,1)}, u32[]{:S(2)}, u32[]{:S(2)}) async-start(bf16[128,8,2048]{2,1,0:T(8,128)(2,1)} %copy-done.4), calls=%async_computation.1 | async-start | bytes 8388608 | tf_op jit(solution)/shard_map/all_to_all | solution.py:584
  195.2 2.6 copy-done.1
  197.8 12.0 %shard_map.147 = bf16[128,8,1280]{2,1,0:T(8,128)(2,1)S(1)} custom-call(bf16[128,8,1280]{2,1,0:T(8,128)(2,1)} %all-to-all-done.2.x_ref, bf16[1,2048,1408]{2,1,0:T(8,128)(2,1)S(1)} %copy-done.1, bf16[1,704,2048]{2,1,0:T(8,128)(2,1)S(1)} %copy-done.5), custom_call_target="tpu_custom_call" | custom-call | tf_op jit(solution)/shard_map/pallas_call | solution.py:424
  211.4 32.6 %all-to-all-done.1.back_ref = bf16[128,8,2048]{2,1,0:T(8,128)(2,1)} async-done(((bf16[128,8,2048]{2,1,0:T(8,128)(2,1)}), bf16[128,8,2048]{2,1,0:T(8,128)(2,1)}, u32[]{:S(2)}, u32[]{:S(2)}) %all-to-all-start.1) | async-done | bytes 4194336 | tf_op jit(solution)/shard_map/all_to_all | solution.py:584
  244.0 7.7 %all-to-all-start.3 = ((bf16[128,8,1280]{2,1,0:T(8,128)(2,1)}), bf16[128,8,1280]{2,1,0:T(8,128)(2,1)S(1)}, u32[]{:S(2)}, u32[]{:S(2)}) async-start(bf16[128,8,1280]{2,1,0:T(8,128)(2,1)} %copy-done.7), calls=%async_computation.3 | async-start | bytes 5242880 | tf_op jit(solution)/shard_map/all_to_all | solution.py:584
  251.7 5.1 %combine_a.1.sum_hbm = f32[128,2048]{1,0:T(8,128)} custom-call(s32[6,128]{1,0:T(8,128)S(1)} %bitcast.7, f32[6,128]{1,0:T(8,128)S(1)} %bitcast.9, bf16[128,2048]{1,0:T(8,128)(2,1)S(1)} %copy-done.11, bf16[128,8,2048]{2,1,0:T(8,128)(2,1)} %all-to-all-done.1.back_ref), custom_call_target="tpu_custom_call" | custom-call | tf_op jit(solution)/shard_map/combine_a/pallas_call | solution.py:464
  256.8 27.3 %all-to-all-done.3.back_ref = bf16[128,8,1280]{2,1,0:T(8,128)(2,1)S(1)} async-done(((bf16[128,8,1280]{2,1,0:T(8,128)(2,1)}), bf16[128,8,1280]{2,1,0:T(8,128)(2,1)S(1)}, u32[]{:S(2)}, u32[]{:S(2)}) %all-to-all-start.3) | async-done | bytes 2621472 | tf_op jit(solution)/shard_map/all_to_all | solution.py:584
  284.2 3.3 %combine_b.1 = bf16[128,2048]{1,0:T(8,128)(2,1)} custom-call(s32[6,128]{1,0:T(8,128)S(1)} %bitcast.8, f32[6,128]{1,0:T(8,128)S(1)} %bitcast.10, f32[128,2048]{1,0:T(8,128)} %combine_a.1.sum_hbm, bf16[128,8,1280]{2,1,0:T(8,128)(2,1)S(1)} %all-to-all-done.3.back_ref), custom_call_target="tpu_custom_call" | custom-call | tf_op jit(solution)/shard_map/combine_b/pallas_call | solution.py:510
  (59 shorter events, 24.8 us)
Async XLA Ops:
  0.0 49.5 %copy-start.12 = (bf16[128,512]{1,0:T(8,128)(2,1)S(1)}, bf16[128,512]{1,0:T(8,128)(2,1)}, u32[]{:S(2)}) copy-start(bf16[128,512]{1,0:T(8,128)(2,1)} %refs_3_.1) | copy-start | bytes 393220
  0.0 49.5 %copy-start.14 = (bf16[64,128]{1,0:T(8,128)(2,1)S(1)}, bf16[64,128]{1,0:T(8,128)(2,1)}, u32[]{:S(2)}) copy-start(bf16[64,128]{1,0:T(8,128)(2,1)} %refs_4_.1) | copy-start | bytes 49156
  1.2 4.8 %collective-permute-start = (bf16[144,512]{1,0:T(8,128)(2,1)S(1)}, bf16[144,512]{1,0:T(8,128)(2,1)S(1)}, u32[]{:S(2)}, u32[]{:S(2)}) collective-permute-start(bf16[144,512]{1,0:T(8,128)(2,1)S(1)} %get-tuple-element.14), channel_id=1, source_target_pairs={{0,4},{1,5},{2,6},{3,7},{4,8},{5,9},{6,10},{7,11},{8,12},{9,13},{1... | collective-permute-start | bytes 442376 | tf_op jit(solution)/shard_map/ppermute | solution.py:541
  2.2 4.5 %collective-permute-start.1 = (bf16[144,512]{1,0:T(8,128)(2,1)S(1)}, bf16[144,512]{1,0:T(8,128)(2,1)S(1)}, u32[]{:S(2)}, u32[]{:S(2)}) collective-permute-start(bf16[144,512]{1,0:T(8,128)(2,1)S(1)} %get-tuple-element.14), channel_id=1, source_target_pairs={{0,12},{1,13},{2,14},{3,15},{4,0},{5,1},{6,2},{7,3},{8,4},{9,5},{1... | collective-permute-start | bytes 442376 | tf_op jit(solution)/shard_map/ppermute | solution.py:541
  2.7 6.0 %collective-permute-start.2 = (bf16[144,512]{1,0:T(8,128)(2,1)S(1)}, bf16[144,512]{1,0:T(8,128)(2,1)S(1)}, u32[]{:S(2)}, u32[]{:S(2)}) collective-permute-start(bf16[144,512]{1,0:T(8,128)(2,1)S(1)} %get-tuple-element.14), channel_id=1, source_target_pairs={{0,8},{1,9},{2,10},{3,11},{4,12},{5,13},{6,14},{7,15},{8,0},{9,1},... | collective-permute-start | bytes 442376 | tf_op jit(solution)/shard_map/ppermute | solution.py:541
  8.7 24.0 %collective-permute-start.3 = (bf16[576,512]{1,0:T(8,128)(2,1)S(1)}, bf16[576,512]{1,0:T(8,128)(2,1)S(1)}, u32[]{:S(2)}, u32[]{:S(2)}) collective-permute-start(bf16[576,512]{1,0:T(8,128)(2,1)S(1)} %constant_dynamic-update-slice_fusion.refs_5_), channel_id=1, source_target_pairs={{0,1},{1,2},{2,3},{3,0},{4,5},{5,6},{6,7},{7,4},{8,9},{9,10},{10,1... | collective-permute-start | bytes 1769480 | tf_op jit(solution)/shard_map/ppermute | solution.py:541
  10.1 16.1 %collective-permute-start.6 = (bf16[144,512]{1,0:T(8,128)(2,1)S(1)}, bf16[144,512]{1,0:T(8,128)(2,1)S(1)}, u32[]{:S(2)}, u32[]{:S(2)}) collective-permute-start(bf16[144,512]{1,0:T(8,128)(2,1)S(1)} %get-tuple-element.15), channel_id=1, source_target_pairs={{0,1},{1,2},{2,3},{3,0},{4,5},{5,6},{6,7},{7,4},{8,9},{9,10},{10,1... | collective-permute-start | bytes 442376 | tf_op jit(solution)/shard_map/ppermute | solution.py:541
  11.4 16.5 %collective-permute-start.7 = (bf16[144,512]{1,0:T(8,128)(2,1)S(1)}, bf16[144,512]{1,0:T(8,128)(2,1)S(1)}, u32[]{:S(2)}, u32[]{:S(2)}) collective-permute-start(bf16[144,512]{1,0:T(8,128)(2,1)S(1)} %get-tuple-element.15), channel_id=1, source_target_pairs={{0,3},{1,0},{2,1},{3,2},{4,7},{5,4},{6,5},{7,6},{8,11},{9,8},{10,9... | collective-permute-start | bytes 442376 | tf_op jit(solution)/shard_map/ppermute | solution.py:541
  12.8 17.4 %collective-permute-start.8 = (bf16[144,512]{1,0:T(8,128)(2,1)S(1)}, bf16[144,512]{1,0:T(8,128)(2,1)S(1)}, u32[]{:S(2)}, u32[]{:S(2)}) collective-permute-start(bf16[144,512]{1,0:T(8,128)(2,1)S(1)} %get-tuple-element.15), channel_id=1, source_target_pairs={{0,2},{1,3},{2,0},{3,1},{4,6},{5,7},{6,4},{7,5},{8,10},{9,11},{10,... | collective-permute-start | bytes 442376 | tf_op jit(solution)/shard_map/ppermute | solution.py:541
  14.2 29.5 %collective-permute-start.4 = (bf16[576,512]{1,0:T(8,128)(2,1)S(1)}, bf16[576,512]{1,0:T(8,128)(2,1)S(1)}, u32[]{:S(2)}, u32[]{:S(2)}) collective-permute-start(bf16[576,512]{1,0:T(8,128)(2,1)S(1)} %constant_dynamic-update-slice_fusion.refs_5_), channel_id=1, source_target_pairs={{0,3},{1,0},{2,1},{3,2},{4,7},{5,4},{6,5},{7,6},{8,11},{9,8},{10,9... | collective-permute-start | bytes 1769480 | tf_op jit(solution)/shard_map/ppermute | solution.py:541
  26.2 17.5 %collective-permute-start.5 = (bf16[576,512]{1,0:T(8,128)(2,1)S(1)}, bf16[576,512]{1,0:T(8,128)(2,1)S(1)}, u32[]{:S(2)}, u32[]{:S(2)}) collective-permute-start(bf16[576,512]{1,0:T(8,128)(2,1)S(1)} %constant_dynamic-update-slice_fusion.refs_5_), channel_id=1, source_target_pairs={{0,2},{1,3},{2,0},{3,1},{4,6},{5,7},{6,4},{7,5},{8,10},{9,11},{10,... | collective-permute-start | bytes 1769480 | tf_op jit(solution)/shard_map/ppermute | solution.py:541
  30.2 13.5 %collective-permute-start.9 = (bf16[576,512]{1,0:T(8,128)(2,1)S(1)}, bf16[576,512]{1,0:T(8,128)(2,1)S(1)}, u32[]{:S(2)}, u32[]{:S(2)}) collective-permute-start(bf16[576,512]{1,0:T(8,128)(2,1)S(1)} %constant_dynamic-update-slice_fusion.4.refs_9_), channel_id=1, source_target_pairs={{0,4},{1,5},{2,6},{3,7},{4,8},{5,9},{6,10},{7,11},{8,12},{9,13},{1... | collective-permute-start | bytes 1769480 | tf_op jit(solution)/shard_map/ppermute | solution.py:541
  32.5 11.2 %collective-permute-start.10 = (bf16[576,512]{1,0:T(8,128)(2,1)S(1)}, bf16[576,512]{1,0:T(8,128)(2,1)S(1)}, u32[]{:S(2)}, u32[]{:S(2)}) collective-permute-start(bf16[576,512]{1,0:T(8,128)(2,1)S(1)} %constant_dynamic-update-slice_fusion.4.refs_9_), channel_id=1, source_target_pairs={{0,12},{1,13},{2,14},{3,15},{4,0},{5,1},{6,2},{7,3},{8,4},{9,5},{1... | collective-permute-start | bytes 1769480 | tf_op jit(solution)/shard_map/ppermute | solution.py:541
  32.8 16.8 %collective-permute-start.11 = (bf16[576,512]{1,0:T(8,128)(2,1)S(1)}, bf16[576,512]{1,0:T(8,128)(2,1)S(1)}, u32[]{:S(2)}, u32[]{:S(2)}) collective-permute-start(bf16[576,512]{1,0:T(8,128)(2,1)S(1)} %constant_dynamic-update-slice_fusion.4.refs_9_), channel_id=1, source_target_pairs={{0,8},{1,9},{2,10},{3,11},{4,12},{5,13},{6,14},{7,15},{8,0},{9,1},... | collective-permute-start | bytes 1769480 | tf_op jit(solution)/shard_map/ppermute | solution.py:541
  41.0 27.6 %copy-start.8 = (bf16[2048,2048]{1,0:T(8,128)(2,1)S(1)}, bf16[2048,2048]{1,0:T(8,128)(2,1)}, u32[]{:S(2)}) copy-start(bf16[2048,2048]{1,0:T(8,128)(2,1)} %wo_ref.1) | copy-start | bytes 25165828
  49.5 19.1 %copy-start.10 = (bf16[128,2048]{1,0:T(8,128)(2,1)S(1)}, bf16[128,2048]{1,0:T(8,128)(2,1)}, u32[]{:S(2)}) copy-start(bf16[128,2048]{1,0:T(8,128)(2,1)} %res_ref.1) | copy-start | bytes 1572868
  49.6 19.1 %copy-start.13 = (s32[128,6]{0,1:T(8,128)S(1)}, s32[128,6]{0,1:T(8,128)}, u32[]{:S(2)}) copy-start(s32[128,6]{0,1:T(8,128)} %param.26) | copy-start | bytes 9220
  76.5 69.8 %all-to-all-start = ((bf16[128,8,2048]{2,1,0:T(8,128)(2,1)}), bf16[128,8,2048]{2,1,0:T(8,128)(2,1)}, u32[]{:S(2)}, u32[]{:S(2)}) async-start(bf16[128,8,2048]{2,1,0:T(8,128)(2,1)} %bitcast.11), calls=%async_computation | async-start | bytes 8388608 | tf_op jit(solution)/shard_map/all_to_all | solution.py:584
  97.5 56.9 %copy-start.5 = (bf16[1,704,2048]{2,1,0:T(8,128)(2,1)S(1)}, bf16[1,704,2048]{2,1,0:T(8,128)(2,1)}, u32[]{:S(2)}) copy-start(bf16[1,704,2048]{2,1,0:T(8,128)(2,1)} %wd_ref.3) | copy-start | bytes 8650756
  146.3 40.3 %all-to-all-start.2 = ((bf16[128,8,1280]{2,1,0:T(8,128)(2,1)}), bf16[128,8,1280]{2,1,0:T(8,128)(2,1)}, u32[]{:S(2)}, u32[]{:S(2)}) async-start(bf16[128,8,1280]{2,1,0:T(8,128)(2,1)} %copy-done.6), calls=%async_computation.2 | async-start | bytes 5242880 | tf_op jit(solution)/shard_map/all_to_all | solution.py:584
  186.6 57.3 %all-to-all-start.1 = ((bf16[128,8,2048]{2,1,0:T(8,128)(2,1)}), bf16[128,8,2048]{2,1,0:T(8,128)(2,1)}, u32[]{:S(2)}, u32[]{:S(2)}) async-start(bf16[128,8,2048]{2,1,0:T(8,128)(2,1)} %copy-done.4), calls=%async_computation.1 | async-start | bytes 8388608 | tf_op jit(solution)/shard_map/all_to_all | solution.py:584
  211.4 40.3 %copy-start.11 = (bf16[128,2048]{1,0:T(8,128)(2,1)S(1)}, bf16[128,2048]{1,0:T(8,128)(2,1)}, u32[]{:S(2)}) copy-start(bf16[128,2048]{1,0:T(8,128)(2,1)} %get-tuple-element.16.hid_ref) | copy-start | bytes 1572868
  211.4 40.3 %copy-start.15 = (f32[128,6]{0,1:T(8,128)S(1)}, f32[128,6]{0,1:T(8,128)}, u32[]{:S(2)}) copy-start(f32[128,6]{0,1:T(8,128)} %param.27) | copy-start | bytes 9220
  244.0 40.2 %all-to-all-start.3 = ((bf16[128,8,1280]{2,1,0:T(8,128)(2,1)}), bf16[128,8,1280]{2,1,0:T(8,128)(2,1)S(1)}, u32[]{:S(2)}, u32[]{:S(2)}) async-start(bf16[128,8,1280]{2,1,0:T(8,128)(2,1)} %copy-done.7), calls=%async_computation.3 | async-start | bytes 5242880 | tf_op jit(solution)/shard_map/all_to_all | solution.py:584
  (8 other events, 32.8 us)
